TPU v7x, 32 devices: a whole 2x2x4 slice. The times are simulated.
32 devices in a mesh: batch: 8 (over y, x, core), tensor: 4 (over z).
Axes of the slice: x: 2, y: 2, z: 4, core: 2. Of those that a mesh axis runs over, the one named last changes fastest.
Arguments:
- tokens: bfloat16 [65536, 1024], P('batch'), may hold values from -6 to 6
- lengths: int32 [32], P('batch'), may hold values from 256 to 2048, as said below
- routes: int32 [32, 256], P('batch'), may hold values from 0 to 2047, as said below
- w_query: float32 [1024, 1024], P('batch', 'tensor'), may hold values from -0.1875 to 0.1875
- w_key: float32 [1024, 1024], P('batch', 'tensor'), may hold values from -0.1875 to 0.1875
- w_value: float32 [1024, 1024], P('batch', 'tensor'), may hold values from -0.1875 to 0.1875
- w_out: float32 [1024, 1024], P('tensor', 'batch'), may hold values from -0.75 to 0.75
- w_up: float32 [1024, 4096], P('batch', 'tensor'), may hold values from -0.1875 to 0.1875
- w_down: float32 [4096, 1024], P('tensor', 'batch'), may hold values from -0.125 to 0.125
- gain_attn: float32 [1024], P('batch'), may hold values from 0.1 to 1.9
- gain_mlp: float32 [1024], P('batch'), may hold values from 0.1 to 1.9
- w_router: float32 [1024], P('batch'), may hold values from -0.1875 to 0.1875
- cotangent: bfloat16 [65536, 1024], P('batch'), may hold values from -6 to 6
Outputs:
- output: bfloat16 [65536, 1024], P('batch')
- grad_tokens: bfloat16 [65536, 1024], P('batch')
- grad_query: float32 [1024, 1024], P('batch', 'tensor')
- grad_key: float32 [1024, 1024], P('batch', 'tensor')
- grad_value: float32 [1024, 1024], P('batch', 'tensor')
- grad_out: float32 [1024, 1024], P('tensor', 'batch')
- grad_up: float32 [1024, 4096], P('batch', 'tensor')
- grad_down: float32 [4096, 1024], P('tensor', 'batch')
- grad_gain_attn: float32 [1024], P('batch')
- grad_gain_mlp: float32 [1024], P('batch')
- grad_router: float32 [1024], P('batch')
Inputs may be any that keep to these rules, and one draw needn't show every extreme that they name: `lengths`: one sequence has exactly 2048 positions and one exactly 256. `routes`: for a sequence of length L, its first L // 8 entries are distinct positions below L in increasing order, L - 1 among them; its other entries are 0.
All inputs are finite; a program needn't handle non-finite values.
Results may differ from a plain program's by a relative error of at most 0.019.
Values may be sent and summed in bfloat16 or wider, within the bound.
No kernel may reach another device: no remote copies, remote signals or barrier semaphores. Data moves between devices by JAX's collectives and lax.ppermute only.
A program may use at most 320 MiB of HBM per device.

v0:
```python
import jax
import jax.numpy as jnp
from jax import lax
from jax.sharding import PartitionSpec as P

HEAD_DIM = 64
BLOCK = 128


EPSILON = 1e-06


def gelu_tanh(values):
    return (
        0.5
        * values
        * (1.0 + jnp.tanh(0.7978845608028654 * (values + 0.044715 * values * values * values)))
    )


def contract_rows(left, right):
    return lax.dot_general(
        left, right, (((0,), (0,)), ((), ())), preferred_element_type=jnp.float32
    )


def times_transposed(left, right):
    return lax.dot_general(
        left, right, (((1,), (1,)), ((), ())), preferred_element_type=jnp.float32
    )


def pick_rows(table, routes, per_block):
    slot_count = table.shape[1]
    column = jnp.arange(slot_count, dtype=jnp.int32)

    def pick_one_sequence(inputs):
        seq_table, seq_routes = inputs
        blocks = seq_routes.reshape(-1, per_block)

        def one_block(block_routes):
            chooser = (block_routes[:, None] == column[None, :]).astype(jnp.bfloat16)
            return jnp.dot(chooser, seq_table, preferred_element_type=jnp.float32)

        return lax.map(one_block, blocks).reshape(seq_routes.shape[0], seq_table.shape[1])

    return lax.map(pick_one_sequence, (table, routes))


def place_rows(values, routes, per_block, slot_count):
    feature_count = values.shape[2]
    column = jnp.arange(slot_count, dtype=jnp.int32)

    def place_one_sequence(inputs):
        seq_values, seq_routes = inputs
        blocks = seq_routes.reshape(-1, per_block)
        value_blocks = seq_values.reshape(-1, per_block, feature_count)

        def add_block(running, pieces):
            block_routes, block_values = pieces
            chooser = (block_routes[:, None] == column[None, :]).astype(jnp.bfloat16)
            return (running + contract_rows(chooser, block_values), None)

        running, _ = lax.scan(
            add_block, jnp.zeros((slot_count, feature_count), jnp.float32), (blocks, value_blocks)
        )
        return running

    return lax.map(place_one_sequence, (values, routes))


def causal_allowed(live_count, capacity):
    position = jnp.arange(capacity)
    allowed = position[None, :] <= position[:, None]
    allowed = allowed[None, None] & (
        position[None, None, None, :] < live_count[:, None, None, None]
    )
    return allowed


def attend_forward(queries, keys_all, vals_all, live_count, scale_qk):
    raw_scores = (
        jnp.einsum("sqhd,skhd->shqk", queries, keys_all, preferred_element_type=jnp.float32)
        * scale_qk
    )
    masked = jnp.where(causal_allowed(live_count, queries.shape[1]), raw_scores, -1e30)
    row_max = jnp.max(masked, axis=-1, keepdims=True)
    exp_scores = jnp.exp(masked - row_max)
    row_total = jnp.sum(exp_scores, axis=-1, keepdims=True)
    attn_probs = (exp_scores / row_total).astype(jnp.bfloat16)
    log_total = row_max + jnp.log(row_total)
    heads_out = jnp.einsum(
        "shqk,skhd->sqhd", attn_probs, vals_all, preferred_element_type=jnp.float32
    )
    return (heads_out.astype(jnp.bfloat16), log_total)


def attend_backward(queries, keys_all, vals_all, d_heads, log_total, live_count, scale_qk):
    raw_scores = (
        jnp.einsum("sqhd,skhd->shqk", queries, keys_all, preferred_element_type=jnp.float32)
        * scale_qk
    )
    masked = jnp.where(causal_allowed(live_count, queries.shape[1]), raw_scores, -1e30)
    attn_probs = jnp.exp(masked - log_total)
    d_vals = jnp.einsum(
        "shqk,sqhd->skhd",
        attn_probs.astype(jnp.bfloat16),
        d_heads,
        preferred_element_type=jnp.float32,
    ).astype(jnp.bfloat16)
    d_probs = jnp.einsum("sqhd,skhd->shqk", d_heads, vals_all, preferred_element_type=jnp.float32)
    d_scores = (
        attn_probs * (d_probs - jnp.sum(d_probs * attn_probs, axis=-1, keepdims=True))
    ).astype(jnp.bfloat16)
    d_queries = (
        jnp.einsum("shqk,skhd->sqhd", d_scores, keys_all, preferred_element_type=jnp.float32)
        * scale_qk
    ).astype(jnp.bfloat16)
    d_keys = (
        jnp.einsum("shqk,sqhd->skhd", d_scores, queries, preferred_element_type=jnp.float32)
        * scale_qk
    ).astype(jnp.bfloat16)
    return (d_queries, d_keys, d_vals)


def norm_backward(d_normed_in, normed, inverse, gain_vec):
    d_scaled = d_normed_in * gain_vec
    d_input = inverse * (d_scaled - normed * jnp.mean(d_scaled * normed, axis=-1, keepdims=True))
    return (d_input, jnp.sum(d_normed_in * normed, axis=0))


def norm_forward(values):
    inverse = lax.rsqrt(jnp.mean(values * values, axis=-1, keepdims=True) + EPSILON)
    return (values * inverse, inverse)


def shards(
    tokens,
    lengths,
    routes,
    w_query,
    w_key,
    w_value,
    w_out,
    w_up,
    w_down,
    gain_attn,
    gain_mlp,
    w_router,
    cotangent,
):
    low_query = w_query.astype(jnp.bfloat16)
    low_key = w_key.astype(jnp.bfloat16)
    low_value = w_value.astype(jnp.bfloat16)
    low_up = w_up.astype(jnp.bfloat16)
    low_out = w_out.astype(jnp.bfloat16)
    low_down = w_down.astype(jnp.bfloat16)
    low_gain_attn = gain_attn.astype(jnp.bfloat16)
    low_gain_mlp = gain_mlp.astype(jnp.bfloat16)
    low_router = w_router.astype(jnp.bfloat16)
    fetched = (
        lax.all_gather(low_query, "batch", axis=0, tiled=True),
        lax.all_gather(low_key, "batch", axis=0, tiled=True),
        lax.all_gather(low_value, "batch", axis=0, tiled=True),
        lax.all_gather(low_up, "batch", axis=0, tiled=True),
        lax.all_gather(low_out, "batch", axis=1, tiled=True),
        lax.all_gather(low_down, "batch", axis=1, tiled=True),
        lax.all_gather(low_gain_attn, "batch", axis=0, tiled=True),
        lax.all_gather(low_gain_mlp, "batch", axis=0, tiled=True),
        lax.all_gather(low_router, "batch", axis=0, tiled=True),
    )
    (
        query_full,
        key_full,
        value_full,
        up_full,
        out_full,
        down_full,
        gain_one_low,
        gain_two_low,
        router_low,
    ) = fetched
    seq_count = routes.shape[0]
    capacity = routes.shape[1]
    feature_count = tokens.shape[1]
    slot_count = tokens.shape[0] // seq_count
    rows_total = seq_count * capacity
    per_block = min(BLOCK, capacity)
    heads_local = query_full.shape[1] // HEAD_DIM
    scale_qk = HEAD_DIM ** (-0.5)
    head_shape = (seq_count, capacity, heads_local, HEAD_DIM)
    routed = pick_rows(
        tokens.reshape(seq_count, slot_count, feature_count), routes, per_block
    ).reshape(rows_total, feature_count)
    routed_low = routed.astype(jnp.bfloat16)
    live_count = lengths // 8
    position = jnp.arange(capacity)
    is_live = (position[None, :] < live_count[:, None]).reshape(rows_total)
    router_score = jnp.dot(routed_low, router_low, preferred_element_type=jnp.float32)
    gate_prob = 1.0 / (1.0 + jnp.exp(-router_score))
    gate_live = jnp.where(is_live, gate_prob, 0.0)
    gain_one = gain_one_low.astype(jnp.float32)
    gain_two = gain_two_low.astype(jnp.float32)
    router_vec = router_low.astype(jnp.float32)
    normed_one, inverse_one = norm_forward(routed)
    attn_in = (normed_one * gain_one).astype(jnp.bfloat16)
    queries = (
        jnp.dot(attn_in, query_full, preferred_element_type=jnp.float32)
        .astype(jnp.bfloat16)
        .reshape(head_shape)
    )
    keys_all = (
        jnp.dot(attn_in, key_full, preferred_element_type=jnp.float32)
        .astype(jnp.bfloat16)
        .reshape(head_shape)
    )
    vals_all = (
        jnp.dot(attn_in, value_full, preferred_element_type=jnp.float32)
        .astype(jnp.bfloat16)
        .reshape(head_shape)
    )
    heads_four, log_total = attend_forward(queries, keys_all, vals_all, live_count, scale_qk)
    heads_out = heads_four.reshape(rows_total, heads_local * HEAD_DIM)
    attn_part = jnp.dot(heads_out, out_full, preferred_element_type=jnp.float32)
    cot_routed = pick_rows(
        cotangent.reshape(seq_count, slot_count, feature_count), routes, per_block
    ).reshape(rows_total, feature_count)
    attn_out = lax.psum(attn_part, "tensor")
    middle = routed + attn_out
    normed_two, inverse_two = norm_forward(middle)
    mlp_in = (normed_two * gain_two).astype(jnp.bfloat16)
    hidden_pre = jnp.dot(mlp_in, up_full, preferred_element_type=jnp.float32)
    hidden = gelu_tanh(hidden_pre).astype(jnp.bfloat16)
    mlp_part = jnp.dot(hidden, down_full, preferred_element_type=jnp.float32)
    mlp_out = lax.psum(mlp_part.astype(jnp.bfloat16), "tensor").astype(jnp.float32)
    branch = attn_out + mlp_out
    update = (gate_live[:, None] * branch).astype(jnp.bfloat16)
    d_branch = gate_live[:, None] * cot_routed
    d_mlp_out = d_branch.astype(jnp.bfloat16)
    d_score = gate_live * (1.0 - gate_prob) * jnp.sum(cot_routed * branch, axis=-1)
    placed = place_rows(
        update.reshape(seq_count, capacity, feature_count), routes, per_block, slot_count
    )
    output = (tokens.astype(jnp.float32) + placed.reshape(-1, feature_count)).astype(jnp.bfloat16)
    d_hidden = times_transposed(d_mlp_out, down_full)
    _, gelu_pull = jax.vjp(gelu_tanh, hidden_pre)
    d_pre = gelu_pull(d_hidden)[0].astype(jnp.bfloat16)
    grad_down = contract_rows(hidden, d_mlp_out)
    grad_up = contract_rows(mlp_in, d_pre)
    d_mlp_part = times_transposed(d_pre, up_full)
    d_mlp_in = lax.psum(d_mlp_part, "tensor")
    d_middle, grad_gain_mlp = norm_backward(d_mlp_in, normed_two, inverse_two, gain_two)
    d_attn_out = (d_middle + d_branch).astype(jnp.bfloat16)
    grad_out = contract_rows(heads_out, d_attn_out)
    d_heads = times_transposed(d_attn_out, out_full).astype(jnp.bfloat16).reshape(head_shape)
    d_queries, d_keys, d_vals = attend_backward(
        queries, keys_all, vals_all, d_heads, log_total, live_count, scale_qk
    )
    flat_shape = (rows_total, heads_local * HEAD_DIM)
    d_queries = d_queries.reshape(flat_shape)
    d_keys = d_keys.reshape(flat_shape)
    d_vals = d_vals.reshape(flat_shape)
    grad_query = contract_rows(attn_in, d_queries)
    grad_key = contract_rows(attn_in, d_keys)
    grad_value = contract_rows(attn_in, d_vals)
    d_attn_part = (
        times_transposed(d_queries, query_full)
        + times_transposed(d_keys, key_full)
        + times_transposed(d_vals, value_full)
    )
    d_attn_in = lax.psum(d_attn_part.astype(jnp.bfloat16), "tensor").astype(jnp.float32)
    d_from_norm, grad_gain_attn = norm_backward(d_attn_in, normed_one, inverse_one, gain_one)
    grad_router = jnp.sum(routed * d_score[:, None], axis=0)
    d_routed = (d_middle + d_from_norm + d_score[:, None] * router_vec).astype(jnp.bfloat16)
    placed_back = place_rows(
        d_routed.reshape(seq_count, capacity, feature_count), routes, per_block, slot_count
    )
    grad_tokens = (cotangent.astype(jnp.float32) + placed_back.reshape(-1, feature_count)).astype(
        jnp.bfloat16
    )
    all_sent = (
        lax.psum_scatter(
            grad_query.astype(jnp.bfloat16), "batch", scatter_dimension=0, tiled=True
        ).astype(jnp.float32),
        lax.psum_scatter(
            grad_key.astype(jnp.bfloat16), "batch", scatter_dimension=0, tiled=True
        ).astype(jnp.float32),
        lax.psum_scatter(
            grad_value.astype(jnp.bfloat16), "batch", scatter_dimension=0, tiled=True
        ).astype(jnp.float32),
        lax.psum_scatter(
            grad_out.astype(jnp.bfloat16), "batch", scatter_dimension=1, tiled=True
        ).astype(jnp.float32),
        lax.psum_scatter(
            grad_up.astype(jnp.bfloat16), "batch", scatter_dimension=0, tiled=True
        ).astype(jnp.float32),
        lax.psum_scatter(
            grad_down.astype(jnp.bfloat16), "batch", scatter_dimension=1, tiled=True
        ).astype(jnp.float32),
        lax.psum_scatter(
            grad_gain_attn.astype(jnp.bfloat16), "batch", scatter_dimension=0, tiled=True
        ).astype(jnp.float32),
        lax.psum_scatter(
            grad_gain_mlp.astype(jnp.bfloat16), "batch", scatter_dimension=0, tiled=True
        ).astype(jnp.float32),
        lax.psum_scatter(
            grad_router.astype(jnp.bfloat16), "batch", scatter_dimension=0, tiled=True
        ).astype(jnp.float32),
    )
    (
        shard_query,
        shard_key,
        shard_value,
        shard_out,
        shard_up,
        shard_down,
        shard_gain_attn,
        shard_gain_mlp,
        shard_router,
    ) = all_sent
    return (
        output,
        grad_tokens,
        shard_query,
        shard_key,
        shard_value,
        shard_out,
        shard_up,
        shard_down,
        shard_gain_attn,
        shard_gain_mlp,
        shard_router,
    )


def solution(mesh):
    in_specs = (
        P("batch", None),
        P("batch"),
        P("batch", None),
        P("batch", "tensor"),
        P("batch", "tensor"),
        P("batch", "tensor"),
        P("tensor", "batch"),
        P("batch", "tensor"),
        P("tensor", "batch"),
        P("batch"),
        P("batch"),
        P("batch"),
        P("batch", None),
    )
    out_specs = (
        P("batch", None),
        P("batch", None),
        P("batch", "tensor"),
        P("batch", "tensor"),
        P("batch", "tensor"),
        P("tensor", "batch"),
        P("batch", "tensor"),
        P("tensor", "batch"),
        P("batch"),
        P("batch"),
        P("batch"),
    )
    return jax.shard_map(shards, mesh=mesh, in_specs=in_specs, out_specs=out_specs, check_vma=False)
```

profile of v0, /device:TPU:0, one launch (start us, length us, event | category | flops | bytes accessed | tf_op | source)
XLA Modules:
  0.0 954.1 jit_solution(3100786415953661033)
XLA Ops:
  10.6 10.2 %all-gather.1 = bf16[8,1,128]{2,1,0:T(2,128)(2,1)S(1)} all-gather(bf16[1,1,128]{2,1,0:T(2,128)(2,1)S(1)} %convert_bitcast_fusion.1), channel_id=1, replica_groups=mesh['batch'=8,'tensor'=4] {'batch'}, dimensions={0}, use_global_device_ids=true | all-gather | bytes 2304 | tf_op jit(solution)/shard_map/all_gather | solution.py:168
  24.4 10.8 %all_gather.31 = bf16[1024,256]{1,0:T(8,128)(2,1)} all-gather(bf16[128,256]{1,0:T(8,128)(2,1)S(1)} %convert_element_type.207), channel_id=1, replica_groups=mesh['batch'=8,'tensor'=4] {'batch'}, dimensions={0}, use_global_device_ids=true | all-gather | bytes 589824 | tf_op jit(solution)/shard_map/all_gather | solution.py:163
  37.8 46.6 %while.91 = (s32[]{:T(128)}, f32[4,256,1024]{2,1,0:T(8,128)}, s32[4,256]{1,0:T(4,128)S(1)}, bf16[4,2048,1024]{2,1,0:T(8,128)(2,1)}, s32[]{:T(128)}, /*index=5*/s32[]{:T(128)}, s32[]{:T(128)}) while((s32[]{:T(128)}, f32[4,256,1024]{2,1,0:T(8,128)}, s32[4,256]{1,0:T(4,128)S(1)}, bf16[4,2048,1024]{2,1,0:T(8,128)(2,1)}, s32[]{:T(128)}, ...), condition=%wide.region_3.4_spmd.clone, body=%wide.region_0.3_spmd.clone.sunk | while | flops 537133056 | bytes 15224558 | solution.py:47
  42.5 5.9 while.98
  54.1 5.9 while.98
  65.8 5.9 while.98
  77.4 5.9 while.98
  93.2 9.0 all_gather.29
  110.5 10.1 %all_gather.30 = bf16[1024,256]{1,0:T(8,128)(2,1)S(1)} all-gather(bf16[128,256]{1,0:T(8,128)(2,1)S(1)} %convert_element_type.205), channel_id=1, replica_groups=mesh['batch'=8,'tensor'=4] {'batch'}, dimensions={0}, use_global_device_ids=true | all-gather | bytes 589824 | tf_op jit(solution)/shard_map/all_gather | solution.py:162
  130.5 9.2 all_gather.32
  147.6 47.5 %while.95 = (s32[]{:T(128)}, f32[4,256,1024]{2,1,0:T(8,128)}, s32[4,256]{1,0:T(4,128)S(1)}, bf16[4,2048,1024]{2,1,0:T(8,128)(2,1)}, s32[]{:T(128)}, /*index=5*/s32[]{:T(128)}, s32[]{:T(128)}) while((s32[]{:T(128)}, f32[4,256,1024]{2,1,0:T(8,128)}, s32[4,256]{1,0:T(4,128)S(1)}, bf16[4,2048,1024]{2,1,0:T(8,128)(2,1)}, s32[]{:T(128)}, ...), condition=%wide.region_17.18_spmd.clone, body=%wide.region_14.17_spmd.clone.sunk | while | flops 537133056 | bytes 15224558 | solution.py:47
  147.6 5.3 dynamic-slice_bitcast_fusion.9
  152.9 6.1 while.100
  164.7 6.0 while.100
  176.3 6.0 while.100
  188.0 6.0 while.100
  195.1 8.5 all-gather.2
  203.6 8.2 all-gather
  215.0 6.6 fusion.72
  221.7 76.7 %all-reduce.9.cloned.1.call-done = f32[1024,1024]{1,0:T(8,128)} async-done(((f32[1024,1024]{1,0:T(8,128)}), f32[1024,1024]{1,0:T(8,128)}) %all-reduce.9.cloned.1.call-update) | async-done | bytes 4194320 | tf_op jit(solution)/shard_map/psum | solution.py:228
  298.4 6.0 multiply_reduce_fusion.4
  304.4 9.9 %fusion.43 = (bf16[1024,1024]{1,0:T(8,128)(2,1)S(1)}, f32[1024,1024]{1,0:T(8,128)}) fusion(f32[1024,1024]{1,0:T(8,128)} %fusion.72, bf16[1024,1024]{1,0:T(8,128)(2,1)} %all-gather.6.cloned.1.call-done, f32[1024,1024]{1,0:T(8,128)} %get-tuple-element.403, f32[1024]{0:T(1024)S(1)} %bitcast.257, f32[1024]{0:T(1024)S(1)} %add_rsqrt_fusion), kind=kOutput, calls=%fused_computation.67 | convolution fusion | flops 2175795200 | bytes 16785408 | tf_op jit(solution)/shard_map/dot_general | solution.py:232
  320.1 5.6 convolution_convert_fusion
  328.5 6.9 convolution_convert_fusion.1
  335.9 6.4 convolution_convert_fusion.2
  342.3 131.7 %all-reduce.11.cloned.1.call-done = f32[1024,1024]{1,0:T(8,128)} async-done(((f32[1024,1024]{1,0:T(8,128)}), f32[1024,1024]{1,0:T(8,128)}) %all-reduce.11.cloned.1.call-update) | async-done | bytes 4194320 | tf_op jit(solution)/shard_map/psum | solution.py:251
  474.0 5.2 multiply_reduce_fusion.1
  508.4 22.5 %reduce-scatter.19.cloned.1.call-done = bf16[128,256]{1,0:T(8,128)(2,1)} async-done(((bf16[1024,256]{1,0:T(8,128)(2,1)}), bf16[128,256]{1,0:T(8,128)(2,1)}) %reduce-scatter.19.cloned.1.call-update) | async-done | bytes 65552
  532.5 123.9 %all-reduce.13.cloned.1.call-done = (bf16[1024,1024]{1,0:T(8,128)(2,1)}, bf16[1024,1024]{1,0:T(8,128)(2,1)}) async-done(((bf16[1024,1024]{1,0:T(8,128)(2,1)}, bf16[1024,1024]{1,0:T(8,128)(2,1)}), (bf16[1024,1024]{1,0:T(8,128)(2,1)}, bf16[1024,1024]{1,0:T(8,128)(2,1)})) %all-reduce.13.cloned.1.call-update) | async-done | bytes 4194320 | tf_op jit(solution)/shard_map/psum | solution.py:235
  656.4 7.6 fusion.39
  671.1 11.4 %broadcast.171.clone = f32[4,2048,1024]{2,1,0:T(8,128)} broadcast(f32[]{:T(128)} %constant.111.clone.1), dimensions={} | broadcast | bytes 33554436 | tf_op jit(solution)/shard_map/broadcast.24
  682.6 85.5 %while.93 = (s32[]{:T(128)}, f32[4,2048,1024]{2,1,0:T(8,128)}, s32[4,256]{1,0:T(4,128)S(1)}, bf16[4,256,1024]{2,1,0:T(8,128)(2,1)S(1)}, s32[]{:T(128)}, /*index=5*/s32[]{:T(128)}, s32[]{:T(128)}, s32[]{:T(128)}) while((s32[]{:T(128)}, f32[4,2048,1024]{2,1,0:T(8,128)}, s32[4,256]{1,0:T(4,128)S(1)}, ...), condition=%wide.region_13.14_spmd.clone, body=%wide.region_10.13_spmd.clone.sunk | while | flops 541327360 | bytes 34885388 | solution.py:69
  682.7 13.1 %while.99 = (s32[]{:T(128)}, f32[2048,1024]{1,0:T(8,128)}, s32[2,128]{1,0:T(2,128)S(1)}, s32[2048]{0:T(1024)S(1)}, bf16[2,128,1024]{2,1,0:T(8,128)(2,1)S(1)}, /*index=5*/s32[]{:T(128)}, s32[]{:T(128)}) while((s32[]{:T(128)}, f32[2048,1024]{1,0:T(8,128)}, s32[2,128]{1,0:T(2,128)S(1)}, s32[2048]{0:T(1024)S(1)}, ...), condition=%wide.region_12.12_spmd.clone, body=%wide.region_11.11_spmd.clone.sunk | while | flops 541327360 | bytes 17049188 | solution.py:64
  682.7 4.8 select_add_fusion.5
  687.5 8.2 select_add_fusion.5
  695.7 8.3 bitcast_dynamic-update-slice_fusion.9
  704.1 13.0 %while.99 = (s32[]{:T(128)}, f32[2048,1024]{1,0:T(8,128)}, s32[2,128]{1,0:T(2,128)S(1)}, s32[2048]{0:T(1024)S(1)}, bf16[2,128,1024]{2,1,0:T(8,128)(2,1)S(1)}, /*index=5*/s32[]{:T(128)}, s32[]{:T(128)}) while((s32[]{:T(128)}, f32[2048,1024]{1,0:T(8,128)}, s32[2,128]{1,0:T(2,128)S(1)}, s32[2048]{0:T(1024)S(1)}, ...), condition=%wide.region_12.12_spmd.clone, body=%wide.region_11.11_spmd.clone.sunk | while | flops 541327360 | bytes 17049188 | solution.py:64
  704.1 4.8 select_add_fusion.5
  708.9 8.1 select_add_fusion.5
  717.1 8.3 bitcast_dynamic-update-slice_fusion.9
  725.4 13.0 %while.99 = (s32[]{:T(128)}, f32[2048,1024]{1,0:T(8,128)}, s32[2,128]{1,0:T(2,128)S(1)}, s32[2048]{0:T(1024)S(1)}, bf16[2,128,1024]{2,1,0:T(8,128)(2,1)S(1)}, /*index=5*/s32[]{:T(128)}, s32[]{:T(128)}) while((s32[]{:T(128)}, f32[2048,1024]{1,0:T(8,128)}, s32[2,128]{1,0:T(2,128)S(1)}, s32[2048]{0:T(1024)S(1)}, ...), condition=%wide.region_12.12_spmd.clone, body=%wide.region_11.11_spmd.clone.sunk | while | flops 541327360 | bytes 17049188 | solution.py:64
  730.2 8.1 select_add_fusion.5
  738.4 8.3 bitcast_dynamic-update-slice_fusion.9
  746.8 13.0 %while.99 = (s32[]{:T(128)}, f32[2048,1024]{1,0:T(8,128)}, s32[2,128]{1,0:T(2,128)S(1)}, s32[2048]{0:T(1024)S(1)}, bf16[2,128,1024]{2,1,0:T(8,128)(2,1)S(1)}, /*index=5*/s32[]{:T(128)}, s32[]{:T(128)}) while((s32[]{:T(128)}, f32[2048,1024]{1,0:T(8,128)}, s32[2,128]{1,0:T(2,128)S(1)}, s32[2048]{0:T(1024)S(1)}, ...), condition=%wide.region_12.12_spmd.clone, body=%wide.region_11.11_spmd.clone.sunk | while | flops 541327360 | bytes 17049188 | solution.py:64
  751.6 8.1 select_add_fusion.5
  759.8 8.3 bitcast_dynamic-update-slice_fusion.9
  768.1 6.4 fusion.38
  774.5 11.3 %broadcast.171.clone.1 = f32[4,2048,1024]{2,1,0:T(8,128)} broadcast(f32[]{:T(128)} %constant.111.clone.1), dimensions={} | broadcast | bytes 33554436 | tf_op jit(solution)/shard_map/broadcast.24
  785.8 85.3 %while.97 = (s32[]{:T(128)}, f32[4,2048,1024]{2,1,0:T(8,128)}, s32[4,256]{1,0:T(4,128)S(1)}, bf16[4,256,1024]{2,1,0:T(8,128)(2,1)S(1)}, s32[]{:T(128)}, /*index=5*/s32[]{:T(128)}, s32[]{:T(128)}, s32[]{:T(128)}) while((s32[]{:T(128)}, f32[4,2048,1024]{2,1,0:T(8,128)}, s32[4,256]{1,0:T(4,128)S(1)}, ...), condition=%wide.region_27.28_spmd.clone, body=%wide.region_24.27_spmd.clone.sunk | while | flops 541327360 | bytes 34885388 | solution.py:69
  785.9 13.0 %while.101 = (s32[]{:T(128)}, f32[2048,1024]{1,0:T(8,128)}, s32[2,128]{1,0:T(2,128)S(1)}, s32[2048]{0:T(1024)S(1)}, bf16[2,128,1024]{2,1,0:T(8,128)(2,1)S(1)}, /*index=5*/s32[]{:T(128)}, s32[]{:T(128)}) while((s32[]{:T(128)}, f32[2048,1024]{1,0:T(8,128)}, s32[2,128]{1,0:T(2,128)S(1)}, s32[2048]{0:T(1024)S(1)}, ...), condition=%wide.region_26.26_spmd.clone, body=%wide.region_25.25_spmd.clone.sunk | while | flops 541327360 | bytes 17049188 | solution.py:64
  790.7 8.1 select_add_fusion.4
  798.8 8.3 bitcast_dynamic-update-slice_fusion.11
  807.2 13.0 %while.101 = (s32[]{:T(128)}, f32[2048,1024]{1,0:T(8,128)}, s32[2,128]{1,0:T(2,128)S(1)}, s32[2048]{0:T(1024)S(1)}, bf16[2,128,1024]{2,1,0:T(8,128)(2,1)S(1)}, /*index=5*/s32[]{:T(128)}, s32[]{:T(128)}) while((s32[]{:T(128)}, f32[2048,1024]{1,0:T(8,128)}, s32[2,128]{1,0:T(2,128)S(1)}, s32[2048]{0:T(1024)S(1)}, ...), condition=%wide.region_26.26_spmd.clone, body=%wide.region_25.25_spmd.clone.sunk | while | flops 541327360 | bytes 17049188 | solution.py:64
  812.0 8.1 select_add_fusion.4
  820.2 8.3 bitcast_dynamic-update-slice_fusion.11
  828.5 13.0 %while.101 = (s32[]{:T(128)}, f32[2048,1024]{1,0:T(8,128)}, s32[2,128]{1,0:T(2,128)S(1)}, s32[2048]{0:T(1024)S(1)}, bf16[2,128,1024]{2,1,0:T(8,128)(2,1)S(1)}, /*index=5*/s32[]{:T(128)}, s32[]{:T(128)}) while((s32[]{:T(128)}, f32[2048,1024]{1,0:T(8,128)}, s32[2,128]{1,0:T(2,128)S(1)}, s32[2048]{0:T(1024)S(1)}, ...), condition=%wide.region_26.26_spmd.clone, body=%wide.region_25.25_spmd.clone.sunk | while | flops 541327360 | bytes 17049188 | solution.py:64
  833.4 8.1 select_add_fusion.4
  841.5 8.3 bitcast_dynamic-update-slice_fusion.11
  849.9 13.0 %while.101 = (s32[]{:T(128)}, f32[2048,1024]{1,0:T(8,128)}, s32[2,128]{1,0:T(2,128)S(1)}, s32[2048]{0:T(1024)S(1)}, bf16[2,128,1024]{2,1,0:T(8,128)(2,1)S(1)}, /*index=5*/s32[]{:T(128)}, s32[]{:T(128)}) while((s32[]{:T(128)}, f32[2048,1024]{1,0:T(8,128)}, s32[2,128]{1,0:T(2,128)S(1)}, s32[2048]{0:T(1024)S(1)}, ...), condition=%wide.region_26.26_spmd.clone, body=%wide.region_25.25_spmd.clone.sunk | while | flops 541327360 | bytes 17049188 | solution.py:64
  854.7 8.1 select_add_fusion.4
  862.8 8.3 bitcast_dynamic-update-slice_fusion.11
  874.4 24.5 %fusion.31 = bf16[8192,1024]{1,0:T(8,128)(2,1)} fusion(f32[4,2048,1024]{2,1,0:T(8,128)} %get-tuple-element.228, bf16[8192,1024]{1,0:T(8,128)(2,1)} %bitcast.222), kind=kLoop, calls=%fused_computation.49 | loop fusion | flops 25165824 | bytes 67108864 | tf_op jit(solution)/shard_map/convert_element_type | solution.py:244
  900.5 22.7 %fusion.30 = bf16[8192,1024]{1,0:T(8,128)(2,1)} fusion(f32[4,2048,1024]{2,1,0:T(8,128)} %get-tuple-element.230, bf16[8192,1024]{1,0:T(8,128)(2,1)} %bitcast.224), kind=kLoop, calls=%fused_computation.47 | loop fusion | flops 25165824 | bytes 67108864 | tf_op jit(solution)/shard_map/convert_element_type | solution.py:278
  923.2 13.8 %all-reduce.3 = (bf16[1024]{0:T(1024)(128)(2,1)S(1)}, bf16[1024]{0:T(1024)(128)(2,1)S(1)}, bf16[1024]{0:T(1024)(128)(2,1)S(1)}) all-reduce(bf16[1024]{0:T(1024)(128)(2,1)S(1)} %copy-done.49, bf16[1024]{0:T(1024)(128)(2,1)S(1)} %copy-done.48, bf16[1024]{0:T(1024)(128)(2,1)S(1)} %copy-done.47), channel_id=8, replica_groups=mesh['batch'=8,'tensor'=4] {'batch'}, use_global_device_ids=true, to_apply=%region_35.36.clone | all-reduce | flops 3072 | bytes 12288
  (354 shorter events, 224.2 us)
Async XLA Ops:
  8.0 29.8 %copy-start.31 = (s32[4,256]{1,0:T(4,128)S(1)}, s32[4,256]{1,0:T(4,128)}, u32[]{:S(2)}) copy-start(s32[4,256]{1,0:T(4,128)} %param.31) | copy-start | bytes 12292
  8.0 207.0 %all-gather.8.cloned.1.call-start = ((), (), s32[]{:S(2)}) async-start(), calls=%async_computation.8 | async-start | bytes 2359296 | tf_op jit(solution)/shard_map/all_gather | solution.py:167
  9.9 288.5 %all-reduce.9.cloned.1.call-start = ((), (), s32[]{:S(2)}) async-start(), calls=%async_computation.6 | async-start | bytes 8388608 | tf_op jit(solution)/shard_map/psum | solution.py:228
  20.8 643.8 %copy-start.32 = (f32[8,1,128]{2,1,0:T(1,128)}, f32[8,1,128]{2,1,0:T(1,128)S(1)}, u32[]{:S(2)}) copy-start(f32[8,1,128]{2,1,0:T(1,128)S(1)} %convert_element_type.261) | copy-start | bytes 12292
  84.4 3.4 copy-start
  87.2 2.4 copy-start.14
  87.8 568.6 %copy-start.38 = (f32[1,2,4,128]{3,1,2,0:T(2,128)}, f32[1,2,4,128]{3,1,2,0:T(2,128)S(1)}, u32[]{:S(2)}) copy-start(f32[1,2,4,128]{3,1,2,0:T(2,128)S(1)} %copy.92) | copy-start | bytes 12292
  88.3 1.3 copy-start.28
  93.2 33.8 %copy-start.6 = (bf16[4,256,4,64]{1,3,2,0:T(8,128)(2,1)}, bf16[4,256,4,64]{1,3,2,0:T(8,128)(2,1)S(1)}, u32[]{:S(2)}) copy-start(bf16[4,256,4,64]{1,3,2,0:T(8,128)(2,1)S(1)} %copy.60) | copy-start | bytes 1572868
  102.3 8.2 copy-start.20
  121.4 5.2 copy-start.52
  126.6 1.9 copy-start.8
  127.0 1.5 copy-start.12
  127.9 2.0 copy-start.1
  130.4 9.2 copy-start.10
  143.2 161.2 %all-gather.6.cloned.1.call-start = ((), (), s32[]{:S(2)}) async-start(), calls=%async_computation.7 | async-start | bytes 2359296 | tf_op jit(solution)/shard_map/all_gather | solution.py:165
  145.0 329.0 %all-reduce.11.cloned.1.call-start = ((), (), s32[]{:S(2)}) async-start(), calls=%async_computation.9 | async-start | bytes 8388608 | tf_op jit(solution)/shard_map/psum | solution.py:251
  147.6 47.5 %copy-start.53 = (f32[128]{0:T(128)S(1)}, f32[128]{0:T(128)}, u32[]{:S(2)}) copy-start(f32[128]{0:T(128)} %param.39) | copy-start | bytes 1540
  147.6 56.0 %copy-start.54 = (f32[128]{0:T(128)S(1)}, f32[128]{0:T(128)}, u32[]{:S(2)}) copy-start(f32[128]{0:T(128)} %param.40) | copy-start | bytes 1540
  203.6 275.7 %copy-start.34 = (f32[8,1,128]{2,1,0:T(1,128)}, f32[8,1,128]{2,1,0:T(1,128)S(1)}, u32[]{:S(2)}) copy-start(f32[8,1,128]{2,1,0:T(1,128)S(1)} %convert_element_type.262) | copy-start | bytes 12292
  215.0 6.7 copy-start.29
  304.4 174.9 %copy-start.36 = (f32[1024]{0:T(1024)}, f32[1024]{0:T(1024)S(1)}, u32[]{:S(2)}) copy-start(f32[1024]{0:T(1024)S(1)} %add_rsqrt_fusion) | copy-start | bytes 12292
  304.4 11.3 %copy-start.51 = (bf16[1024,1024]{1,0:T(8,128)(2,1)S(1)}, bf16[1024,1024]{1,0:T(8,128)(2,1)}, u32[]{:S(2)}) copy-start(bf16[1024,1024]{1,0:T(8,128)(2,1)} %all-gather.6.cloned.1.call-done) | copy-start | bytes 6291460
  314.3 1.4 copy-start.56
  320.1 184.5 %reduce-scatter.21.cloned.1.call-start = ((), (), s32[]{:S(2)}) async-start(), calls=%async_computation.15 | async-start | bytes 2359296
  328.4 178.1 %reduce-scatter.17.cloned.1.call-start = ((), (), s32[]{:S(2)}) async-start(), calls=%async_computation.13 | async-start | bytes 2359296 | tf_op jit(solution)/shard_map/reduce_scatter | solution.py:294
  328.5 7.4 copy-start.50
  335.4 195.4 %reduce-scatter.19.cloned.1.call-start = ((), (), s32[]{:S(2)}) async-start(), calls=%async_computation.14 | async-start | bytes 589824
  474.0 5.3 copy-start.3
  474.0 5.9 copy-start.4
  479.9 3.2 copy-start.40
  479.9 3.2 copy-start.11
  483.1 1.7 copy-start.25
  486.0 4.2 copy-start.13
  486.6 3.6 copy-start.2
  491.3 1.1 copy-start.7
  492.4 1.0 copy-start.9
  492.8 1.8 copy-start.15
  493.4 4.4 copy-start.16
  494.1 3.6 copy-start.23
  494.7 2.8 copy-start.18
  497.5 1.0 copy-start.21
  497.5 158.8 %all-reduce.13.cloned.1.call-start = ((), (), s32[]{:S(2)}) async-start(), calls=%async_computation.16 | async-start | bytes 8388608 | tf_op jit(solution)/shard_map/psum | solution.py:235
  497.7 2.2 copy-start.5
  502.1 436.7 %reduce-scatter.15.cloned.1.call-start = ((), (), s32[]{:S(2)}) async-start(), calls=%async_computation.12 | async-start | bytes 589824 | tf_op jit(solution)/shard_map/reduce_scatter | solution.py:288
  656.4 8.2 copy-start.44
  664.0 7.0 copy-start.42
  668.1 1.4 copy-start.26
  671.1 269.2 %reduce-scatter.13.cloned.1.call-start = ((), (), s32[]{:S(2)}) async-start(), calls=%async_computation.11 | async-start | bytes 589824 | tf_op jit(solution)/shard_map/reduce_scatter | solution.py:285
  682.5 85.5 %copy-start.33 = (f32[8,1,128]{2,1,0:T(1,128)S(1)}, f32[8,1,128]{2,1,0:T(1,128)}, u32[]{:S(2)}) copy-start(f32[8,1,128]{2,1,0:T(1,128)} %copy-done.32) | copy-start | bytes 12292
  682.5 85.5 %copy-start.35 = (f32[8,1,128]{2,1,0:T(1,128)S(1)}, f32[8,1,128]{2,1,0:T(1,128)}, u32[]{:S(2)}) copy-start(f32[8,1,128]{2,1,0:T(1,128)} %copy-done.34) | copy-start | bytes 12292
  682.5 85.5 %copy-start.37 = (f32[1024]{0:T(1024)S(1)}, f32[1024]{0:T(1024)}, u32[]{:S(2)}) copy-start(f32[1024]{0:T(1024)} %copy-done.36) | copy-start | bytes 12292
  682.5 85.5 %copy-start.39 = (f32[1,2,4,128]{3,1,2,0:T(2,128)S(1)}, f32[1,2,4,128]{3,1,2,0:T(2,128)}, u32[]{:S(2)}) copy-start(f32[1,2,4,128]{3,1,2,0:T(2,128)} %copy-done.38) | copy-start | bytes 12292
  682.5 85.5 %copy-start.41 = (f32[1024]{0:T(1024)S(1)}, f32[1024]{0:T(1024)}, u32[]{:S(2)}) copy-start(f32[1024]{0:T(1024)} %copy-done.40) | copy-start | bytes 12292
  682.5 85.5 %copy-start.43 = (f32[1024]{0:T(1024)S(1)}, f32[1024]{0:T(1024)}, u32[]{:S(2)}) copy-start(f32[1024]{0:T(1024)} %copy-done.42) | copy-start | bytes 12292
  682.5 85.5 %copy-start.45 = (f32[1024]{0:T(1024)S(1)}, f32[1024]{0:T(1024)}, u32[]{:S(2)}) copy-start(f32[1024]{0:T(1024)} %bitcast_convert_fusion.1) | copy-start | bytes 12292
  682.5 85.5 %copy-start.46 = (f32[1024]{0:T(1024)S(1)}, f32[1024]{0:T(1024)}, u32[]{:S(2)}) copy-start(f32[1024]{0:T(1024)} %broadcast_multiply_fusion) | copy-start | bytes 12292
  785.8 85.3 %copy-start.19 = (bf16[32,8,4,256]{3,1,2,0:T(8,128)(2,1)S(1)}, bf16[32,8,4,256]{3,1,2,0:T(8,128)(2,1)}, u32[]{:S(2)}) copy-start(bf16[32,8,4,256]{3,1,2,0:T(8,128)(2,1)} %copy-done.18) | copy-start | bytes 1572868
  874.3 70.5 %reduce-scatter.11.cloned.1.call-start = ((), (), s32[]{:S(2)}) async-start(), calls=%async_computation.10 | async-start | bytes 589824 | tf_op jit(solution)/shard_map/reduce_scatter | solution.py:282
  874.4 24.5 %copy-start.17 = (bf16[32,8,4,256]{3,1,2,0:T(8,128)(2,1)S(1)}, bf16[32,8,4,256]{3,1,2,0:T(8,128)(2,1)}, u32[]{:S(2)}) copy-start(bf16[32,8,4,256]{3,1,2,0:T(8,128)(2,1)} %copy-done.16) | copy-start | bytes 1572868
  874.4 24.5 %copy-start.27 = (bf16[4,256,1024]{2,1,0:T(8,128)(2,1)S(1)}, bf16[4,256,1024]{2,1,0:T(8,128)(2,1)}, u32[]{:S(2)}) copy-start(bf16[4,256,1024]{2,1,0:T(8,128)(2,1)} %copy-done.26) | copy-start | bytes 6291460
  900.4 22.7 %copy-start.47 = (bf16[1024]{0:T(1024)(128)(2,1)S(1)}, bf16[1024]{0:T(1024)(128)(2,1)}, u32[]{:S(2)}) copy-start(bf16[1024]{0:T(1024)(128)(2,1)} %get-tuple-element.406) | copy-start | bytes 6148
  900.5 22.7 %copy-start.48 = (bf16[1024]{0:T(1024)(128)(2,1)S(1)}, bf16[1024]{0:T(1024)(128)(2,1)}, u32[]{:S(2)}) copy-start(bf16[1024]{0:T(1024)(128)(2,1)} %get-tuple-element.321) | copy-start | bytes 6148
  900.5 22.7 %copy-start.49 = (bf16[1024]{0:T(1024)(128)(2,1)S(1)}, bf16[1024]{0:T(1024)(128)(2,1)}, u32[]{:S(2)}) copy-start(bf16[1024]{0:T(1024)(128)(2,1)} %get-tuple-element.323) | copy-start | bytes 6148
  (4 other events, 3.3 us)
Sparse Core Ops, SparseCore 0:
  10.9 30.8 all-gather.7
  146.1 28.2 all-gather.5
  328.5 40.2 reduce-scatter.20
  372.0 41.1 reduce-scatter.16
  497.6 33.1 reduce-scatter.18
  671.2 33.1 reduce-scatter.14
  874.4 33.0 reduce-scatter.12
  910.6 34.1 reduce-scatter.10
Sparse Core Ops, SparseCore 1:
  143.3 155.0 all-reduce.8
  320.2 153.8 all-reduce.10
  502.2 154.1 all-reduce.12
where the time goes:
time: 962 us; the launch traced here: 954 us
  waiting for transfers between devices  358 us (37%)
  matrix products  221 us (23%)
  local copies, waits for them, and re-layouts  171 us (18%)
  other arithmetic  105 us (11%)
  blocking collectives  79.9 us (8%)
  between operations  17.4 us (2%)
    psum x1, waiting for transfers between devices, shards(): d_mlp_in = lax.psum(d_mlp_part, 'tensor')  132 us
    psum x1, waiting for transfers between devices, shards(): lax.psum(mlp_part.astype(jnp.bfloat16), 'tensor').astype(jnp.float32)  124 us
    dot_general x22, matrix products, contract_rows(): lax.dot_general(left, right, (((0,), (0,)), ((), ())), preferred_element_...  123 us
    psum x1, waiting for transfers between devices, shards(): attn_out = lax.psum(attn_part, 'tensor')  76.7 us
    dynamic_update_slice x8, local copies, waits for them, and re-layouts, place_rows(): return lax.map(place_one_sequence, (values, routes))  66.4 us
    dot_general x16, matrix products, one_block(): return jnp.dot(chooser, seq_table, preferred_element_type=jnp.float32)  47.4 us
    squeeze x8, local copies, waits for them, and re-layouts, pick_rows(): return lax.map(pick_one_sequence, (table, routes))  37.7 us
    another operation x4, local copies, waits for them, and re-layouts  27.8 us
  transfers between devices with their start and end apart: 11, of which 5 were waited for; matrix products, arithmetic and copies ran while one was open for 48% of the time, Pallas kernels for 0%

commit v1 on v0

v1 whole, which is shorter than its diff:
```python
import functools

import jax
import jax.numpy as jnp
from jax import lax
from jax.experimental import pallas as pl
from jax.experimental.pallas import tpu as pltpu
from jax.sharding import PartitionSpec as P

HEAD_DIM = 64
SLOT_BLOCK = 512
EPSILON = 1e-06


def gelu_tanh(values):
    return (
        0.5
        * values
        * (1.0 + jnp.tanh(0.7978845608028654 * (values + 0.044715 * values * values * values)))
    )


def product(left, right):
    return jnp.dot(left, right, preferred_element_type=jnp.float32)


def contract_rows(left, right):
    return lax.dot_general(
        left, right, (((0,), (0,)), ((), ())), preferred_element_type=jnp.float32
    )


def times_transposed(left, right):
    return lax.dot_general(
        left, right, (((1,), (1,)), ((), ())), preferred_element_type=jnp.float32
    )


def norm_backward(d_normed_in, normed, inverse, gain_vec):
    d_scaled = d_normed_in * gain_vec
    d_input = inverse * (d_scaled - normed * jnp.mean(d_scaled * normed, axis=-1, keepdims=True))
    return (d_input, jnp.sum(d_normed_in * normed, axis=0))


def norm_forward(values):
    inverse = lax.rsqrt(jnp.mean(values * values, axis=-1, keepdims=True) + EPSILON)
    return (values * inverse, inverse)


def pick_kernel(order_ref, routes_ref, tokens_ref, cot_ref, routed_ref, cot_routed_ref):
    block = pl.program_id(1)
    capacity = routes_ref.shape[1]
    slots = tokens_ref.shape[1]
    column = lax.broadcasted_iota(jnp.int32, (capacity, slots), 1) + block * slots
    chooser = (routes_ref[0] == column).astype(jnp.bfloat16)
    part = product(chooser, tokens_ref[0])
    cot_part = product(chooser, cot_ref[0])

    @pl.when(block == 0)
    def _():
        routed_ref[0] = part
        cot_routed_ref[0] = cot_part

    @pl.when(block > 0)
    def _():
        routed_ref[0] += part
        cot_routed_ref[0] += cot_part


def pick_rows(tokens, cotangent, routes, order, count):
    seq_count, slots, features = tokens.shape
    capacity = routes.shape[1]
    per_block = min(SLOT_BLOCK, slots)
    table = pl.BlockSpec((1, per_block, features), lambda i, j, order: (order[i], j, 0))
    picked = pl.BlockSpec((1, capacity, features), lambda i, j, order: (i, 0, 0))
    shape = jax.ShapeDtypeStruct((count, capacity, features), jnp.float32)
    return pl.pallas_call(
        pick_kernel,
        out_shape=(shape, shape),
        grid_spec=pltpu.PrefetchScalarGridSpec(
            num_scalar_prefetch=1,
            grid=(count, slots // per_block),
            in_specs=[
                pl.BlockSpec((1, capacity, 1), lambda i, j, order: (order[i], 0, 0)),
                table,
                table,
            ],
            out_specs=[picked, picked],
        ),
        compiler_params=pltpu.CompilerParams(vmem_limit_bytes=32 << 20),
        name="pick_rows",
    )(order, routes[:, :, None], tokens, cotangent)


def place_kernel(order_ref, routes_ref, table_ref, values_ref, out_ref):
    block = pl.program_id(1)
    slots = table_ref.shape[1]
    capacity = routes_ref.shape[2]
    row = lax.broadcasted_iota(jnp.int32, (slots, capacity), 0) + block * slots
    chooser = (routes_ref[0] == row).astype(jnp.bfloat16)
    placed = product(chooser, values_ref[0])
    out_ref[0] = (table_ref[0].astype(jnp.float32) + placed).astype(jnp.bfloat16)


def place_rows(table, values, routes, order):
    seq_count, slots, features = table.shape
    capacity = routes.shape[1]
    per_block = min(SLOT_BLOCK, slots)
    tall = pl.BlockSpec((1, per_block, features), lambda i, j, order: (order[i], j, 0))
    return pl.pallas_call(
        place_kernel,
        out_shape=jax.ShapeDtypeStruct(table.shape, table.dtype),
        grid_spec=pltpu.PrefetchScalarGridSpec(
            num_scalar_prefetch=1,
            grid=(seq_count, slots // per_block),
            in_specs=[
                pl.BlockSpec((1, 1, capacity), lambda i, j, order: (order[i], 0, 0)),
                tall,
                pl.BlockSpec((1, capacity, features), lambda i, j, order: (i, 0, 0)),
            ],
            out_specs=tall,
        ),
        compiler_params=pltpu.CompilerParams(vmem_limit_bytes=32 << 20),
        name="place_rows",
    )(order, routes[:, None, :], table, values)


def causal_allowed(live_count, capacity):
    position = jnp.arange(capacity)
    allowed = position[None, :] <= position[:, None]
    allowed = allowed[None, None] & (
        position[None, None, None, :] < live_count[:, None, None, None]
    )
    return allowed


def attend_forward(queries, keys_all, vals_all, live_count, scale_qk):
    raw_scores = (
        jnp.einsum("sqhd,skhd->shqk", queries, keys_all, preferred_element_type=jnp.float32)
        * scale_qk
    )
    masked = jnp.where(causal_allowed(live_count, queries.shape[1]), raw_scores, -1e30)
    row_max = jnp.max(masked, axis=-1, keepdims=True)
    exp_scores = jnp.exp(masked - row_max)
    row_total = jnp.sum(exp_scores, axis=-1, keepdims=True)
    attn_probs = (exp_scores / row_total).astype(jnp.bfloat16)
    log_total = row_max + jnp.log(row_total)
    heads_out = jnp.einsum(
        "shqk,skhd->sqhd", attn_probs, vals_all, preferred_element_type=jnp.float32
    )
    return (heads_out.astype(jnp.bfloat16), log_total)


def attend_backward(queries, keys_all, vals_all, d_heads, log_total, live_count, scale_qk):
    raw_scores = (
        jnp.einsum("sqhd,skhd->shqk", queries, keys_all, preferred_element_type=jnp.float32)
        * scale_qk
    )
    masked = jnp.where(causal_allowed(live_count, queries.shape[1]), raw_scores, -1e30)
    attn_probs = jnp.exp(masked - log_total)
    d_vals = jnp.einsum(
        "shqk,sqhd->skhd",
        attn_probs.astype(jnp.bfloat16),
        d_heads,
        preferred_element_type=jnp.float32,
    ).astype(jnp.bfloat16)
    d_probs = jnp.einsum("sqhd,skhd->shqk", d_heads, vals_all, preferred_element_type=jnp.float32)
    d_scores = (
        attn_probs * (d_probs - jnp.sum(d_probs * attn_probs, axis=-1, keepdims=True))
    ).astype(jnp.bfloat16)
    d_queries = (
        jnp.einsum("shqk,skhd->sqhd", d_scores, keys_all, preferred_element_type=jnp.float32)
        * scale_qk
    ).astype(jnp.bfloat16)
    d_keys = (
        jnp.einsum("shqk,sqhd->skhd", d_scores, queries, preferred_element_type=jnp.float32)
        * scale_qk
    ).astype(jnp.bfloat16)
    return (d_queries, d_keys, d_vals)


class Exchange:
    def __init__(self, mesh):
        self.batch = mesh.shape["batch"]
        self.tensor = mesh.shape["tensor"]
        bits = []
        bit = self.batch // 2
        while bit:
            bits.append(bit)
            bit //= 2
        self.core = bits[-1]
        self.chips = bits[:-1]

    def swap(self, array, bit):
        return lax.ppermute(array, "batch", [(i, i ^ bit) for i in range(self.batch)])

    def shift(self, array, step):
        size = self.tensor
        return lax.ppermute(array, "tensor", [(i, (i + step) % size) for i in range(size)])

    def block_order(self):
        order = [0]
        for bit in reversed([self.core] + self.chips):
            order = order + [place ^ bit for place in order]
        return order

    def gather_rows(self, array, flip):
        rows, width = array.shape
        places = len(self.chips)
        total = array.reshape((1,) * places + array.shape)
        sequence = range(places)
        for place in sequence if flip else reversed(sequence):
            other = self.swap(total, self.chips[place])
            total = jnp.concatenate([total, other], axis=place)
        half = total.reshape(rows * self.batch // 2, width)
        return half, self.swap(half, self.core)

    def gather_tensor(self, array):
        pieces = [array]
        for _ in range(self.tensor - 1):
            pieces.append(self.shift(pieces[-1], 1))
        return pieces

    def scatter_rows(self, kept, sent, flip):
        places = len(self.chips)
        total = add_rounded(kept, self.swap(sent, self.core))
        rows = total.shape[0] // (self.batch // 2)
        total = total.reshape((2,) * places + (rows, total.shape[1]))
        sequence = range(places)
        for place in reversed(sequence) if flip else sequence:
            own = lax.slice_in_dim(total, 0, 1, axis=place)
            other = lax.slice_in_dim(total, 1, 2, axis=place)
            total = add_rounded(own, self.swap(other, self.chips[place]))
        return total.reshape(rows, total.shape[-1])

    def scatter_tensor(self, pieces):
        total = pieces[-1]
        for piece in reversed(pieces[:-1]):
            total = add_rounded(piece, self.shift(total, -1))
        return total


def add_rounded(left, right):
    return (left.astype(jnp.float32) + right.astype(jnp.float32)).astype(jnp.bfloat16)


def swap_blocks(values, device, bits, blocks):
    shape = values.shape
    spread = values.reshape(shape[:-1] + (2,) * len(bits) + (shape[-1] // blocks,))
    first = len(shape) - 1
    for place, bit in enumerate(bits):
        spread = jnp.where((device & bit) != 0, jnp.flip(spread, axis=first + place), spread)
    return spread.reshape(shape)


def shards(
    mesh,
    tokens,
    lengths,
    routes,
    w_query,
    w_key,
    w_value,
    w_out,
    w_up,
    w_down,
    gain_attn,
    gain_mlp,
    w_router,
    cotangent,
):
    low = jnp.bfloat16
    moves = Exchange(mesh)
    device = lax.axis_index("batch")
    column = lax.axis_index("tensor")
    seq_count, capacity = routes.shape
    feature_count = tokens.shape[1]
    slot_count = tokens.shape[0] // seq_count
    tokens = tokens.reshape(seq_count, slot_count, feature_count)
    cotangent = cotangent.reshape(seq_count, slot_count, feature_count)
    bits = moves.chips + [moves.core]
    ways = len(bits)

    repeats = max(1, moves.tensor // seq_count)
    local_count = max(1, seq_count // moves.tensor)
    first = column // repeats if repeats > 1 else column * local_count
    order = (first + jnp.arange(local_count)).astype(jnp.int32)
    counts_once = (column % repeats) == 0

    def once(values):
        return jnp.where(counts_once, values, 0.0) if repeats > 1 else values

    def relative(values):
        swapped = swap_blocks(values, device, bits, moves.batch)
        shape = values.shape
        spread = swapped.reshape(shape[:-1] + (2,) * ways + (shape[-1] // moves.batch,))
        lead = len(shape) - 1
        axes = tuple(range(lead)) + (lead + ways - 1,) + tuple(range(lead, lead + ways - 1))
        return spread.transpose(axes + (lead + ways,)).reshape(shape)

    def absolute(values):
        shape = values.shape
        spread = values.reshape(shape[:-1] + (2,) * ways + (shape[-1] // moves.batch,))
        lead = len(shape) - 1
        axes = tuple(range(lead)) + tuple(range(lead + 1, lead + ways)) + (lead,)
        spread = spread.transpose(axes + (lead + ways,)).reshape(shape)
        return swap_blocks(spread, device, bits, moves.batch)

    wide = w_query.shape[1]
    wide_up = w_up.shape[1] // 2

    def fetch(parts, flip):
        pieces = moves.gather_tensor(jnp.concatenate([p.astype(low) for p in parts], axis=1))
        width = parts[0].shape[1]
        ordered = [
            piece[:, i * width : (i + 1) * width] for i in range(len(parts)) for piece in pieces
        ]
        return moves.gather_rows(jnp.concatenate(ordered, axis=1), flip)

    down_turned = w_down.astype(low).T
    query_key = fetch((w_query, w_key), False)
    value_out = fetch((w_value, w_out.astype(low).T), True)
    up_one = fetch((w_up[:, :wide_up],), False)
    up_two = fetch((w_up[:, wide_up:],), True)
    down_one = fetch((down_turned[:, :wide_up],), False)
    down_two = fetch((down_turned[:, wide_up:],), True)
    small = jnp.concatenate([gain_attn, gain_mlp, w_router]).astype(low)
    small = lax.all_gather(small, "batch", axis=0)
    small = small.reshape(moves.batch, 3, -1).transpose(1, 0, 2).reshape(3, feature_count)
    small = relative(small.astype(jnp.float32))
    gain_one, gain_two, router_vec = small[0], small[1], small[2]

    half = feature_count // 2
    heads_wide = wide * moves.tensor

    def forward_product(left, pair):
        return product(left[:, :half], pair[0]) + product(left[:, half:], pair[1])

    def backward_product(lefts, pairs):
        halves = []
        for side in range(2):
            total = times_transposed(lefts[0], pairs[0][side])
            for left, pair in zip(lefts[1:], pairs[1:]):
                total = total + times_transposed(left, pair[side])
            halves.append(total)
        return jnp.concatenate(halves, axis=1)

    routed, cot_routed = pick_rows(tokens, cotangent, routes, order, local_count)
    rows_total = local_count * capacity
    routed = relative(routed.reshape(rows_total, feature_count))
    cot_routed = relative(cot_routed.reshape(rows_total, feature_count))
    live_count = lax.dynamic_slice_in_dim(lengths, first, local_count) // 8
    position = jnp.arange(capacity)
    is_live = (position[None, :] < live_count[:, None]).reshape(rows_total)
    router_score = jnp.sum(routed * router_vec, axis=-1)
    gate_prob = 1.0 / (1.0 + jnp.exp(-router_score))
    gate_live = jnp.where(is_live, gate_prob, 0.0)
    scale_qk = HEAD_DIM ** (-0.5)
    head_shape = (local_count, capacity, heads_wide // HEAD_DIM, HEAD_DIM)
    value_pair = tuple(side[:, :heads_wide] for side in value_out)
    out_pair = tuple(side[:, heads_wide:] for side in value_out)

    normed_one, inverse_one = norm_forward(routed)
    attn_in = (normed_one * gain_one).astype(low)
    both = forward_product(attn_in, query_key).astype(low)
    queries = both[:, :heads_wide].reshape(head_shape)
    keys_all = both[:, heads_wide:].reshape(head_shape)
    vals_all = forward_product(attn_in, value_pair).astype(low).reshape(head_shape)
    heads_four, log_total = attend_forward(queries, keys_all, vals_all, live_count, scale_qk)
    heads_out = heads_four.reshape(rows_total, heads_wide)
    attn_out = backward_product([heads_out], [out_pair])
    middle = routed + attn_out
    normed_two, inverse_two = norm_forward(middle)
    mlp_in = (normed_two * gain_two).astype(low)
    ups = (up_one, up_two)
    downs = (down_one, down_two)
    pre = [forward_product(mlp_in, pair) for pair in ups]
    hidden = [gelu_tanh(values).astype(low) for values in pre]
    mlp_out = backward_product(hidden, downs)
    branch = attn_out + mlp_out
    update = (gate_live[:, None] * branch).astype(low)
    d_branch = gate_live[:, None] * cot_routed
    d_mlp_out = d_branch.astype(low)
    d_score = gate_live * (1.0 - gate_prob) * jnp.sum(cot_routed * branch, axis=-1)

    def spread_out(rows, table):
        pieces = moves.gather_tensor(absolute(rows))
        kept = pieces[::repeats] if repeats > 1 else pieces
        values = jnp.concatenate(
            [piece.reshape(local_count, capacity, feature_count) for piece in kept], axis=0
        )
        steps = jnp.arange(0, moves.tensor, repeats)
        owners = ((column - steps) % moves.tensor).astype(jnp.int32)
        if repeats > 1:
            places = owners // repeats
        else:
            places = (owners[:, None] * local_count + jnp.arange(local_count)).reshape(-1)
        return place_rows(table, values, routes, places.astype(jnp.int32)).reshape(
            -1, feature_count
        )

    output = spread_out(update, tokens)

    def reduce(grad_of, parts, flip):
        kept = once(grad_of(0, half)).astype(low)
        sent = once(grad_of(half, feature_count)).astype(low)
        total = moves.scatter_rows(kept, sent, flip)
        width = total.shape[1] // parts // moves.tensor
        pieces = [
            jnp.concatenate(
                [
                    total[:, (i * moves.tensor + k) * width : (i * moves.tensor + k + 1) * width]
                    for i in range(parts)
                ],
                axis=1,
            )
            for k in range(moves.tensor)
        ]
        return moves.scatter_tensor(pieces)

    def reduce_product(left, right, parts, flip):
        return reduce(lambda a, b: contract_rows(left[:, a:b], right), parts, flip)

    grad_down = [
        reduce_product(d_mlp_out, values, 1, flip) for values, flip in zip(hidden, (False, True))
    ]
    d_hidden = [forward_product(d_mlp_out, pair) for pair in downs]
    d_pre = [
        jax.vjp(gelu_tanh, values)[1](grad)[0].astype(low) for values, grad in zip(pre, d_hidden)
    ]
    grad_up = [
        reduce_product(mlp_in, values, 1, flip) for values, flip in zip(d_pre, (False, True))
    ]
    d_mlp_in = backward_product(d_pre, ups)
    d_middle, grad_gain_mlp = norm_backward(d_mlp_in, normed_two, inverse_two, gain_two)
    d_attn_out = (d_middle + d_branch).astype(low)
    d_heads = forward_product(d_attn_out, out_pair).astype(low).reshape(head_shape)
    d_queries, d_keys, d_vals = attend_backward(
        queries, keys_all, vals_all, d_heads, log_total, live_count, scale_qk
    )
    flat_shape = (rows_total, heads_wide)
    d_both = jnp.concatenate([d_queries.reshape(flat_shape), d_keys.reshape(flat_shape)], axis=1)
    d_vals = d_vals.reshape(flat_shape)
    grad_query_key = reduce_product(attn_in, d_both, 2, False)
    grad_value_out = reduce(
        lambda a, b: jnp.concatenate(
            [
                contract_rows(attn_in[:, a:b], d_vals),
                contract_rows(d_attn_out[:, a:b], heads_out),
            ],
            axis=1,
        ),
        2,
        True,
    )
    d_attn_in = backward_product([d_both, d_vals], [query_key, value_pair])
    d_from_norm, grad_gain_attn = norm_backward(d_attn_in, normed_one, inverse_one, gain_one)
    grad_router = jnp.sum(routed * d_score[:, None], axis=0)
    d_routed = (d_middle + d_from_norm + d_score[:, None] * router_vec).astype(low)
    grad_tokens = spread_out(d_routed, cotangent)

    small_grads = absolute(jnp.stack([grad_gain_attn, grad_gain_mlp, grad_router]))
    small_grads = lax.psum(once(small_grads), ("batch", "tensor"))
    own = feature_count // moves.batch
    small_grads = lax.dynamic_slice_in_dim(small_grads, device * own, own, axis=1)

    full = jnp.float32
    return (
        output,
        grad_tokens,
        grad_query_key[:, :wide].astype(full),
        grad_query_key[:, wide:].astype(full),
        grad_value_out[:, :wide].astype(full),
        grad_value_out[:, wide:].T.astype(full),
        jnp.concatenate(grad_up, axis=1).astype(full),
        jnp.concatenate(grad_down, axis=1).T.astype(full),
        small_grads[0],
        small_grads[1],
        small_grads[2],
    )


def solution(mesh):
    in_specs = (
        P("batch", None),
        P("batch"),
        P("batch", None),
        P("batch", "tensor"),
        P("batch", "tensor"),
        P("batch", "tensor"),
        P("tensor", "batch"),
        P("batch", "tensor"),
        P("tensor", "batch"),
        P("batch"),
        P("batch"),
        P("batch"),
        P("batch", None),
    )
    out_specs = (
        P("batch", None),
        P("batch", None),
        P("batch", "tensor"),
        P("batch", "tensor"),
        P("batch", "tensor"),
        P("tensor", "batch"),
        P("batch", "tensor"),
        P("tensor", "batch"),
        P("batch"),
        P("batch"),
        P("batch"),
    )
    return jax.shard_map(
        functools.partial(shards, mesh),
        mesh=mesh,
        in_specs=in_specs,
        out_specs=out_specs,
        check_vma=False,
    )
```

time: 962 us -> 722 us (0.75)
  waiting for transfers between devices: 358 us -> 227 us
  matrix products: 221 us -> 116 us
  starting transfers between devices: 1.04 us -> 84.5 us
  local copies, waits for them, and re-layouts: 171 us -> 115 us
  Pallas kernels: 0 us -> 30.3 us
  blocking collectives: 79.9 us -> 52 us
  other arithmetic: 105 us -> 80.2 us
  between operations: 17.4 us -> 5.55 us
    psum x3 -> x0, waiting for transfers between devices: 332 us -> none  [the longest x1 132 us: shards(): d_mlp_in = lax.psum(d_mlp_part, 'tensor')]
    ppermute x0 -> x78, waiting for transfers between devices: none -> 227 us  [the longest x36 146 us: swap(): lax.ppermute(array, 'batch', [(i, i ^ bit) for i in range(self.batch)])]
    dot_general x22 -> x14, matrix products: 123 us -> 29.8 us  [contract_rows(): lax.dot_general(left, right, (((0,), (0,)), ((), ())), preferred_element_...]
    ppermute x0 -> x78, starting transfers between devices: none -> 84.5 us  [the longest x42 52.1 us: shift(): lax.ppermute(array, 'tensor', [(i, (i + step) % size) for i in range(size)])]
    dynamic_update_slice x16 -> x0, local copies, waits for them, and re-layouts: 74.8 us -> none  [the longest x8 66.4 us: place_rows(): return lax.map(place_one_sequence, (values, routes))]
    convert_element_type x25 -> x35, other arithmetic: 78.8 us -> 16.4 us  [the longest x25 9.94 us: add_rounded(): (left.astype(jnp.float32) + right.astype(jnp.float32)).astype(jnp.bfloat16)]
    all_gather x7 -> x1, blocking collectives: 66 us -> 8.91 us  [shards(): small = lax.all_gather(small, 'batch', axis=0)]
    psum x0 -> x1, blocking collectives: none -> 43.1 us  [shards(): small_grads = lax.psum(once(small_grads), ('batch', 'tensor'))]
  transfers between devices with their start and end apart: 11 -> 78, of which waited for: 5 -> 36; matrix products, arithmetic and copies ran while one was open for 48% -> 28% of each run, Pallas kernels for 0% -> 4%
where the time goes in v1:
time: 722 us; the launch traced here: 710 us
  waiting for transfers between devices  227 us (31%)
  matrix products  116 us (16%)
  local copies, waits for them, and re-layouts  115 us (16%)
  starting transfers between devices  84.5 us (12%)
  other arithmetic  80.2 us (11%)
  blocking collectives  52 us (7%)
  Pallas kernels  30.3 us (4%)
    ppermute x36, waiting for transfers between devices, swap(): lax.ppermute(array, 'batch', [(i, i ^ bit) for i in range(self.batch)])  146 us
    ppermute x42, waiting for transfers between devices, shift(): lax.ppermute(array, 'tensor', [(i, (i + step) % size) for i in range(size)])  80.2 us
    ppermute x42, starting transfers between devices, shift(): lax.ppermute(array, 'tensor', [(i, (i + step) % size) for i in range(size)])  52.1 us
    dot_general x14, matrix products, product(): return jnp.dot(left, right, preferred_element_type=jnp.float32)  43.7 us
    psum x1, blocking collectives, shards(): small_grads = lax.psum(once(small_grads), ('batch', 'tensor'))  43.1 us
    unnamed x202, local copies, waits for them, and re-layouts  42.7 us
    dot_general x14, matrix products, times_transposed(): lax.dot_general(left, right, (((1,), (1,)), ((), ())), preferred_element_...  33.1 us
    ppermute x36, starting transfers between devices, swap(): lax.ppermute(array, 'batch', [(i, i ^ bit) for i in range(self.batch)])  32.4 us
  transfers between devices with their start and end apart: 78, of which 36 were waited for; matrix products, arithmetic and copies ran while one was open for 28% of the time, Pallas kernels for 4%

profile of v1, /device:TPU:0, one launch (start us, length us, event | category | flops | bytes accessed | tf_op | source)
XLA Modules:
  0.0 710.2 jit_solution(2882193089494060296)
XLA Ops:
  2.7 3.0 collective-permute-start.12
  17.1 8.9 %all-gather = bf16[8,1,384]{2,1,0:T(2,128)(2,1)S(1)} all-gather(bf16[1,1,384]{2,1,0:T(2,128)(2,1)S(1)} %maximum_bitcast_fusion.5), channel_id=1, replica_groups=mesh['batch'=8,'tensor'=4] {'batch'}, dimensions={0}, use_global_device_ids=true | all-gather | bytes 6912 | tf_op jit(solution)/shard_map/all_gather | solution.py:328
  27.6 5.8 copy-done.1
  33.4 5.5 pick_rows.1
  43.3 4.1 rev.65
  60.6 6.1 rev.74
  69.2 5.2 collective-permute-done
  76.5 3.5 collective-permute-start.24
  80.0 2.7 collective-permute-done.7
  82.7 13.4 %collective-permute-done.30 = bf16[128,512]{1,0:T(8,128)(2,1)S(1)} collective-permute-done((bf16[128,512]{1,0:T(8,128)(2,1)}, bf16[128,512]{1,0:T(8,128)(2,1)S(1)}, u32[]{:S(2)}, u32[]{:S(2)}) %collective-permute-start.30) | collective-permute-done | bytes 131104 | tf_op jit(solution)/shard_map/ppermute | solution.py:199
  97.6 4.2 collective-permute-start.14
  101.8 5.4 collective-permute-done.31
  118.1 13.8 %collective-permute-done.3 = bf16[1,1,128,2048]{3,2,1,0:T(8,128)(2,1)S(1)} collective-permute-done((bf16[1,1,128,2048]{3,2,1,0:T(8,128)(2,1)}, bf16[1,1,128,2048]{3,2,1,0:T(8,128)(2,1)S(1)}, u32[]{:S(2)}, u32[]{:S(2)}) %collective-permute-start.3) | collective-permute-done | bytes 524320 | tf_op jit(solution)/shard_map/ppermute | solution.py:195
  139.4 7.4 %collective-permute-done.26 = bf16[1,1,128,2048]{3,2,1,0:T(8,128)(2,1)S(1)} collective-permute-done((bf16[1,1,128,2048]{3,2,1,0:T(8,128)(2,1)S(1)}, bf16[1,1,128,2048]{3,2,1,0:T(8,128)(2,1)S(1)}, u32[]{:S(2)}, u32[]{:S(2)}) %collective-permute-start.26) | collective-permute-done | bytes 524320 | tf_op jit(solution)/shard_map/ppermute | solution.py:195
  148.3 23.6 %collective-permute-done.15 = bf16[1,1,128,2048]{3,2,1,0:T(8,128)(2,1)S(1)} collective-permute-done((bf16[1,1,128,2048]{3,2,1,0:T(8,128)(2,1)S(1)}, bf16[1,1,128,2048]{3,2,1,0:T(8,128)(2,1)S(1)}, u32[]{:S(2)}, u32[]{:S(2)}) %collective-permute-start.15) | collective-permute-done | bytes 524320 | tf_op jit(solution)/shard_map/ppermute | solution.py:195
  174.3 8.8 %collective-permute-done.21 = bf16[1,1,128,2048]{3,2,1,0:T(8,128)(2,1)S(1)} collective-permute-done((bf16[1,1,128,2048]{3,2,1,0:T(8,128)(2,1)S(1)}, bf16[1,1,128,2048]{3,2,1,0:T(8,128)(2,1)S(1)}, u32[]{:S(2)}, u32[]{:S(2)}) %collective-permute-start.21) | collective-permute-done | bytes 524320 | tf_op jit(solution)/shard_map/ppermute | solution.py:195
  184.5 3.8 collective-permute-done.16
  192.4 13.2 %collective-permute-done.27 = bf16[2,1,128,2048]{3,2,1,0:T(8,128)(2,1)S(1)} collective-permute-done((bf16[2,1,128,2048]{3,2,1,0:T(8,128)(2,1)S(1)}, bf16[2,1,128,2048]{3,2,1,0:T(8,128)(2,1)S(1)}, u32[]{:S(2)}, u32[]{:S(2)}) %collective-permute-start.27) | collective-permute-done | bytes 1048608 | tf_op jit(solution)/shard_map/ppermute | solution.py:195
  207.1 2.7 collective-permute-done.22
  211.5 10.4 %collective-permute-done.33 = bf16[2,1,128,2048]{3,2,1,0:T(8,128)(2,1)S(1)} collective-permute-done((bf16[2,1,128,2048]{3,2,1,0:T(8,128)(2,1)S(1)}, bf16[2,1,128,2048]{3,2,1,0:T(8,128)(2,1)S(1)}, u32[]{:S(2)}, u32[]{:S(2)}) %collective-permute-start.33) | collective-permute-done | bytes 1048608 | tf_op jit(solution)/shard_map/ppermute | solution.py:195
  234.5 3.3 fusion.28
  245.6 15.2 %fusion.74 = f32[256,2048]{1,0:T(8,128)S(1)} fusion(bf16[512,2048]{1,0:T(8,128)(2,1)} %collective-permute-done.28, bf16[256,1024]{1,0:T(8,128)(2,1)S(1)} %multiply_convert_fusion.4), kind=kOutput, calls=%fused_computation.208 | convolution fusion | flops 536870912 | bytes 4456448 | tf_op jit(solution)/shard_map/dot_general | solution.py:24
  260.8 4.0 multiply_convert_fusion.1
  264.8 3.5 fusion.104
  273.0 4.1 multiply_convert_fusion.2
  277.1 3.1 convolution_add_fusion.11
  282.4 3.2 convolution_add_fusion.12
  287.8 5.6 multiply_reduce_fusion.4
  294.9 3.1 reshape.602
  299.3 2.5 fusion.64
  301.9 4.1 fusion.10
  306.0 2.7 fusion.106
  311.3 4.1 fusion.6
  316.4 3.2 convolution_add_fusion.10
  321.7 2.7 fusion.107
  324.5 3.1 convolution_add_fusion.9
  329.8 5.6 multiply_reduce_fusion.2
  343.9 3.1 fusion.21
  369.0 3.3 convolution_add_fusion.7
  374.6 5.5 multiply_reduce_fusion.3
  380.1 5.5 fusion.55
  387.2 4.0 rev.77
  392.6 4.0 rev.71
  403.1 2.8 pad_maximum_fusion.8
  405.9 11.1 %collective-permute-done.36 = bf16[256,1024]{1,0:T(8,128)(2,1)} collective-permute-done((bf16[256,1024]{1,0:T(8,128)(2,1)}, bf16[256,1024]{1,0:T(8,128)(2,1)}, u32[]{:S(2)}, u32[]{:S(2)}) %collective-permute-start.36) | collective-permute-done | bytes 524320 | tf_op jit(solution)/shard_map/ppermute | solution.py:199
  417.0 11.2 %collective-permute-done.39 = bf16[256,1024]{1,0:T(8,128)(2,1)} collective-permute-done((bf16[256,1024]{1,0:T(8,128)(2,1)S(1)}, bf16[256,1024]{1,0:T(8,128)(2,1)}, u32[]{:S(2)}, u32[]{:S(2)}) %collective-permute-start.39) | collective-permute-done | bytes 524320 | tf_op jit(solution)/shard_map/ppermute | solution.py:199
  428.3 43.1 %psum.7 = f32[3,1024]{1,0:T(4,128)S(1)} all-reduce(f32[3,1024]{1,0:T(4,128)S(1)} %reshape.621), channel_id=1, replica_groups=mesh['batch'=8,'tensor'=4] {'batch','tensor'}, use_global_device_ids=true, to_apply=%region_12.13 | all-reduce | flops 3072 | bytes 24576 | tf_op jit(solution)/shard_map/psum | solution.py:463
  471.4 3.4 convolution_convert_fusion.8
  483.3 17.8 %collective-permute-done.41 = bf16[256,1024]{1,0:T(8,128)(2,1)} collective-permute-done((bf16[256,1024]{1,0:T(8,128)(2,1)}, bf16[256,1024]{1,0:T(8,128)(2,1)}, u32[]{:S(2)}, u32[]{:S(2)}) %collective-permute-start.41) | collective-permute-done | bytes 524320 | tf_op jit(solution)/shard_map/ppermute | solution.py:199
  502.7 5.8 copy-done
  508.5 12.5 %place_rows.3 = bf16[4,2048,1024]{2,1,0:T(8,128)(2,1)} custom-call(s32[4]{0:T(128)S(1)} %and_select_fusion.order_ref, s32[4,1,256]{2,1,0:T(1,128)S(1)} %broadcast_in_dim.24.routes_ref, bf16[4,2048,1024]{2,1,0:T(8,128)(2,1)S(1)} %bitcast.196, bf16[4,256,1024]{2,1,0:T(8,128)(2,1)S(1)} %pad_maximum_fusion.7.values_ref), custom_call_target="tpu_custom_call" | custom-call | tf_op jit(solution)/shard_map/place_rows/pallas_call | solution.py:110
  523.1 5.8 copy-done.2
  528.9 12.3 %place_rows.2 = bf16[4,2048,1024]{2,1,0:T(8,128)(2,1)} custom-call(s32[4]{0:T(128)S(1)} %and_select_fusion.order_ref, s32[4,1,256]{2,1,0:T(1,128)S(1)} %broadcast_in_dim.24.routes_ref, bf16[4,2048,1024]{2,1,0:T(8,128)(2,1)S(1)} %bitcast.198, bf16[4,256,1024]{2,1,0:T(8,128)(2,1)S(1)} %pad_maximum_fusion.6.values_ref), custom_call_target="tpu_custom_call" | custom-call | tf_op jit(solution)/shard_map/place_rows/pallas_call | solution.py:110
  559.9 2.7 add_convert_fusion.2
  587.8 10.6 %collective-permute-done.61 = bf16[2,1,128,2048]{3,2,1,0:T(8,128)(2,1)} collective-permute-done((bf16[2,1,128,2048]{3,2,1,0:T(8,128)(2,1)}, bf16[2,1,128,2048]{3,2,1,0:T(8,128)(2,1)}, u32[]{:S(2)}, u32[]{:S(2)}) %collective-permute-start.61) | collective-permute-done | bytes 1048608 | tf_op jit(solution)/shard_map/ppermute | solution.py:195
  601.3 5.8 collective-permute-done.55
  610.4 10.4 %collective-permute-done.49 = bf16[2,1,128,2048]{2,3,1,0:T(8,128)(2,1)S(1)} collective-permute-done((bf16[2,1,128,2048]{2,3,1,0:T(8,128)(2,1)}, bf16[2,1,128,2048]{2,3,1,0:T(8,128)(2,1)S(1)}, u32[]{:S(2)}, u32[]{:S(2)}) %collective-permute-start.49) | collective-permute-done | bytes 1048608 | tf_op jit(solution)/shard_map/ppermute | solution.py:195
  622.3 7.2 %collective-permute-done.43 = bf16[1,2,128,2048]{3,2,1,0:T(8,128)(2,1)S(1)} collective-permute-done((bf16[1,2,128,2048]{3,2,1,0:T(8,128)(2,1)S(1)}, bf16[1,2,128,2048]{3,2,1,0:T(8,128)(2,1)S(1)}, u32[]{:S(2)}, u32[]{:S(2)}) %collective-permute-start.43) | collective-permute-done | bytes 1048608 | tf_op jit(solution)/shard_map/ppermute | solution.py:195
  631.5 9.2 %collective-permute-done.74 = bf16[1,1,128,2048]{2,3,1,0:T(8,128)(2,1)S(1)} collective-permute-done((bf16[1,1,128,2048]{2,3,1,0:T(8,128)(2,1)S(1)}, bf16[1,1,128,2048]{2,3,1,0:T(8,128)(2,1)S(1)}, u32[]{:S(2)}, u32[]{:S(2)}) %collective-permute-start.74) | collective-permute-done | bytes 524320 | tf_op jit(solution)/shard_map/ppermute | solution.py:195
  642.4 9.5 %collective-permute-done.62 = bf16[1,1,128,2048]{3,2,1,0:T(8,128)(2,1)S(1)} collective-permute-done((bf16[1,1,128,2048]{3,2,1,0:T(8,128)(2,1)S(1)}, bf16[1,1,128,2048]{3,2,1,0:T(8,128)(2,1)S(1)}, u32[]{:S(2)}, u32[]{:S(2)}) %collective-permute-start.62) | collective-permute-done | bytes 524320 | tf_op jit(solution)/shard_map/ppermute | solution.py:195
  653.4 9.0 %collective-permute-done.50 = bf16[1,1,128,2048]{2,3,1,0:T(8,128)(2,1)S(1)} collective-permute-done((bf16[1,1,128,2048]{2,3,1,0:T(8,128)(2,1)S(1)}, bf16[1,1,128,2048]{2,3,1,0:T(8,128)(2,1)S(1)}, u32[]{:S(2)}, u32[]{:S(2)}) %collective-permute-start.50) | collective-permute-done | bytes 524320 | tf_op jit(solution)/shard_map/ppermute | solution.py:195
  665.0 3.2 collective-permute-start.76
  697.0 2.8 collective-permute-done.65
  699.8 5.3 collective-permute-done.53
  (515 shorter events, 253.1 us)
Async XLA Ops:
  2.7 72.4 %collective-permute-start.12 = (bf16[128,512]{1,0:T(8,128)(2,1)}, bf16[128,512]{1,0:T(8,128)(2,1)}, u32[]{:S(2)}, u32[]{:S(2)}) collective-permute-start(bf16[128,512]{1,0:T(8,128)(2,1)} %get-tuple-element.95), channel_id=1, source_target_pairs={{0,1},{1,2},{2,3},{3,0},{4,5},{5,6},{6,7},{7,4},{8,9},{9,10},{10,1... | collective-permute-start | bytes 393224 | tf_op jit(solution)/shard_map/ppermute | solution.py:199
  5.7 70.7 %collective-permute-start.23 = (bf16[128,512]{1,0:T(8,128)(2,1)}, bf16[128,512]{1,0:T(8,128)(2,1)}, u32[]{:S(2)}, u32[]{:S(2)}) collective-permute-start(bf16[128,512]{1,0:T(8,128)(2,1)} %get-tuple-element.96), channel_id=1, source_target_pairs={{0,1},{1,2},{2,3},{3,0},{4,5},{5,6},{6,7},{7,4},{8,9},{9,10},{10,1... | collective-permute-start | bytes 393224 | tf_op jit(solution)/shard_map/ppermute | solution.py:199
  9.1 67.4 %collective-permute-start.18 = (bf16[128,512]{1,0:T(8,128)(2,1)S(1)}, bf16[128,512]{1,0:T(8,128)(2,1)}, u32[]{:S(2)}, u32[]{:S(2)}) collective-permute-start(bf16[128,512]{1,0:T(8,128)(2,1)S(1)} %get-tuple-element.93), channel_id=1, source_target_pairs={{0,1},{1,2},{2,3},{3,0},{4,5},{5,6},{6,7},{7,4},{8,9},{9,10},{10,1... | collective-permute-start | bytes 393224 | tf_op jit(solution)/shard_map/ppermute | solution.py:199
  10.7 69.3 %collective-permute-start.29 = (bf16[128,512]{1,0:T(8,128)(2,1)}, bf16[128,512]{1,0:T(8,128)(2,1)}, u32[]{:S(2)}, u32[]{:S(2)}) collective-permute-start(bf16[128,512]{1,0:T(8,128)(2,1)} %get-tuple-element.94), channel_id=1, source_target_pairs={{0,1},{1,2},{2,3},{3,0},{4,5},{5,6},{6,7},{7,4},{8,9},{9,10},{10,1... | collective-permute-start | bytes 393224 | tf_op jit(solution)/shard_map/ppermute | solution.py:199
  12.1 54.6 %collective-permute-start.6 = (bf16[128,512]{1,0:T(8,128)(2,1)}, bf16[128,512]{1,0:T(8,128)(2,1)}, u32[]{:S(2)}, u32[]{:S(2)}) collective-permute-start(bf16[128,512]{1,0:T(8,128)(2,1)} %pad_maximum_fusion.20), channel_id=1, source_target_pairs={{0,1},{1,2},{2,3},{3,0},{4,5},{5,6},{6,7},{7,4},{8,9},{9,10},{10,1... | collective-permute-start | bytes 393224 | tf_op jit(solution)/shard_map/ppermute | solution.py:199
  75.0 21.1 %collective-permute-start.1 = (bf16[128,512]{1,0:T(8,128)(2,1)S(1)}, bf16[128,512]{1,0:T(8,128)(2,1)S(1)}, u32[]{:S(2)}, u32[]{:S(2)}) collective-permute-start(bf16[128,512]{1,0:T(8,128)(2,1)S(1)} %collective-permute-done), channel_id=1, source_target_pairs={{0,1},{1,2},{2,3},{3,0},{4,5},{5,6},{6,7},{7,4},{8,9},{9,10},{10,1... | collective-permute-start | bytes 393224 | tf_op jit(solution)/shard_map/ppermute | solution.py:199
  76.4 20.5 %collective-permute-start.13 = (bf16[128,512]{1,0:T(8,128)(2,1)}, bf16[128,512]{1,0:T(8,128)(2,1)S(1)}, u32[]{:S(2)}, u32[]{:S(2)}) collective-permute-start(bf16[128,512]{1,0:T(8,128)(2,1)} %collective-permute-done.12), channel_id=1, source_target_pairs={{0,1},{1,2},{2,3},{3,0},{4,5},{5,6},{6,7},{7,4},{8,9},{9,10},{10,1... | collective-permute-start | bytes 393224 | tf_op jit(solution)/shard_map/ppermute | solution.py:199
  76.5 21.1 %collective-permute-start.24 = (bf16[128,512]{1,0:T(8,128)(2,1)}, bf16[128,512]{1,0:T(8,128)(2,1)S(1)}, u32[]{:S(2)}, u32[]{:S(2)}) collective-permute-start(bf16[128,512]{1,0:T(8,128)(2,1)} %collective-permute-done.23), channel_id=1, source_target_pairs={{0,1},{1,2},{2,3},{3,0},{4,5},{5,6},{6,7},{7,4},{8,9},{9,10},{10,1... | collective-permute-start | bytes 393224 | tf_op jit(solution)/shard_map/ppermute | solution.py:199
  80.0 21.8 %collective-permute-start.19 = (bf16[128,512]{1,0:T(8,128)(2,1)}, bf16[128,512]{1,0:T(8,128)(2,1)S(1)}, u32[]{:S(2)}, u32[]{:S(2)}) collective-permute-start(bf16[128,512]{1,0:T(8,128)(2,1)} %collective-permute-done.18), channel_id=1, source_target_pairs={{0,1},{1,2},{2,3},{3,0},{4,5},{5,6},{6,7},{7,4},{8,9},{9,10},{10,1... | collective-permute-start | bytes 393224 | tf_op jit(solution)/shard_map/ppermute | solution.py:199
  97.6 36.9 %collective-permute-start.14 = (bf16[128,512]{1,0:T(8,128)(2,1)S(1)}, bf16[128,512]{1,0:T(8,128)(2,1)S(1)}, u32[]{:S(2)}, u32[]{:S(2)}) collective-permute-start(bf16[128,512]{1,0:T(8,128)(2,1)S(1)} %collective-permute-done.13), channel_id=1, source_target_pairs={{0,1},{1,2},{2,3},{3,0},{4,5},{5,6},{6,7},{7,4},{8,9},{9,10},{10,1... | collective-permute-start | bytes 393224 | tf_op jit(solution)/shard_map/ppermute | solution.py:199
  107.2 30.6 %collective-permute-start.20 = (bf16[128,512]{1,0:T(8,128)(2,1)S(1)}, bf16[128,512]{1,0:T(8,128)(2,1)S(1)}, u32[]{:S(2)}, u32[]{:S(2)}) collective-permute-start(bf16[128,512]{1,0:T(8,128)(2,1)S(1)} %collective-permute-done.19), channel_id=1, source_target_pairs={{0,1},{1,2},{2,3},{3,0},{4,5},{5,6},{6,7},{7,4},{8,9},{9,10},{10,1... | collective-permute-start | bytes 393224 | tf_op jit(solution)/shard_map/ppermute | solution.py:199
  108.5 75.6 %collective-permute-start.32 = (bf16[1,1,128,2048]{3,2,1,0:T(8,128)(2,1)S(1)}, bf16[1,1,128,2048]{3,2,1,0:T(8,128)(2,1)S(1)}, u32[]{:S(2)}, u32[]{:S(2)}) collective-permute-start(bf16[1,1,128,2048]{3,2,1,0:T(8,128)(2,1)S(1)} %maximum_bitcast_fusion.3), channel_id=1, source_target_pairs={{0,16},{4,20},{8,24},{12,28},{16,0},{20,4},{24,8},{28,12},{1,17},{... | collective-permute-start | bytes 1572872 | tf_op jit(solution)/shard_map/ppermute | solution.py:195
  113.2 18.6 %collective-permute-start.3 = (bf16[1,1,128,2048]{3,2,1,0:T(8,128)(2,1)}, bf16[1,1,128,2048]{3,2,1,0:T(8,128)(2,1)S(1)}, u32[]{:S(2)}, u32[]{:S(2)}) collective-permute-start(bf16[1,1,128,2048]{3,2,1,0:T(8,128)(2,1)} %bitcast.250), channel_id=1, source_target_pairs={{0,16},{4,20},{8,24},{12,28},{16,0},{20,4},{24,8},{28,12},{1,17},{... | collective-permute-start | bytes 1572872 | tf_op jit(solution)/shard_map/ppermute | solution.py:195
  115.6 20.6 %collective-permute-start.9 = (bf16[1,1,128,2048]{3,2,1,0:T(8,128)(2,1)S(1)}, bf16[1,1,128,2048]{3,2,1,0:T(8,128)(2,1)S(1)}, u32[]{:S(2)}, u32[]{:S(2)}) collective-permute-start(bf16[1,1,128,2048]{3,2,1,0:T(8,128)(2,1)S(1)} %bitcast.247), channel_id=1, source_target_pairs={{0,8},{4,12},{8,0},{12,4},{16,24},{20,28},{24,16},{28,20},{1,9},{5... | collective-permute-start | bytes 1572872 | tf_op jit(solution)/shard_map/ppermute | solution.py:195
  131.9 14.9 %collective-permute-start.26 = (bf16[1,1,128,2048]{3,2,1,0:T(8,128)(2,1)S(1)}, bf16[1,1,128,2048]{3,2,1,0:T(8,128)(2,1)S(1)}, u32[]{:S(2)}, u32[]{:S(2)}) collective-permute-start(bf16[1,1,128,2048]{3,2,1,0:T(8,128)(2,1)S(1)} %maximum_bitcast_fusion.2), channel_id=1, source_target_pairs={{0,16},{4,20},{8,24},{12,28},{16,0},{20,4},{24,8},{28,12},{1,17},{... | collective-permute-start | bytes 1572872 | tf_op jit(solution)/shard_map/ppermute | solution.py:195
  134.5 38.0 %collective-permute-start.4 = (bf16[2,1,128,2048]{3,2,1,0:T(8,128)(2,1)S(1)}, bf16[2,1,128,2048]{3,2,1,0:T(8,128)(2,1)S(1)}, u32[]{:S(2)}, u32[]{:S(2)}) collective-permute-start(bf16[2,1,128,2048]{3,2,1,0:T(8,128)(2,1)S(1)} %pad_maximum_fusion.9), channel_id=1, source_target_pairs={{0,8},{4,12},{8,0},{12,4},{16,24},{20,28},{24,16},{28,20},{1,9},{5... | collective-permute-start | bytes 3145736 | tf_op jit(solution)/shard_map/ppermute | solution.py:195
  136.1 35.8 %collective-permute-start.15 = (bf16[1,1,128,2048]{3,2,1,0:T(8,128)(2,1)S(1)}, bf16[1,1,128,2048]{3,2,1,0:T(8,128)(2,1)S(1)}, u32[]{:S(2)}, u32[]{:S(2)}) collective-permute-start(bf16[1,1,128,2048]{3,2,1,0:T(8,128)(2,1)S(1)} %maximum_bitcast_fusion), channel_id=1, source_target_pairs={{0,8},{4,12},{8,0},{12,4},{16,24},{20,28},{24,16},{28,20},{1,9},{5... | collective-permute-start | bytes 1572872 | tf_op jit(solution)/shard_map/ppermute | solution.py:195
  137.8 45.4 %collective-permute-start.10 = (bf16[1,2,128,2048]{3,2,1,0:T(8,128)(2,1)S(1)}, bf16[1,2,128,2048]{3,2,1,0:T(8,128)(2,1)S(1)}, u32[]{:S(2)}, u32[]{:S(2)}) collective-permute-start(bf16[1,2,128,2048]{3,2,1,0:T(8,128)(2,1)S(1)} %pad_maximum_fusion.10), channel_id=1, source_target_pairs={{0,16},{4,20},{8,24},{12,28},{16,0},{20,4},{24,8},{28,12},{1,17},{... | collective-permute-start | bytes 3145736 | tf_op jit(solution)/shard_map/ppermute | solution.py:195
  146.7 36.4 %collective-permute-start.21 = (bf16[1,1,128,2048]{3,2,1,0:T(8,128)(2,1)S(1)}, bf16[1,1,128,2048]{3,2,1,0:T(8,128)(2,1)S(1)}, u32[]{:S(2)}, u32[]{:S(2)}) collective-permute-start(bf16[1,1,128,2048]{3,2,1,0:T(8,128)(2,1)S(1)} %maximum_bitcast_fusion.1), channel_id=1, source_target_pairs={{0,8},{4,12},{8,0},{12,4},{16,24},{20,28},{24,16},{28,20},{1,9},{5... | collective-permute-start | bytes 1572872 | tf_op jit(solution)/shard_map/ppermute | solution.py:195
  171.9 33.7 %collective-permute-start.27 = (bf16[2,1,128,2048]{3,2,1,0:T(8,128)(2,1)S(1)}, bf16[2,1,128,2048]{3,2,1,0:T(8,128)(2,1)S(1)}, u32[]{:S(2)}, u32[]{:S(2)}) collective-permute-start(bf16[2,1,128,2048]{3,2,1,0:T(8,128)(2,1)S(1)} %pad_maximum_fusion.14), channel_id=1, source_target_pairs={{0,8},{4,12},{8,0},{12,4},{16,24},{20,28},{24,16},{28,20},{1,9},{5... | collective-permute-start | bytes 3145736 | tf_op jit(solution)/shard_map/ppermute | solution.py:195
  172.6 15.8 %collective-permute-start.16 = (bf16[1,2,128,2048]{3,2,1,0:T(8,128)(2,1)S(1)}, bf16[1,2,128,2048]{3,2,1,0:T(8,128)(2,1)S(1)}, u32[]{:S(2)}, u32[]{:S(2)}) collective-permute-start(bf16[1,2,128,2048]{3,2,1,0:T(8,128)(2,1)S(1)} %pad_maximum_fusion.12), channel_id=1, source_target_pairs={{0,16},{4,20},{8,24},{12,28},{16,0},{20,4},{24,8},{28,12},{1,17},{... | collective-permute-start | bytes 3145736 | tf_op jit(solution)/shard_map/ppermute | solution.py:195
  183.2 40.3 %collective-permute-start.5 = (bf16[512,2048]{1,0:T(8,128)(2,1)S(1)}, bf16[512,2048]{1,0:T(8,128)(2,1)S(1)}, u32[]{:S(2)}, u32[]{:S(2)}) collective-permute-start(bf16[512,2048]{1,0:T(8,128)(2,1)S(1)} %bitcast.208), channel_id=1, source_target_pairs={{0,4},{4,0},{8,12},{12,8},{16,20},{20,16},{24,28},{28,24},{1,5},{5... | collective-permute-start | bytes 6291464 | tf_op jit(solution)/shard_map/ppermute | solution.py:195
  183.3 26.6 %collective-permute-start.22 = (bf16[1,2,128,2048]{3,2,1,0:T(8,128)(2,1)S(1)}, bf16[1,2,128,2048]{3,2,1,0:T(8,128)(2,1)S(1)}, u32[]{:S(2)}, u32[]{:S(2)}) collective-permute-start(bf16[1,2,128,2048]{3,2,1,0:T(8,128)(2,1)S(1)} %pad_maximum_fusion.13), channel_id=1, source_target_pairs={{0,16},{4,20},{8,24},{12,28},{16,0},{20,4},{24,8},{28,12},{1,17},{... | collective-permute-start | bytes 3145736 | tf_op jit(solution)/shard_map/ppermute | solution.py:195
  184.1 41.5 %collective-permute-start.11 = (bf16[512,2048]{1,0:T(8,128)(2,1)S(1)}, bf16[512,2048]{1,0:T(8,128)(2,1)S(1)}, u32[]{:S(2)}, u32[]{:S(2)}) collective-permute-start(bf16[512,2048]{1,0:T(8,128)(2,1)S(1)} %bitcast.204), channel_id=1, source_target_pairs={{0,4},{4,0},{8,12},{12,8},{16,20},{20,16},{24,28},{28,24},{1,5},{5... | collective-permute-start | bytes 6291464 | tf_op jit(solution)/shard_map/ppermute | solution.py:195
  188.4 33.5 %collective-permute-start.33 = (bf16[2,1,128,2048]{3,2,1,0:T(8,128)(2,1)S(1)}, bf16[2,1,128,2048]{3,2,1,0:T(8,128)(2,1)S(1)}, u32[]{:S(2)}, u32[]{:S(2)}) collective-permute-start(bf16[2,1,128,2048]{3,2,1,0:T(8,128)(2,1)S(1)} %pad_maximum_fusion.15), channel_id=1, source_target_pairs={{0,8},{4,12},{8,0},{12,4},{16,24},{20,28},{24,16},{28,20},{1,9},{5... | collective-permute-start | bytes 3145736 | tf_op jit(solution)/shard_map/ppermute | solution.py:195
  205.6 65.1 %collective-permute-start.17 = (bf16[512,2048]{1,0:T(8,128)(2,1)}, bf16[512,2048]{1,0:T(8,128)(2,1)}, u32[]{:S(2)}, u32[]{:S(2)}) collective-permute-start(bf16[512,2048]{1,0:T(8,128)(2,1)} %bitcast.33), channel_id=1, source_target_pairs={{0,4},{4,0},{8,12},{12,8},{16,20},{20,16},{24,28},{28,24},{1,5},{5... | collective-permute-start | bytes 6291464 | tf_op jit(solution)/shard_map/ppermute | solution.py:195
  209.9 35.7 %collective-permute-start.28 = (bf16[512,2048]{1,0:T(8,128)(2,1)}, bf16[512,2048]{1,0:T(8,128)(2,1)}, u32[]{:S(2)}, u32[]{:S(2)}) collective-permute-start(bf16[512,2048]{1,0:T(8,128)(2,1)} %bitcast.38), channel_id=1, source_target_pairs={{0,4},{4,0},{8,12},{12,8},{16,20},{20,16},{24,28},{28,24},{1,5},{5... | collective-permute-start | bytes 6291464 | tf_op jit(solution)/shard_map/ppermute | solution.py:195
  221.8 55.3 %collective-permute-start.34 = (bf16[512,2048]{1,0:T(8,128)(2,1)}, bf16[512,2048]{1,0:T(8,128)(2,1)}, u32[]{:S(2)}, u32[]{:S(2)}) collective-permute-start(bf16[512,2048]{1,0:T(8,128)(2,1)} %bitcast.36), channel_id=1, source_target_pairs={{0,4},{4,0},{8,12},{12,8},{16,20},{20,16},{24,28},{28,24},{1,5},{5... | collective-permute-start | bytes 6291464 | tf_op jit(solution)/shard_map/ppermute | solution.py:195
  223.4 44.9 %collective-permute-start.35 = (bf16[512,2048]{1,0:T(8,128)(2,1)}, bf16[512,2048]{1,0:T(8,128)(2,1)}, u32[]{:S(2)}, u32[]{:S(2)}) collective-permute-start(bf16[512,2048]{1,0:T(8,128)(2,1)} %bitcast.40), channel_id=1, source_target_pairs={{0,4},{4,0},{8,12},{12,8},{16,20},{20,16},{24,28},{28,24},{1,5},{5... | collective-permute-start | bytes 6291464 | tf_op jit(solution)/shard_map/ppermute | solution.py:195
  362.5 178.8 %collective-permute-start.72 = (bf16[512,2048]{1,0:T(8,128)(2,1)}, bf16[512,2048]{1,0:T(8,128)(2,1)}, u32[]{:S(2)}, u32[]{:S(2)}) collective-permute-start(bf16[512,2048]{1,0:T(8,128)(2,1)} %convolution_convert_fusion), channel_id=1, source_target_pairs={{0,4},{4,0},{8,12},{12,8},{16,20},{20,16},{24,28},{28,24},{1,5},{5... | collective-permute-start | bytes 6291464 | tf_op jit(solution)/shard_map/ppermute | solution.py:195
  362.8 186.8 %collective-permute-start.66 = (bf16[512,2048]{1,0:T(8,128)(2,1)}, bf16[512,2048]{1,0:T(8,128)(2,1)}, u32[]{:S(2)}, u32[]{:S(2)}) collective-permute-start(bf16[512,2048]{1,0:T(8,128)(2,1)} %convolution_convert_fusion.2), channel_id=1, source_target_pairs={{0,4},{4,0},{8,12},{12,8},{16,20},{20,16},{24,28},{28,24},{1,5},{5... | collective-permute-start | bytes 6291464 | tf_op jit(solution)/shard_map/ppermute | solution.py:195
  363.0 195.3 %collective-permute-start.60 = (bf16[512,2048]{1,0:T(8,128)(2,1)}, bf16[512,2048]{1,0:T(8,128)(2,1)}, u32[]{:S(2)}, u32[]{:S(2)}) collective-permute-start(bf16[512,2048]{1,0:T(8,128)(2,1)} %convolution_convert_fusion.4), channel_id=1, source_target_pairs={{0,4},{4,0},{8,12},{12,8},{16,20},{20,16},{24,28},{28,24},{1,5},{5... | collective-permute-start | bytes 6291464 | tf_op jit(solution)/shard_map/ppermute | solution.py:195
  401.5 15.5 %collective-permute-start.36 = (bf16[256,1024]{1,0:T(8,128)(2,1)}, bf16[256,1024]{1,0:T(8,128)(2,1)}, u32[]{:S(2)}, u32[]{:S(2)}) collective-permute-start(bf16[256,1024]{1,0:T(8,128)(2,1)} %reshape.597), channel_id=1, source_target_pairs={{0,1},{1,2},{2,3},{3,0},{4,5},{5,6},{6,7},{7,4},{8,9},{9,10},{10,1... | collective-permute-start | bytes 1572872 | tf_op jit(solution)/shard_map/ppermute | solution.py:199
  401.5 26.7 %collective-permute-start.39 = (bf16[256,1024]{1,0:T(8,128)(2,1)S(1)}, bf16[256,1024]{1,0:T(8,128)(2,1)}, u32[]{:S(2)}, u32[]{:S(2)}) collective-permute-start(bf16[256,1024]{1,0:T(8,128)(2,1)S(1)} %reshape.607), channel_id=1, source_target_pairs={{0,1},{1,2},{2,3},{3,0},{4,5},{5,6},{6,7},{7,4},{8,9},{9,10},{10,1... | collective-permute-start | bytes 1572872 | tf_op jit(solution)/shard_map/ppermute | solution.py:199
  417.0 57.8 %collective-permute-start.37 = (bf16[256,1024]{1,0:T(8,128)(2,1)}, bf16[256,1024]{1,0:T(8,128)(2,1)}, u32[]{:S(2)}, u32[]{:S(2)}) collective-permute-start(bf16[256,1024]{1,0:T(8,128)(2,1)} %collective-permute-done.36), channel_id=1, source_target_pairs={{0,1},{1,2},{2,3},{3,0},{4,5},{5,6},{6,7},{7,4},{8,9},{9,10},{10,1... | collective-permute-start | bytes 1572872 | tf_op jit(solution)/shard_map/ppermute | solution.py:199
  428.3 46.6 %collective-permute-start.40 = (bf16[256,1024]{1,0:T(8,128)(2,1)}, bf16[256,1024]{1,0:T(8,128)(2,1)}, u32[]{:S(2)}, u32[]{:S(2)}) collective-permute-start(bf16[256,1024]{1,0:T(8,128)(2,1)} %collective-permute-done.39), channel_id=1, source_target_pairs={{0,1},{1,2},{2,3},{3,0},{4,5},{5,6},{6,7},{7,4},{8,9},{9,10},{10,1... | collective-permute-start | bytes 1572872 | tf_op jit(solution)/shard_map/ppermute | solution.py:199
  474.8 46.2 %collective-permute-start.38 = (bf16[256,1024]{1,0:T(8,128)(2,1)}, bf16[256,1024]{1,0:T(8,128)(2,1)}, u32[]{:S(2)}, u32[]{:S(2)}) collective-permute-start(bf16[256,1024]{1,0:T(8,128)(2,1)} %collective-permute-done.37), channel_id=1, source_target_pairs={{0,1},{1,2},{2,3},{3,0},{4,5},{5,6},{6,7},{7,4},{8,9},{9,10},{10,1... | collective-permute-start | bytes 1572872 | tf_op jit(solution)/shard_map/ppermute | solution.py:199
  474.8 26.2 %collective-permute-start.41 = (bf16[256,1024]{1,0:T(8,128)(2,1)}, bf16[256,1024]{1,0:T(8,128)(2,1)}, u32[]{:S(2)}, u32[]{:S(2)}) collective-permute-start(bf16[256,1024]{1,0:T(8,128)(2,1)} %collective-permute-done.40), channel_id=1, source_target_pairs={{0,1},{1,2},{2,3},{3,0},{4,5},{5,6},{6,7},{7,4},{8,9},{9,10},{10,1... | collective-permute-start | bytes 1572872 | tf_op jit(solution)/shard_map/ppermute | solution.py:199
  501.1 62.7 %collective-permute-start.54 = (bf16[512,2048]{1,0:T(8,128)(2,1)}, bf16[512,2048]{1,0:T(8,128)(2,1)}, u32[]{:S(2)}, u32[]{:S(2)}) collective-permute-start(bf16[512,2048]{1,0:T(8,128)(2,1)} %convolution_convert_fusion.6), channel_id=1, source_target_pairs={{0,4},{4,0},{8,12},{12,8},{16,20},{20,16},{24,28},{28,24},{1,5},{5... | collective-permute-start | bytes 6291464 | tf_op jit(solution)/shard_map/ppermute | solution.py:195
  521.0 47.0 %collective-permute-start.48 = (bf16[512,2048]{1,0:T(8,128)(2,1)}, bf16[512,2048]{1,0:T(8,128)(2,1)}, u32[]{:S(2)}, u32[]{:S(2)}) collective-permute-start(bf16[512,2048]{1,0:T(8,128)(2,1)} %pad_maximum_fusion.8), channel_id=1, source_target_pairs={{0,4},{4,0},{8,12},{12,8},{16,20},{20,16},{24,28},{28,24},{1,5},{5... | collective-permute-start | bytes 6291464 | tf_op jit(solution)/shard_map/ppermute | solution.py:195
  541.2 35.7 %collective-permute-start.42 = (bf16[512,2048]{1,0:T(8,128)(2,1)}, bf16[512,2048]{1,0:T(8,128)(2,1)}, u32[]{:S(2)}, u32[]{:S(2)}) collective-permute-start(bf16[512,2048]{1,0:T(8,128)(2,1)} %convolution_convert_fusion.8), channel_id=1, source_target_pairs={{0,4},{4,0},{8,12},{12,8},{16,20},{20,16},{24,28},{28,24},{1,5},{5... | collective-permute-start | bytes 6291464 | tf_op jit(solution)/shard_map/ppermute | solution.py:195
  549.6 31.4 %collective-permute-start.73 = (bf16[2,1,128,2048]{2,3,1,0:T(8,128)(2,1)}, bf16[2,1,128,2048]{2,3,1,0:T(8,128)(2,1)}, u32[]{:S(2)}, u32[]{:S(2)}) collective-permute-start(bf16[2,1,128,2048]{2,3,1,0:T(8,128)(2,1)} %copy.126), channel_id=1, source_target_pairs={{0,8},{4,12},{8,0},{12,4},{16,24},{20,28},{24,16},{28,20},{1,9},{5... | collective-permute-start | bytes 3145736 | tf_op jit(solution)/shard_map/ppermute | solution.py:195
  558.3 26.3 %collective-permute-start.67 = (bf16[1,2,128,2048]{2,3,1,0:T(8,128)(2,1)}, bf16[1,2,128,2048]{2,3,1,0:T(8,128)(2,1)}, u32[]{:S(2)}, u32[]{:S(2)}) collective-permute-start(bf16[1,2,128,2048]{2,3,1,0:T(8,128)(2,1)} %copy.114), channel_id=1, source_target_pairs={{0,16},{4,20},{8,24},{12,28},{16,0},{20,4},{24,8},{28,12},{1,17},{... | collective-permute-start | bytes 3145736 | tf_op jit(solution)/shard_map/ppermute | solution.py:195
  563.7 34.6 %collective-permute-start.61 = (bf16[2,1,128,2048]{3,2,1,0:T(8,128)(2,1)}, bf16[2,1,128,2048]{3,2,1,0:T(8,128)(2,1)}, u32[]{:S(2)}, u32[]{:S(2)}) collective-permute-start(bf16[2,1,128,2048]{3,2,1,0:T(8,128)(2,1)} %slice.494), channel_id=1, source_target_pairs={{0,8},{4,12},{8,0},{12,4},{16,24},{20,28},{24,16},{28,20},{1,9},{5... | collective-permute-start | bytes 3145736 | tf_op jit(solution)/shard_map/ppermute | solution.py:195
  568.0 39.1 %collective-permute-start.55 = (bf16[1,2,128,2048]{3,2,1,0:T(8,128)(2,1)}, bf16[1,2,128,2048]{3,2,1,0:T(8,128)(2,1)}, u32[]{:S(2)}, u32[]{:S(2)}) collective-permute-start(bf16[1,2,128,2048]{3,2,1,0:T(8,128)(2,1)} %bitcast.79), channel_id=1, source_target_pairs={{0,16},{4,20},{8,24},{12,28},{16,0},{20,4},{24,8},{28,12},{1,17},{... | collective-permute-start | bytes 3145736 | tf_op jit(solution)/shard_map/ppermute | solution.py:195
  576.9 43.8 %collective-permute-start.49 = (bf16[2,1,128,2048]{2,3,1,0:T(8,128)(2,1)}, bf16[2,1,128,2048]{2,3,1,0:T(8,128)(2,1)S(1)}, u32[]{:S(2)}, u32[]{:S(2)}) collective-permute-start(bf16[2,1,128,2048]{2,3,1,0:T(8,128)(2,1)} %copy.124), channel_id=1, source_target_pairs={{0,8},{4,12},{8,0},{12,4},{16,24},{20,28},{24,16},{28,20},{1,9},{5... | collective-permute-start | bytes 3145736 | tf_op jit(solution)/shard_map/ppermute | solution.py:195
  581.0 48.5 %collective-permute-start.43 = (bf16[1,2,128,2048]{3,2,1,0:T(8,128)(2,1)S(1)}, bf16[1,2,128,2048]{3,2,1,0:T(8,128)(2,1)S(1)}, u32[]{:S(2)}, u32[]{:S(2)}) collective-permute-start(bf16[1,2,128,2048]{3,2,1,0:T(8,128)(2,1)S(1)} %bitcast.262), channel_id=1, source_target_pairs={{0,16},{4,20},{8,24},{12,28},{16,0},{20,4},{24,8},{28,12},{1,17},{... | collective-permute-start | bytes 3145736 | tf_op jit(solution)/shard_map/ppermute | solution.py:195
  584.6 56.1 %collective-permute-start.74 = (bf16[1,1,128,2048]{2,3,1,0:T(8,128)(2,1)S(1)}, bf16[1,1,128,2048]{2,3,1,0:T(8,128)(2,1)S(1)}, u32[]{:S(2)}, u32[]{:S(2)}) collective-permute-start(bf16[1,1,128,2048]{2,3,1,0:T(8,128)(2,1)S(1)} %slice.512), channel_id=1, source_target_pairs={{0,16},{4,20},{8,24},{12,28},{16,0},{20,4},{24,8},{28,12},{1,17},{... | collective-permute-start | bytes 1572872 | tf_op jit(solution)/shard_map/ppermute | solution.py:195
  598.3 43.3 %collective-permute-start.68 = (bf16[1,1,128,2048]{2,3,1,0:T(8,128)(2,1)S(1)}, bf16[1,1,128,2048]{2,3,1,0:T(8,128)(2,1)S(1)}, u32[]{:S(2)}, u32[]{:S(2)}) collective-permute-start(bf16[1,1,128,2048]{2,3,1,0:T(8,128)(2,1)S(1)} %slice.504), channel_id=1, source_target_pairs={{0,8},{4,12},{8,0},{12,4},{16,24},{20,28},{24,16},{28,20},{1,9},{5... | collective-permute-start | bytes 1572872 | tf_op jit(solution)/shard_map/ppermute | solution.py:195
  607.1 44.8 %collective-permute-start.62 = (bf16[1,1,128,2048]{3,2,1,0:T(8,128)(2,1)S(1)}, bf16[1,1,128,2048]{3,2,1,0:T(8,128)(2,1)S(1)}, u32[]{:S(2)}, u32[]{:S(2)}) collective-permute-start(bf16[1,1,128,2048]{3,2,1,0:T(8,128)(2,1)S(1)} %slice.496), channel_id=1, source_target_pairs={{0,16},{4,20},{8,24},{12,28},{16,0},{20,4},{24,8},{28,12},{1,17},{... | collective-permute-start | bytes 1572872 | tf_op jit(solution)/shard_map/ppermute | solution.py:195
  620.7 31.9 %collective-permute-start.56 = (bf16[1,1,128,2048]{3,2,1,0:T(8,128)(2,1)S(1)}, bf16[1,1,128,2048]{3,2,1,0:T(8,128)(2,1)S(1)}, u32[]{:S(2)}, u32[]{:S(2)}) collective-permute-start(bf16[1,1,128,2048]{3,2,1,0:T(8,128)(2,1)S(1)} %slice.488), channel_id=1, source_target_pairs={{0,8},{4,12},{8,0},{12,4},{16,24},{20,28},{24,16},{28,20},{1,9},{5... | collective-permute-start | bytes 1572872 | tf_op jit(solution)/shard_map/ppermute | solution.py:195
  629.5 33.0 %collective-permute-start.50 = (bf16[1,1,128,2048]{2,3,1,0:T(8,128)(2,1)S(1)}, bf16[1,1,128,2048]{2,3,1,0:T(8,128)(2,1)S(1)}, u32[]{:S(2)}, u32[]{:S(2)}) collective-permute-start(bf16[1,1,128,2048]{2,3,1,0:T(8,128)(2,1)S(1)} %slice.474), channel_id=1, source_target_pairs={{0,16},{4,20},{8,24},{12,28},{16,0},{20,4},{24,8},{28,12},{1,17},{... | collective-permute-start | bytes 1572872 | tf_op jit(solution)/shard_map/ppermute | solution.py:195
  640.7 22.5 %collective-permute-start.44 = (bf16[1,1,128,2048]{3,2,1,0:T(8,128)(2,1)S(1)}, bf16[1,1,128,2048]{3,2,1,0:T(8,128)(2,1)S(1)}, u32[]{:S(2)}, u32[]{:S(2)}) collective-permute-start(bf16[1,1,128,2048]{3,2,1,0:T(8,128)(2,1)S(1)} %slice.460), channel_id=1, source_target_pairs={{0,8},{4,12},{8,0},{12,4},{16,24},{20,28},{24,16},{28,20},{1,9},{5... | collective-permute-start | bytes 1572872 | tf_op jit(solution)/shard_map/ppermute | solution.py:195
  641.7 22.6 %collective-permute-start.75 = (bf16[128,512]{0,1:T(8,128)(2,1)S(1)}, bf16[128,512]{0,1:T(8,128)(2,1)S(1)}, u32[]{:S(2)}, u32[]{:S(2)}) collective-permute-start(bf16[128,512]{0,1:T(8,128)(2,1)S(1)} %slice.516), channel_id=1, source_target_pairs={{0,3},{1,0},{2,1},{3,2},{4,7},{5,4},{6,5},{7,6},{8,11},{9,8},{10,9... | collective-permute-start | bytes 393224 | tf_op jit(solution)/shard_map/ppermute | solution.py:199
  652.6 15.7 %collective-permute-start.63 = (bf16[128,512]{1,0:T(8,128)(2,1)S(1)}, bf16[128,512]{1,0:T(8,128)(2,1)S(1)}, u32[]{:S(2)}, u32[]{:S(2)}) collective-permute-start(bf16[128,512]{1,0:T(8,128)(2,1)S(1)} %slice.500), channel_id=1, source_target_pairs={{0,3},{1,0},{2,1},{3,2},{4,7},{5,4},{6,5},{7,6},{8,11},{9,8},{10,9... | collective-permute-start | bytes 393224 | tf_op jit(solution)/shard_map/ppermute | solution.py:199
  669.0 14.0 %collective-permute-start.64 = (bf16[128,512]{1,0:T(8,128)(2,1)S(1)}, bf16[128,512]{1,0:T(8,128)(2,1)S(1)}, u32[]{:S(2)}, u32[]{:S(2)}) collective-permute-start(bf16[128,512]{1,0:T(8,128)(2,1)S(1)} %add_convert_fusion.25), channel_id=1, source_target_pairs={{0,3},{1,0},{2,1},{3,2},{4,7},{5,4},{6,5},{7,6},{8,11},{9,8},{10,9... | collective-permute-start | bytes 393224 | tf_op jit(solution)/shard_map/ppermute | solution.py:199
  671.7 14.0 %collective-permute-start.58 = (bf16[128,512]{1,0:T(8,128)(2,1)S(1)}, bf16[128,512]{1,0:T(8,128)(2,1)S(1)}, u32[]{:S(2)}, u32[]{:S(2)}) collective-permute-start(bf16[128,512]{1,0:T(8,128)(2,1)S(1)} %add_convert_fusion.28), channel_id=1, source_target_pairs={{0,3},{1,0},{2,1},{3,2},{4,7},{5,4},{6,5},{7,6},{8,11},{9,8},{10,9... | collective-permute-start | bytes 393224 | tf_op jit(solution)/shard_map/ppermute | solution.py:199
  674.5 14.0 %collective-permute-start.52 = (bf16[128,512]{0,1:T(8,128)(2,1)S(1)}, bf16[128,512]{0,1:T(8,128)(2,1)S(1)}, u32[]{:S(2)}, u32[]{:S(2)}) collective-permute-start(bf16[128,512]{0,1:T(8,128)(2,1)S(1)} %add_convert_fusion.31), channel_id=1, source_target_pairs={{0,3},{1,0},{2,1},{3,2},{4,7},{5,4},{6,5},{7,6},{8,11},{9,8},{10,9... | collective-permute-start | bytes 393224 | tf_op jit(solution)/shard_map/ppermute | solution.py:199
  677.3 14.0 %collective-permute-start.46 = (bf16[128,512]{1,0:T(8,128)(2,1)S(1)}, bf16[128,512]{1,0:T(8,128)(2,1)S(1)}, u32[]{:S(2)}, u32[]{:S(2)}) collective-permute-start(bf16[128,512]{1,0:T(8,128)(2,1)S(1)} %add_convert_fusion.34), channel_id=1, source_target_pairs={{0,3},{1,0},{2,1},{3,2},{4,7},{5,4},{6,5},{7,6},{8,11},{9,8},{10,9... | collective-permute-start | bytes 393224 | tf_op jit(solution)/shard_map/ppermute | solution.py:199
  680.1 14.0 %collective-permute-start.77 = (bf16[128,512]{0,1:T(8,128)(2,1)S(1)}, bf16[128,512]{0,1:T(8,128)(2,1)S(1)}, u32[]{:S(2)}, u32[]{:S(2)}) collective-permute-start(bf16[128,512]{0,1:T(8,128)(2,1)S(1)} %add_convert_fusion.18), channel_id=1, source_target_pairs={{0,3},{1,0},{2,1},{3,2},{4,7},{5,4},{6,5},{7,6},{8,11},{9,8},{10,9... | collective-permute-start | bytes 393224 | tf_op jit(solution)/shard_map/ppermute | solution.py:199
  682.9 14.0 %collective-permute-start.71 = (bf16[128,512]{0,1:T(8,128)(2,1)S(1)}, bf16[128,512]{0,1:T(8,128)(2,1)S(1)}, u32[]{:S(2)}, u32[]{:S(2)}) collective-permute-start(bf16[128,512]{0,1:T(8,128)(2,1)S(1)} %add_convert_fusion.21), channel_id=1, source_target_pairs={{0,3},{1,0},{2,1},{3,2},{4,7},{5,4},{6,5},{7,6},{8,11},{9,8},{10,9... | collective-permute-start | bytes 393224 | tf_op jit(solution)/shard_map/ppermute | solution.py:199
  685.7 14.0 %collective-permute-start.65 = (bf16[128,512]{1,0:T(8,128)(2,1)S(1)}, bf16[128,512]{1,0:T(8,128)(2,1)S(1)}, u32[]{:S(2)}, u32[]{:S(2)}) collective-permute-start(bf16[128,512]{1,0:T(8,128)(2,1)S(1)} %add_convert_fusion.24), channel_id=1, source_target_pairs={{0,3},{1,0},{2,1},{3,2},{4,7},{5,4},{6,5},{7,6},{8,11},{9,8},{10,9... | collective-permute-start | bytes 393224 | tf_op jit(solution)/shard_map/ppermute | solution.py:199
  688.5 20.4 %collective-permute-start.59 = (bf16[128,512]{1,0:T(8,128)(2,1)S(1)}, bf16[128,512]{1,0:T(8,128)(2,1)S(1)}, u32[]{:S(2)}, u32[]{:S(2)}) collective-permute-start(bf16[128,512]{1,0:T(8,128)(2,1)S(1)} %add_convert_fusion.27), channel_id=1, source_target_pairs={{0,3},{1,0},{2,1},{3,2},{4,7},{5,4},{6,5},{7,6},{8,11},{9,8},{10,9... | collective-permute-start | bytes 393224 | tf_op jit(solution)/shard_map/ppermute | solution.py:199
  691.3 13.8 %collective-permute-start.53 = (bf16[128,512]{0,1:T(8,128)(2,1)S(1)}, bf16[128,512]{0,1:T(8,128)(2,1)S(1)}, u32[]{:S(2)}, u32[]{:S(2)}) collective-permute-start(bf16[128,512]{0,1:T(8,128)(2,1)S(1)} %add_convert_fusion.30), channel_id=1, source_target_pairs={{0,3},{1,0},{2,1},{3,2},{4,7},{5,4},{6,5},{7,6},{8,11},{9,8},{10,9... | collective-permute-start | bytes 393224 | tf_op jit(solution)/shard_map/ppermute | solution.py:199
  (106 other events, 995.7 us)

commit v2 on v1

v2 whole, which is shorter than its diff:
```python
import functools

import jax
import jax.numpy as jnp
from jax import lax
from jax.experimental import pallas as pl
from jax.experimental.pallas import tpu as pltpu
from jax.sharding import PartitionSpec as P

HEAD_DIM = 64
SLOT_BLOCK = 512
EPSILON = 1e-06


CURVE = 0.7978845608028654
CUBIC = 0.044715


def gelu_tanh(values):
    return 0.5 * values * (1.0 + jnp.tanh(CURVE * (values + CUBIC * values * values * values)))


def gelu_slope(values):
    square = values * values
    bend = jnp.tanh(CURVE * (values + CUBIC * values * square))
    inner = CURVE * (1.0 + 3.0 * CUBIC * square)
    return 0.5 * (1.0 + bend) + 0.5 * values * (1.0 - bend * bend) * inner


def product(left, right):
    return jnp.dot(left, right, preferred_element_type=jnp.float32)


def contract_rows(left, right):
    return lax.dot_general(
        left, right, (((0,), (0,)), ((), ())), preferred_element_type=jnp.float32
    )


def times_transposed(left, right):
    return lax.dot_general(
        left, right, (((1,), (1,)), ((), ())), preferred_element_type=jnp.float32
    )


def norm_backward(d_normed_in, normed, inverse, gain_vec):
    d_scaled = d_normed_in * gain_vec
    d_input = inverse * (d_scaled - normed * jnp.mean(d_scaled * normed, axis=-1, keepdims=True))
    return (d_input, jnp.sum(d_normed_in * normed, axis=0, keepdims=True))


def norm_forward(values):
    inverse = lax.rsqrt(jnp.mean(values * values, axis=-1, keepdims=True) + EPSILON)
    return (values * inverse, inverse)


LOW = jnp.bfloat16
FULL = jnp.float32


def pick_kernel(order_ref, routes_ref, turn_ref, tokens_ref, cot_ref, routed_ref, cot_routed_ref, total, cot_total):
    block = pl.program_id(1)
    capacity = routes_ref.shape[1]
    slots = tokens_ref.shape[1]
    column = lax.broadcasted_iota(jnp.int32, (capacity, slots), 1) + block * slots
    chooser = (routes_ref[0] == column).astype(LOW)
    part = product(chooser, tokens_ref[0])
    cot_part = product(chooser, cot_ref[0])

    @pl.when(block == 0)
    def _():
        total[...] = part
        cot_total[...] = cot_part

    @pl.when(block > 0)
    def _():
        total[...] += part
        cot_total[...] += cot_part

    @pl.when(block == pl.num_programs(1) - 1)
    def _():
        routed_ref[0] = product(total[...].astype(LOW), turn_ref[...]).astype(LOW)
        cot_routed_ref[0] = product(cot_total[...].astype(LOW), turn_ref[...]).astype(LOW)


def pick_rows(tokens, cotangent, routes, order, count, turn):
    seq_count, slots, features = tokens.shape
    capacity = routes.shape[1]
    per_block = min(SLOT_BLOCK, slots)
    table = pl.BlockSpec((1, per_block, features), lambda i, j, order: (order[i], j, 0))
    picked = pl.BlockSpec((1, capacity, features), lambda i, j, order: (i, 0, 0))
    shape = jax.ShapeDtypeStruct((count, capacity, features), LOW)
    return pl.pallas_call(
        pick_kernel,
        out_shape=(shape, shape),
        grid_spec=pltpu.PrefetchScalarGridSpec(
            num_scalar_prefetch=1,
            grid=(count, slots // per_block),
            in_specs=[
                pl.BlockSpec((1, capacity, 1), lambda i, j, order: (order[i], 0, 0)),
                pl.BlockSpec((features, features), lambda i, j, order: (0, 0)),
                table,
                table,
            ],
            out_specs=[picked, picked],
            scratch_shapes=[pltpu.VMEM((capacity, features), FULL)] * 2,
        ),
        compiler_params=pltpu.CompilerParams(vmem_limit_bytes=48 << 20),
        cost_estimate=pl.CostEstimate(
            flops=4 * count * capacity * slots * features,
            bytes_accessed=4 * count * slots * features,
            transcendentals=0,
        ),
        name="pick_rows",
    )(order, routes[:, :, None], turn, tokens, cotangent)


def place_kernel(order_ref, routes_ref, table_ref, values_ref, out_ref):
    block = pl.program_id(1)
    slots = table_ref.shape[1]
    capacity = routes_ref.shape[2]
    row = lax.broadcasted_iota(jnp.int32, (slots, capacity), 0) + block * slots
    chooser = (routes_ref[0] == row).astype(LOW)
    placed = product(chooser, values_ref[0])
    out_ref[0] = (table_ref[0].astype(FULL) + placed).astype(LOW)


def place_rows(table, values, routes, order):
    seq_count, slots, features = table.shape
    capacity = routes.shape[1]
    per_block = min(SLOT_BLOCK, slots)
    tall = pl.BlockSpec((1, per_block, features), lambda i, j, order: (order[i], j, 0))
    return pl.pallas_call(
        place_kernel,
        out_shape=jax.ShapeDtypeStruct(table.shape, table.dtype),
        grid_spec=pltpu.PrefetchScalarGridSpec(
            num_scalar_prefetch=1,
            grid=(seq_count, slots // per_block),
            in_specs=[
                pl.BlockSpec((1, 1, capacity), lambda i, j, order: (order[i], 0, 0)),
                tall,
                pl.BlockSpec((1, capacity, features), lambda i, j, order: (i, 0, 0)),
            ],
            out_specs=tall,
        ),
        compiler_params=pltpu.CompilerParams(vmem_limit_bytes=48 << 20),
        cost_estimate=pl.CostEstimate(
            flops=2 * seq_count * capacity * slots * features,
            bytes_accessed=4 * seq_count * slots * features,
            transcendentals=0,
        ),
        name="place_rows",
    )(order, routes[:, None, :], table, values)


def gates(routed, router_vec, live_ref, capacity):
    rows = routed.shape[0]
    score = jnp.sum(routed * router_vec, axis=-1, keepdims=True)
    gate_prob = 1.0 / (1.0 + jnp.exp(-score))
    live = [
        lax.broadcasted_iota(jnp.int32, (capacity, 1), 0) < live_ref[seq]
        for seq in range(rows // capacity)
    ]
    live = live[0] if len(live) == 1 else jnp.concatenate(live, axis=0)
    return gate_prob, jnp.where(live, gate_prob, 0.0)


def probabilities(queries, keys_all, live_count, scale_qk):
    scores = times_transposed(queries, keys_all) * scale_qk
    row = lax.broadcasted_iota(jnp.int32, scores.shape, 0)
    column = lax.broadcasted_iota(jnp.int32, scores.shape, 1)
    masked = jnp.where((column <= row) & (column < live_count), scores, -1e30)
    exp_scores = jnp.exp(masked - jnp.max(masked, axis=-1, keepdims=True))
    return exp_scores / jnp.sum(exp_scores, axis=-1, keepdims=True)


def split_heads(pair):
    owner = lax.broadcasted_iota(jnp.int32, pair.shape, 1) // HEAD_DIM
    return [jnp.where(owner == i, pair, jnp.zeros_like(pair)) for i in range(pair.shape[1] // HEAD_DIM)]


def attend_kernel(
    capacity, live_ref, routed_ref, cot_ref, small_ref, qk_own, qk_other, vo_own, vo_other,
    attn_in_ref, qkv_ref, heads_ref, attn_out_ref, mlp_in_ref, d_mlp_out_ref,
):
    routed = routed_ref[...].astype(FULL)
    rows, features = routed.shape
    half = features // 2
    wide = qkv_ref.shape[1] // 3
    _, gate_live = gates(routed, small_ref[2:3], live_ref, capacity)
    d_mlp_out_ref[...] = (gate_live * cot_ref[...].astype(FULL)).astype(LOW)
    normed, _ = norm_forward(routed)
    attn_in = (normed * small_ref[0:1]).astype(LOW)
    attn_in_ref[...] = attn_in
    left, right = attn_in[:, :half], attn_in[:, half:]
    qkv_ref[:, : 2 * wide] = (product(left, qk_own[...]) + product(right, qk_other[...])).astype(LOW)
    qkv_ref[:, 2 * wide :] = (
        product(left, vo_own[:, :wide]) + product(right, vo_other[:, :wide])
    ).astype(LOW)
    tile = 2 * HEAD_DIM
    for seq in range(rows // capacity):
        at = slice(seq * capacity, (seq + 1) * capacity)
        for start in range(0, wide, tile):
            keys_all = qkv_ref[at, wide + start : wide + start + tile]
            queries = split_heads(qkv_ref[at, start : start + tile])
            vals = split_heads(qkv_ref[at, 2 * wide + start : 2 * wide + start + tile])
            total = None
            for query, val in zip(queries, vals):
                probs = probabilities(query, keys_all, live_ref[seq], HEAD_DIM ** (-0.5))
                part = product(probs.astype(LOW), val)
                total = part if total is None else total + part
            heads_ref[at, start : start + tile] = total.astype(LOW)
    heads_out = heads_ref[...]
    attn_out_ref[:, :half] = times_transposed(heads_out, vo_own[:, wide:])
    attn_out_ref[:, half:] = times_transposed(heads_out, vo_other[:, wide:])
    normed_two, _ = norm_forward(routed + attn_out_ref[...])
    mlp_in_ref[...] = (normed_two * small_ref[1:2]).astype(LOW)


def whole_specs(count):
    return [pl.BlockSpec(memory_space=pltpu.VMEM)] * count


def attend(live_count, routed, cot_routed, small, query_key, value_out, capacity):
    rows, features = routed.shape
    wide = query_key[0].shape[1] // 2
    return pl.pallas_call(
        functools.partial(attend_kernel, capacity),
        out_shape=(
            jax.ShapeDtypeStruct((rows, features), LOW),
            jax.ShapeDtypeStruct((rows, 3 * wide), LOW),
            jax.ShapeDtypeStruct((rows, wide), LOW),
            jax.ShapeDtypeStruct((rows, features), FULL),
            jax.ShapeDtypeStruct((rows, features), LOW),
            jax.ShapeDtypeStruct((rows, features), LOW),
        ),
        in_specs=[pl.BlockSpec(memory_space=pltpu.SMEM)] + whole_specs(7),
        out_specs=tuple(whole_specs(6)),
        compiler_params=pltpu.CompilerParams(vmem_limit_bytes=56 << 20),
        cost_estimate=pl.CostEstimate(
            flops=8 * rows * features * wide + 4 * rows * capacity * wide,
            bytes_accessed=8 * features * wide + 14 * rows * features,
            transcendentals=rows * capacity * wide // HEAD_DIM,
        ),
        name="attend",
    )(live_count, routed, cot_routed, small, *query_key, *value_out)


def up_kernel(mlp_in_ref, d_mlp_out_ref, *refs):
    weights, outs = refs[:4], refs[4:]
    mlp_in = mlp_in_ref[...]
    d_mlp_out = d_mlp_out_ref[...]
    half = mlp_in.shape[1] // 2
    for stream in range(2):
        own, other = weights[2 * stream : 2 * stream + 2]
        pre_ref, hidden_ref, kept_ref, sent_ref = outs[4 * stream : 4 * stream + 4]
        pre = product(mlp_in[:, :half], own[...]) + product(mlp_in[:, half:], other[...])
        hidden = gelu_tanh(pre).astype(LOW)
        pre_ref[...] = pre
        hidden_ref[...] = hidden
        sent_ref[...] = contract_rows(d_mlp_out[:, half:], hidden).astype(LOW)
        kept_ref[...] = contract_rows(d_mlp_out[:, :half], hidden).astype(LOW)


TILE = 512


def up_layer(mlp_in, d_mlp_out, ups):
    rows, features = mlp_in.shape
    half = features // 2
    width = ups[0][0].shape[1]
    tile = min(TILE, width)
    whole = pl.BlockSpec((rows, features), lambda i: (0, 0))
    weight = pl.BlockSpec((half, tile), lambda i: (0, i))
    tall = pl.BlockSpec((rows, tile), lambda i: (0, i))
    outs = [
        jax.ShapeDtypeStruct((rows, width), FULL),
        jax.ShapeDtypeStruct((rows, width), LOW),
        jax.ShapeDtypeStruct((half, width), LOW),
        jax.ShapeDtypeStruct((half, width), LOW),
    ]
    got = pl.pallas_call(
        up_kernel,
        grid=(width // tile,),
        out_shape=tuple(outs * 2),
        in_specs=[whole, whole] + [weight] * 4,
        out_specs=tuple([tall, tall, weight, weight] * 2),
        compiler_params=pltpu.CompilerParams(vmem_limit_bytes=56 << 20),
        cost_estimate=pl.CostEstimate(
            flops=8 * rows * features * width,
            bytes_accessed=8 * features * width + 12 * rows * width,
            transcendentals=2 * rows * width,
        ),
        name="up_layer",
    )(mlp_in, d_mlp_out, *ups[0], *ups[1])
    return got[:4], got[4:]


def down_kernel(
    capacity, live_ref, routed_ref, cot_ref, small_ref, turn_ref, attn_out_ref, mlp_in_ref, d_mlp_out_ref, *refs
):
    weights, middle, outs = refs[:8], refs[8:12], refs[12:]
    update_ref, d_mlp_in_ref, dot_ref = outs[:3]
    grads, mlp_out = outs[3:7], outs[7]
    mlp_in = mlp_in_ref[...]
    d_mlp_out = d_mlp_out_ref[...]
    half = mlp_in.shape[1] // 2

    @pl.when(pl.program_id(0) == 0)
    def _():
        mlp_out[...] = jnp.zeros_like(mlp_out)
        d_mlp_in_ref[...] = jnp.zeros_like(d_mlp_in_ref)

    for stream in range(2):
        up_own, up_other, down_own, down_other = weights[4 * stream : 4 * stream + 4]
        pre_ref, hidden_ref = middle[2 * stream : 2 * stream + 2]
        kept_ref, sent_ref = grads[2 * stream : 2 * stream + 2]
        d_hidden = product(d_mlp_out[:, :half], down_own[...]) + product(
            d_mlp_out[:, half:], down_other[...]
        )
        d_pre = (d_hidden * gelu_slope(pre_ref[...])).astype(LOW)
        sent_ref[...] = contract_rows(mlp_in[:, half:], d_pre).astype(LOW)
        kept_ref[...] = contract_rows(mlp_in[:, :half], d_pre).astype(LOW)
        d_mlp_in_ref[:, :half] += times_transposed(d_pre, up_own[...])
        d_mlp_in_ref[:, half:] += times_transposed(d_pre, up_other[...])
        hidden = hidden_ref[...]
        mlp_out[:, :half] += times_transposed(hidden, down_own[...])
        mlp_out[:, half:] += times_transposed(hidden, down_other[...])

    @pl.when(pl.program_id(0) == pl.num_programs(0) - 1)
    def _():
        _, gate_live = gates(routed_ref[...].astype(FULL), small_ref[2:3], live_ref, capacity)
        branch = attn_out_ref[...] + mlp_out[...]
        update = (gate_live * branch).astype(LOW)
        update_ref[...] = times_transposed(update, turn_ref[...]).astype(LOW)
        dot_ref[...] = jnp.sum(cot_ref[...].astype(FULL) * branch, axis=-1, keepdims=True)


def down_layer(live_count, routed, cot_routed, small, turn, attn_out, mlp_in, d_mlp_out, ups, downs, kept, capacity):
    rows, features = mlp_in.shape
    half = features // 2
    width = ups[0][0].shape[1]
    tile = min(TILE, width)
    whole = pl.BlockSpec((rows, features), lambda i: (0, 0))
    weight = pl.BlockSpec((half, tile), lambda i: (0, i))
    tall = pl.BlockSpec((rows, tile), lambda i: (0, i))
    outs = (
        jax.ShapeDtypeStruct((rows, features), LOW),
        jax.ShapeDtypeStruct((rows, features), FULL),
        jax.ShapeDtypeStruct((rows, 1), FULL),
    ) + (jax.ShapeDtypeStruct((half, width), LOW),) * 4
    got = pl.pallas_call(
        functools.partial(down_kernel, capacity),
        grid=(width // tile,),
        out_shape=outs,
        in_specs=[
            pl.BlockSpec(memory_space=pltpu.SMEM),
            whole,
            whole,
            pl.BlockSpec(small.shape, lambda i: (0, 0)),
            pl.BlockSpec(turn.shape, lambda i: (0, 0)),
            whole,
            whole,
            whole,
        ]
        + [weight] * 8
        + [tall] * 4,
        out_specs=(whole, whole, pl.BlockSpec((rows, 1), lambda i: (0, 0))) + (weight,) * 4,
        scratch_shapes=[pltpu.VMEM((rows, features), FULL)],
        compiler_params=pltpu.CompilerParams(vmem_limit_bytes=56 << 20),
        cost_estimate=pl.CostEstimate(
            flops=16 * rows * features * width,
            bytes_accessed=12 * features * width + 12 * rows * width,
            transcendentals=2 * rows * width,
        ),
        name="down_layer",
    )(
        live_count, routed, cot_routed, small, turn, attn_out, mlp_in, d_mlp_out,
        *ups[0], *downs[0], *ups[1], *downs[1],
        *[array for stream in kept for array in stream[:2]],
    )
    return got[0], got[1], got[2], got[3:5], got[5:7]


def attend_back_kernel(
    capacity, live_ref, routed_ref, cot_ref, small_ref, turn_ref, attn_out_ref, d_mlp_in_ref, dot_ref, qkv_ref,
    qk_own, qk_other, vo_own, vo_other, d_routed_ref, d_attn_out_ref, d_qkv_ref, small_grads_ref, d_heads_ref,
):
    routed = routed_ref[...].astype(FULL)
    rows, features = routed.shape
    half = features // 2
    wide = qkv_ref.shape[1] // 3
    scale_qk = HEAD_DIM ** (-0.5)
    gate_prob, gate_live = gates(routed, small_ref[2:3], live_ref, capacity)
    normed_two, inverse_two = norm_forward(routed + attn_out_ref[...])
    d_middle, small_grads_ref[1:2] = norm_backward(
        d_mlp_in_ref[...], normed_two, inverse_two, small_ref[1:2]
    )
    d_attn_out = (d_middle + gate_live * cot_ref[...].astype(FULL)).astype(LOW)
    d_attn_out_ref[...] = d_attn_out
    d_heads_ref[...] = (
        product(d_attn_out[:, :half], vo_own[:, wide:]) + product(d_attn_out[:, half:], vo_other[:, wide:])
    ).astype(LOW)
    tile = 2 * HEAD_DIM
    for seq in range(rows // capacity):
        at = slice(seq * capacity, (seq + 1) * capacity)
        for start in range(0, wide, tile):
            query_pair = qkv_ref[at, start : start + tile]
            key_pair = qkv_ref[at, wide + start : wide + start + tile]
            val_pair = qkv_ref[at, 2 * wide + start : 2 * wide + start + tile]
            d_query, d_key, d_val = 0.0, 0.0, 0.0
            for query, key, d_head in zip(
                split_heads(query_pair), split_heads(key_pair), split_heads(d_heads_ref[at, start : start + tile])
            ):
                probs = probabilities(query, key_pair, live_ref[seq], scale_qk)
                d_val = d_val + contract_rows(probs.astype(LOW), d_head)
                d_probs = times_transposed(d_head, val_pair)
                d_scores = (
                    probs * (d_probs - jnp.sum(d_probs * probs, axis=-1, keepdims=True))
                ).astype(LOW)
                d_query = d_query + product(d_scores, key)
                d_key = d_key + contract_rows(d_scores, query)
            d_qkv_ref[at, start : start + tile] = (d_query * scale_qk).astype(LOW)
            d_qkv_ref[at, wide + start : wide + start + tile] = (d_key * scale_qk).astype(LOW)
            d_qkv_ref[at, 2 * wide + start : 2 * wide + start + tile] = d_val.astype(LOW)
    d_both = d_qkv_ref[:, : 2 * wide]
    d_vals = d_qkv_ref[:, 2 * wide :]
    d_attn_in = jnp.concatenate(
        [
            times_transposed(d_both, qk[...]) + times_transposed(d_vals, vo[:, :wide])
            for qk, vo in ((qk_own, vo_own), (qk_other, vo_other))
        ],
        axis=1,
    )
    normed_one, inverse_one = norm_forward(routed)
    d_from_norm, small_grads_ref[0:1] = norm_backward(d_attn_in, normed_one, inverse_one, small_ref[0:1])
    d_score = gate_live * (1.0 - gate_prob) * dot_ref[...]
    small_grads_ref[2:3] = jnp.sum(routed * d_score, axis=0, keepdims=True)
    d_routed = (d_middle + d_from_norm + d_score * small_ref[2:3]).astype(LOW)
    d_routed_ref[...] = times_transposed(d_routed, turn_ref[...]).astype(LOW)


def attend_back(live_count, routed, cot_routed, small, turn, attn_out, d_mlp_in, dot, qkv, query_key, value_out, capacity):
    rows, features = routed.shape
    wide = query_key[0].shape[1] // 2
    return pl.pallas_call(
        functools.partial(attend_back_kernel, capacity),
        out_shape=(
            jax.ShapeDtypeStruct((rows, features), LOW),
            jax.ShapeDtypeStruct((rows, features), LOW),
            jax.ShapeDtypeStruct((rows, 3 * wide), LOW),
            jax.ShapeDtypeStruct((3, features), FULL),
        ),
        in_specs=[pl.BlockSpec(memory_space=pltpu.SMEM)] + whole_specs(12),
        out_specs=tuple(whole_specs(4)),
        scratch_shapes=[pltpu.VMEM((rows, wide), LOW)],
        compiler_params=pltpu.CompilerParams(vmem_limit_bytes=56 << 20),
        cost_estimate=pl.CostEstimate(
            flops=8 * rows * features * wide + 10 * rows * capacity * wide,
            bytes_accessed=8 * features * wide + 14 * rows * features,
            transcendentals=rows * capacity * wide // HEAD_DIM,
        ),
        name="attend_back",
    )(live_count, routed, cot_routed, small, turn, attn_out, d_mlp_in, dot, qkv, *query_key, *value_out)


def grads_kernel(attn_in_ref, d_attn_out_ref, heads_ref, d_qkv_ref, qk_kept, qk_sent, vo_kept, vo_sent):
    half = attn_in_ref.shape[1] // 2
    wide = heads_ref.shape[1]
    for at, qk_ref, vo_ref in (
        (slice(half, 2 * half), qk_sent, vo_sent),
        (slice(0, half), qk_kept, vo_kept),
    ):
        attn_in = attn_in_ref[:, at]
        qk_ref[...] = contract_rows(attn_in, d_qkv_ref[:, : 2 * wide]).astype(LOW)
        vo_ref[:, :wide] = contract_rows(attn_in, d_qkv_ref[:, 2 * wide :]).astype(LOW)
        vo_ref[:, wide:] = contract_rows(d_attn_out_ref[:, at], heads_ref[...]).astype(LOW)


def attend_grads(attn_in, d_attn_out, heads_out, d_qkv):
    rows, features = attn_in.shape
    wide = heads_out.shape[1]
    got = pl.pallas_call(
        grads_kernel,
        out_shape=(jax.ShapeDtypeStruct((features // 2, 2 * wide), LOW),) * 4,
        in_specs=whole_specs(4),
        out_specs=tuple(whole_specs(4)),
        compiler_params=pltpu.CompilerParams(vmem_limit_bytes=56 << 20),
        cost_estimate=pl.CostEstimate(
            flops=8 * rows * features * wide,
            bytes_accessed=8 * features * wide + 8 * rows * features,
            transcendentals=0,
        ),
        name="attend_grads",
    )(attn_in, d_attn_out, heads_out, d_qkv)
    return got[:2], got[2:]


class Exchange:
    def __init__(self, mesh):
        self.batch = mesh.shape["batch"]
        self.tensor = mesh.shape["tensor"]
        bits = []
        bit = self.batch // 2
        while bit:
            bits.append(bit)
            bit //= 2
        self.core = bits[-1]
        self.chips = bits[:-1]

    def swap(self, array, bit):
        return lax.ppermute(array, "batch", [(i, i ^ bit) for i in range(self.batch)])

    def shift(self, array, step):
        size = self.tensor
        return lax.ppermute(array, "tensor", [(i, (i + step) % size) for i in range(size)])

    def block_order(self):
        order = [0]
        for bit in reversed([self.core] + self.chips):
            order = order + [place ^ bit for place in order]
        return order

    def gather_rows(self, array, flip):
        rows, width = array.shape
        places = len(self.chips)
        total = array.reshape((1,) * places + array.shape)
        sequence = range(places)
        for place in sequence if flip else reversed(sequence):
            other = self.swap(total, self.chips[place])
            total = jnp.concatenate([total, other], axis=place)
        half = total.reshape(rows * self.batch // 2, width)
        return half, self.swap(half, self.core)

    def gather_tensor(self, array):
        pieces = [array]
        for _ in range(self.tensor - 1):
            pieces.append(self.shift(pieces[-1], 1))
        return pieces

    def gather_small(self, array):
        total = array[None]
        for bit in reversed([self.core] + self.chips):
            total = jnp.concatenate([total, self.swap(total, bit)], axis=0)
        return total.transpose(1, 0, 2).reshape(array.shape[0], -1)

    def sum_all(self, array):
        for bit in self.chips + [self.core]:
            array = array + self.swap(array, bit)
        total = array
        for step in range(1, self.tensor):
            total = total + self.shift(array, step)
        return total

    def scatter_rows(self, kept, sent, flip):
        places = len(self.chips)
        total = add_rounded(kept, self.swap(sent, self.core))
        rows = total.shape[0] // (self.batch // 2)
        total = total.reshape((2,) * places + (rows, total.shape[1]))
        sequence = range(places)
        for place in reversed(sequence) if flip else sequence:
            own = lax.slice_in_dim(total, 0, 1, axis=place)
            other = lax.slice_in_dim(total, 1, 2, axis=place)
            total = add_rounded(own, self.swap(other, self.chips[place]))
        return total.reshape(rows, total.shape[-1])

    def scatter_tensor(self, pieces):
        total = pieces[-1]
        for piece in reversed(pieces[:-1]):
            total = add_rounded(piece, self.shift(total, -1))
        return total


def add_rounded(left, right):
    return (left.astype(FULL) + right.astype(FULL)).astype(LOW)


def shards(
    mesh,
    tokens,
    lengths,
    routes,
    w_query,
    w_key,
    w_value,
    w_out,
    w_up,
    w_down,
    gain_attn,
    gain_mlp,
    w_router,
    cotangent,
):
    moves = Exchange(mesh)
    device = lax.axis_index("batch")
    column = lax.axis_index("tensor")
    seq_count, capacity = routes.shape
    features = tokens.shape[1]
    tokens = tokens.reshape(seq_count, -1, features)
    cotangent = cotangent.reshape(tokens.shape)

    repeats = max(1, moves.tensor // seq_count)
    local_count = max(1, seq_count // moves.tensor)
    first = column // repeats if repeats > 1 else column * local_count
    order = (first + jnp.arange(local_count)).astype(jnp.int32)
    counts_once = (column % repeats) == 0

    def once(values):
        return jnp.where(counts_once, values, jnp.zeros_like(values)) if repeats > 1 else values

    own = features // moves.batch
    place_block = jnp.asarray(moves.block_order(), jnp.int32)
    source = ((place_block ^ device)[:, None] * own + jnp.arange(own, dtype=jnp.int32)).reshape(-1)
    turn = (jnp.arange(features, dtype=jnp.int32)[:, None] == source[None, :]).astype(LOW)

    wide = w_query.shape[1]
    wide_up = w_up.shape[1] // 2

    def fetch(parts, flip):
        pieces = moves.gather_tensor(jnp.concatenate([p.astype(LOW) for p in parts], axis=1))
        width = parts[0].shape[1]
        ordered = [
            piece[:, i * width : (i + 1) * width] for i in range(len(parts)) for piece in pieces
        ]
        return moves.gather_rows(jnp.concatenate(ordered, axis=1), flip)

    down_turned = w_down.astype(LOW).T
    query_key = fetch((w_query, w_key), False)
    value_out = fetch((w_value, w_out.astype(LOW).T), True)
    ups = (fetch((w_up[:, :wide_up],), False), fetch((w_up[:, wide_up:],), True))
    downs = (fetch((down_turned[:, :wide_up],), False), fetch((down_turned[:, wide_up:],), True))
    small = jnp.stack([gain_attn, gain_mlp, w_router]).astype(LOW)
    small = moves.gather_small(small).astype(FULL)

    rows_total = local_count * capacity
    routed, cot_routed = pick_rows(tokens, cotangent, routes, order, local_count, turn)
    routed = routed.reshape(rows_total, features)
    cot_routed = cot_routed.reshape(rows_total, features)
    live_count = lax.dynamic_slice_in_dim(lengths, first, local_count) // 8
    attn_in, qkv, heads_out, attn_out, mlp_in, d_mlp_out = attend(
        live_count, routed, cot_routed, small, query_key, value_out, capacity
    )

    def reduce(kept, sent, parts, flip):
        total = moves.scatter_rows(once(kept), once(sent), flip)
        width = total.shape[1] // parts // moves.tensor
        pieces = [
            jnp.concatenate(
                [
                    total[:, (i * moves.tensor + k) * width : (i * moves.tensor + k + 1) * width]
                    for i in range(parts)
                ],
                axis=1,
            )
            for k in range(moves.tensor)
        ]
        return moves.scatter_tensor(pieces)

    kept = up_layer(mlp_in, d_mlp_out, ups)
    grad_down = [reduce(*stream[2:], 1, flip) for stream, flip in zip(kept, (False, True))]
    update, d_mlp_in, dot, *up_grads = down_layer(
        live_count, routed, cot_routed, small, turn, attn_out, mlp_in, d_mlp_out, ups, downs, kept, capacity
    )
    grad_up = [reduce(*stream, 1, flip) for stream, flip in zip(up_grads, (False, True))]

    def spread_out(rows, table):
        pieces = moves.gather_tensor(rows)
        kept = pieces[::repeats] if repeats > 1 else pieces
        values = jnp.concatenate(
            [piece.reshape(local_count, capacity, features) for piece in kept], axis=0
        )
        steps = jnp.arange(0, moves.tensor, repeats)
        owners = ((column - steps) % moves.tensor).astype(jnp.int32)
        if repeats > 1:
            places = owners // repeats
        else:
            places = (owners[:, None] * local_count + jnp.arange(local_count)).reshape(-1)
        return place_rows(table, values, routes, places.astype(jnp.int32)).reshape(-1, features)

    output = spread_out(update, tokens)
    d_routed, d_attn_out, d_qkv, small_grads = attend_back(
        live_count, routed, cot_routed, small, turn, attn_out, d_mlp_in, dot, qkv, query_key, value_out, capacity
    )
    grad_tokens = spread_out(d_routed, cotangent)
    qk_grads, vo_grads = attend_grads(attn_in, d_attn_out, heads_out, d_qkv)
    grad_query_key = reduce(*qk_grads, 2, False)
    grad_value_out = reduce(*vo_grads, 2, True)

    small_grads = lax.dot_general(
        small_grads, turn.astype(FULL), (((1,), (1,)), ((), ())), precision=lax.Precision.HIGHEST
    )
    small_grads = moves.sum_all(once(small_grads))
    small_grads = lax.dynamic_slice_in_dim(small_grads, device * own, own, axis=1)

    return (
        output,
        grad_tokens,
        grad_query_key[:, :wide].astype(FULL),
        grad_query_key[:, wide:].astype(FULL),
        grad_value_out[:, :wide].astype(FULL),
        grad_value_out[:, wide:].T.astype(FULL),
        jnp.concatenate(grad_up, axis=1).astype(FULL),
        jnp.concatenate(grad_down, axis=1).T.astype(FULL),
        small_grads[0],
        small_grads[1],
        small_grads[2],
    )


def solution(mesh):
    in_specs = (
        P("batch", None),
        P("batch"),
        P("batch", None),
        P("batch", "tensor"),
        P("batch", "tensor"),
        P("batch", "tensor"),
        P("tensor", "batch"),
        P("batch", "tensor"),
        P("tensor", "batch"),
        P("batch"),
        P("batch"),
        P("batch"),
        P("batch", None),
    )
    out_specs = (
        P("batch", None),
        P("batch", None),
        P("batch", "tensor"),
        P("batch", "tensor"),
        P("batch", "tensor"),
        P("tensor", "batch"),
        P("batch", "tensor"),
        P("tensor", "batch"),
        P("batch"),
        P("batch"),
        P("batch"),
    )
    return jax.shard_map(
        functools.partial(shards, mesh),
        mesh=mesh,
        in_specs=in_specs,
        out_specs=out_specs,
        check_vma=False,
    )
```

time: 722 us -> 531 us (0.74)
  matrix products: 116 us -> 2.64 us
  Pallas kernels: 30.3 us -> 116 us
  local copies, waits for them, and re-layouts: 115 us -> 32.5 us
  blocking collectives: 52 us -> 0 us
  other arithmetic: 80.2 us -> 58.1 us
  waiting for transfers between devices: 227 us -> 238 us
  starting transfers between devices: 84.5 us -> 73.7 us
    dot_general x48 -> x1, matrix products: 116 us -> 2.64 us  [shards(): lax.dot_general(small_grads, turn.astype(FULL), (((1,), (1,)), ((), ())),...]
    pallas_call x0 -> x5, Pallas kernels: none -> 66.6 us  [the longest x1 20.5 us: down_layer(): pl.pallas_call(functools.partial(down_kernel, capacity), grid=(width // t...]
    psum x1 -> x0, blocking collectives: 43.1 us -> none  [shards(): small_grads = lax.psum(once(small_grads), ('batch', 'tensor'))]
    unnamed x202 -> x69, local copies, waits for them, and re-layouts: 42.7 us -> 12 us
    reduce_sum x6 -> x0, other arithmetic: 22 us -> none  [the longest x2 11 us: norm_backward(): return (d_input, jnp.sum(d_normed_in * normed, axis=0))]
    rev x6 -> x0, local copies, waits for them, and re-layouts: 18.2 us -> none  [swap_blocks(): jnp.flip(spread, axis=first + place)]
    pallas_call x2, Pallas kernels: 24.8 us -> 41.6 us  [place_rows(): pl.pallas_call(place_kernel, out_shape=jax.ShapeDtypeStruct(table.shape,...]
    ppermute x42 -> x45, waiting for transfers between devices: 80.2 us -> 96.4 us  [shift(): lax.ppermute(array, 'tensor', [(i, (i + step) % size) for i in range(size)])]
  transfers between devices with their start and end apart: 78 -> 87, of which waited for: 36 -> 47; matrix products, arithmetic and copies ran while one was open for 28% -> 17% of each run, Pallas kernels for 4% -> 15%
where the time goes in v2:
time: 531 us; the launch traced here: 526 us
  waiting for transfers between devices  238 us (45%)
  Pallas kernels  116 us (22%)
  starting transfers between devices  73.7 us (14%)
  other arithmetic  58.1 us (11%)
  local copies, waits for them, and re-layouts  32.5 us (6%)
    ppermute x42, waiting for transfers between devices, swap(): lax.ppermute(array, 'batch', [(i, i ^ bit) for i in range(self.batch)])  142 us
    ppermute x45, waiting for transfers between devices, shift(): lax.ppermute(array, 'tensor', [(i, (i + step) % size) for i in range(size)])  96.4 us
    ppermute x45, starting transfers between devices, shift(): lax.ppermute(array, 'tensor', [(i, (i + step) % size) for i in range(size)])  43.1 us
    pallas_call x2, Pallas kernels, place_rows(): pl.pallas_call(place_kernel, out_shape=jax.ShapeDtypeStruct(table.shape,...  41.6 us
    ppermute x42, starting transfers between devices, swap(): lax.ppermute(array, 'batch', [(i, i ^ bit) for i in range(self.batch)])  30.6 us
    convert_element_type x30, other arithmetic, add_rounded(): return (left.astype(FULL) + right.astype(FULL)).astype(LOW)  21.4 us
    concatenate x12, other arithmetic, gather_rows(): total = jnp.concatenate([total, other], axis=place)  21.4 us
    pallas_call x1, Pallas kernels, down_layer(): pl.pallas_call(functools.partial(down_kernel, capacity), grid=(width // t...  20.5 us
  transfers between devices with their start and end apart: 87, of which 47 were waited for; matrix products, arithmetic and copies ran while one was open for 17% of the time, Pallas kernels for 15%

profile of v2, /device:TPU:0, one launch (start us, length us, event | category | flops | bytes accessed | tf_op | source)
XLA Modules:
  0.0 525.7 jit_solution(2168827547795274133)
XLA Ops:
  2.7 3.1 collective-permute-start.9
  16.8 2.1 collective-permute-done.1
  27.2 2.7 collective-permute-done.33
  29.9 2.8 collective-permute-done.10
  32.7 2.8 collective-permute-done.4
  35.5 2.8 collective-permute-done.16
  38.3 2.8 collective-permute-done.28
  41.1 2.8 collective-permute-done.22
  43.9 2.8 collective-permute-done.34
  46.7 2.8 collective-permute-done.11
  49.6 2.7 collective-permute-done.5
  55.7 6.9 %collective-permute-done.12 = bf16[1,1,128,2048]{2,3,1,0:T(8,128)(2,1)S(1)} collective-permute-done((bf16[1,1,128,2048]{2,3,1,0:T(8,128)(2,1)S(1)}, bf16[1,1,128,2048]{2,3,1,0:T(8,128)(2,1)S(1)}, u32[]{:S(2)}, u32[]{:S(2)}) %collective-permute-start.12) | collective-permute-done | bytes 524320 | tf_op jit(solution)/shard_map/ppermute | solution.py:512
  72.6 8.6 %collective-permute-done.18 = bf16[1,1,128,2048]{3,2,1,0:T(8,128)(2,1)S(1)} collective-permute-done((bf16[1,1,128,2048]{3,2,1,0:T(8,128)(2,1)S(1)}, bf16[1,1,128,2048]{3,2,1,0:T(8,128)(2,1)S(1)}, u32[]{:S(2)}, u32[]{:S(2)}) %collective-permute-start.18) | collective-permute-done | bytes 524320 | tf_op jit(solution)/shard_map/ppermute | solution.py:512
  83.8 19.9 %collective-permute-done.13 = bf16[2,1,128,2048]{2,3,1,0:T(8,128)(2,1)S(1)} collective-permute-done((bf16[2,1,128,2048]{2,3,1,0:T(8,128)(2,1)S(1)}, bf16[2,1,128,2048]{2,3,1,0:T(8,128)(2,1)S(1)}, u32[]{:S(2)}, u32[]{:S(2)}) %collective-permute-start.13) | collective-permute-done | bytes 1048608 | tf_op jit(solution)/shard_map/ppermute | solution.py:512
  106.8 3.1 copy.38
  117.0 2.7 pad_maximum_fusion
  119.7 16.4 %collective-permute-done.19 = bf16[1,2,128,2048]{3,2,1,0:T(8,128)(2,1)} collective-permute-done((bf16[1,2,128,2048]{3,2,1,0:T(8,128)(2,1)}, bf16[1,2,128,2048]{3,2,1,0:T(8,128)(2,1)}, u32[]{:S(2)}, u32[]{:S(2)}) %collective-permute-start.19) | collective-permute-done | bytes 1048608 | tf_op jit(solution)/shard_map/ppermute | solution.py:512
  136.1 2.8 pad_maximum_fusion.2
  139.4 2.6 pad_maximum_fusion.4
  142.0 10.2 %collective-permute-done.25 = bf16[1,2,128,2048]{2,3,1,0:T(8,128)(2,1)S(1)} collective-permute-done((bf16[1,2,128,2048]{2,3,1,0:T(8,128)(2,1)S(1)}, bf16[1,2,128,2048]{2,3,1,0:T(8,128)(2,1)S(1)}, u32[]{:S(2)}, u32[]{:S(2)}) %collective-permute-start.25) | collective-permute-done | bytes 1048608 | tf_op jit(solution)/shard_map/ppermute | solution.py:512
  152.3 2.7 pad_maximum_fusion.3
  155.0 4.3 collective-permute-done.37
  159.3 2.7 pad_maximum_fusion.5
  162.0 4.0 copy.39
  166.0 4.0 copy.40
  175.0 8.1 %pick_rows.1 = (bf16[1,256,1024]{2,1,0:T(8,128)(2,1)S(1)}, bf16[1,256,1024]{2,1,0:T(8,128)(2,1)S(1)}) custom-call(s32[1]{0:T(128)} %bitcast.1.order_ref, s32[4,256,1]{2,1,0:T(8,128)S(1)} %copy.36.routes_ref, bf16[1024,1024]{1,0:T(8,128)(2,1)S(1)} %fusion.1.turn_ref, bf16[4,2048,1024]{2,1,0:T(8,128)(2,1)} %bitcast.93, bf16[4,2048,1024]{2,1,0:T(8,128)(2,1)} %bitcast.91), custom_call_target="tpu_custom_call" | custom-call | flops 2147483648 | bytes 8388608 | tf_op jit(solution)/shard_map/pick_rows/pallas_call | solution.py:93
  185.3 11.1 %attend.1 = (bf16[256,1024]{1,0:T(8,128)(2,1)}, bf16[256,3072]{1,0:T(8,128)(2,1)}, bf16[256,1024]{1,0:T(8,128)(2,1)}, f32[256,1024]{1,0:T(8,128)}, bf16[256,1024]{1,0:T(8,128)(2,1)}, /*index=5*/bf16[256,1024]{1,0:T(8,128)(2,1)}) custom-call(s32[1]{0:T(128)S(6)} %select_n.22.live_ref, bf16[256,1024]{1,0:T(8,128)(2,1)} %bitcast.85, ...), custom_call_target="tpu_custom_call" | custom-call | flops 2415919104 | bytes 12058624 | tf_op jit(solution)/shard_map/attend/pallas_call | solution.py:227
  196.4 11.6 %up_layer.1 = (f32[256,2048]{1,0:T(8,128)}, bf16[256,2048]{1,0:T(8,128)(2,1)}, bf16[512,2048]{1,0:T(8,128)(2,1)}, bf16[512,2048]{1,0:T(8,128)(2,1)}, f32[256,204...) custom-call(bf16[256,1024]{1,0:T(8,128)(2,1)} %get-tuple-element.45.mlp_in_ref, ...), custom_call_target="tpu_custom_call" | custom-call | flops 4294967296 | bytes 23068672 | tf_op jit(solution)/shard_map/up_layer/pallas_call | solution.py:282
  209.3 20.5 %down_layer.1 = (bf16[256,1024]{1,0:T(8,128)(2,1)}, f32[256,1024]{1,0:T(8,128)}, f32[256,1]{1,0:T(8,128)}, bf16[512,2048]{1,0:T(8,128)(2,1)}, bf16[512,2048]{1,0...) custom-call(s32[1]{0:T(128)S(6)} %select_n.22.live_ref, bf16[256,1024]{1,0:T(8,128)(2,1)} %bitcast.86, ...), custom_call_target="tpu_custom_call" | custom-call | flops 8589934592 | bytes 31457280 | tf_op jit(solution)/shard_map/down_layer/pallas_call | solution.py:352
  229.8 17.4 %attend_back.1 = (bf16[256,1024]{1,0:T(8,128)(2,1)}, bf16[256,1024]{1,0:T(8,128)(2,1)}, bf16[256,3072]{1,0:T(8,128)(2,1)}, f32[3,1024]{1,0:T(4,128)}) custom-call(s32[1]{0:T(128)S(6)} %select_n.22.live_ref, bf16[256,1024]{1,0:T(8,128)(2,1)} %bitcast.87, bf16[256,1024]{1,0:T(8,128)(2,1)} %bitcast.90, f32[3,1024]{1,0:T(4,128)} %convert_bitcast_fusion.4.small_ref, ...), custom_call_target="tpu_custom_call" | custom-call | flops 2818572288 | bytes 12058624 | tf_op jit(solution)/shard_map/attend_back/pallas_call | solution.py:446
  247.3 16.8 %collective-permute-done.42 = bf16[256,1024]{1,0:T(8,128)(2,1)} collective-permute-done((bf16[256,1024]{1,0:T(8,128)(2,1)}, bf16[256,1024]{1,0:T(8,128)(2,1)}, u32[]{:S(2)}, u32[]{:S(2)}) %collective-permute-start.42) | collective-permute-done | bytes 524320 | tf_op jit(solution)/shard_map/ppermute | solution.py:516
  264.1 11.1 %collective-permute-done.39 = bf16[256,1024]{1,0:T(8,128)(2,1)S(1)} collective-permute-done((bf16[256,1024]{1,0:T(8,128)(2,1)S(1)}, bf16[256,1024]{1,0:T(8,128)(2,1)S(1)}, u32[]{:S(2)}, u32[]{:S(2)}) %collective-permute-start.39) | collective-permute-done | bytes 524320 | tf_op jit(solution)/shard_map/ppermute | solution.py:516
  275.4 2.6 fusion
  278.5 3.2 collective-permute-done.81
  282.3 3.2 collective-permute-done.82
  286.7 4.4 collective-permute-start.85
  291.2 6.7 %collective-permute-done.84 = f32[3,1024]{1,0:T(4,128)S(1)} collective-permute-done((f32[3,1024]{1,0:T(4,128)S(1)}, f32[3,1024]{1,0:T(4,128)S(1)}, u32[]{:S(2)}, u32[]{:S(2)}) %collective-permute-start.84) | collective-permute-done | bytes 12320 | tf_op jit(solution)/shard_map/ppermute | solution.py:516
  297.8 2.0 collective-permute-start.44
  299.9 6.1 %attend_grads.1 = (bf16[512,2048]{1,0:T(8,128)(2,1)}, bf16[512,2048]{1,0:T(8,128)(2,1)}, bf16[512,2048]{1,0:T(8,128)(2,1)}, bf16[512,2048]{1,0:T(8,128)(2,1)}) custom-call(bf16[256,1024]{1,0:T(8,128)(2,1)} %get-tuple-element.56.attn_in_ref, bf16[256,1024]{1,0:T(8,128)(2,1)} %get-tuple-element.57.d_attn_out_ref, ...), custom_call_target="tpu_custom_call" | custom-call | flops 2147483648 | bytes 10485760 | tf_op jit(solution)/shard_map/attend_grads/pallas_call | solution.py:483
  307.0 7.7 %collective-permute-done.44 = bf16[256,1024]{1,0:T(8,128)(2,1)S(1)} collective-permute-done((bf16[256,1024]{1,0:T(8,128)(2,1)}, bf16[256,1024]{1,0:T(8,128)(2,1)S(1)}, u32[]{:S(2)}, u32[]{:S(2)}) %collective-permute-start.44) | collective-permute-done | bytes 524320 | tf_op jit(solution)/shard_map/ppermute | solution.py:516
  316.2 8.3 %collective-permute-done.41 = bf16[256,1024]{1,0:T(8,128)(2,1)S(1)} collective-permute-done((bf16[256,1024]{1,0:T(8,128)(2,1)}, bf16[256,1024]{1,0:T(8,128)(2,1)S(1)}, u32[]{:S(2)}, u32[]{:S(2)}) %collective-permute-start.41) | collective-permute-done | bytes 524320 | tf_op jit(solution)/shard_map/ppermute | solution.py:516
  325.7 20.8 %place_rows.3 = bf16[4,2048,1024]{2,1,0:T(8,128)(2,1)} custom-call(s32[4]{0:T(128)S(1)} %and_select_fusion.order_ref, s32[4,1,256]{2,1,0:T(1,128)S(1)} %broadcast_in_dim.4.routes_ref, bf16[4,2048,1024]{2,1,0:T(8,128)(2,1)} %bitcast.92, bf16[4,256,1024]{2,1,0:T(8,128)(2,1)S(1)} %pad_maximum_fusion.7.values_ref), custom_call_target="tpu_custom_call" | custom-call | flops 4294967296 | bytes 33554432 | tf_op jit(solution)/shard_map/place_rows/pallas_call | solution.py:133
  346.5 20.8 %place_rows.2 = bf16[4,2048,1024]{2,1,0:T(8,128)(2,1)} custom-call(s32[4]{0:T(128)S(1)} %and_select_fusion.order_ref, s32[4,1,256]{2,1,0:T(1,128)S(1)} %broadcast_in_dim.4.routes_ref, bf16[4,2048,1024]{2,1,0:T(8,128)(2,1)} %bitcast.94, bf16[4,256,1024]{2,1,0:T(8,128)(2,1)S(1)} %pad_maximum_fusion.6.values_ref), custom_call_target="tpu_custom_call" | custom-call | flops 4294967296 | bytes 33554432 | tf_op jit(solution)/shard_map/place_rows/pallas_call | solution.py:133
  372.6 2.4 add_convert_fusion
  377.8 3.0 add_convert_fusion.3
  383.5 2.4 add_convert_fusion.2
  388.5 2.4 add_convert_fusion.4
  392.3 2.3 copy.49
  394.6 2.3 copy.48
  397.8 3.0 add_convert_fusion.5
  406.7 13.9 %collective-permute-done.58 = bf16[1,2,128,2048]{3,2,1,0:T(8,128)(2,1)} collective-permute-done((bf16[1,2,128,2048]{3,2,1,0:T(8,128)(2,1)}, bf16[1,2,128,2048]{3,2,1,0:T(8,128)(2,1)}, u32[]{:S(2)}, u32[]{:S(2)}) %collective-permute-start.58) | collective-permute-done | bytes 1048608 | tf_op jit(solution)/shard_map/ppermute | solution.py:512
  422.8 3.2 collective-permute-done.64
  428.2 20.2 %collective-permute-done.52 = bf16[2,1,128,2048]{2,3,1,0:T(8,128)(2,1)S(1)} collective-permute-done((bf16[2,1,128,2048]{2,3,1,0:T(8,128)(2,1)}, bf16[2,1,128,2048]{2,3,1,0:T(8,128)(2,1)S(1)}, u32[]{:S(2)}, u32[]{:S(2)}) %collective-permute-start.52) | collective-permute-done | bytes 1048608 | tf_op jit(solution)/shard_map/ppermute | solution.py:512
  451.3 8.4 %collective-permute-done.71 = bf16[1,1,128,2048]{2,3,1,0:T(8,128)(2,1)S(1)} collective-permute-done((bf16[1,1,128,2048]{2,3,1,0:T(8,128)(2,1)S(1)}, bf16[1,1,128,2048]{2,3,1,0:T(8,128)(2,1)S(1)}, u32[]{:S(2)}, u32[]{:S(2)}) %collective-permute-start.71) | collective-permute-done | bytes 524320 | tf_op jit(solution)/shard_map/ppermute | solution.py:512
  460.6 10.3 %collective-permute-done.59 = bf16[1,1,128,2048]{3,2,1,0:T(8,128)(2,1)S(1)} collective-permute-done((bf16[1,1,128,2048]{3,2,1,0:T(8,128)(2,1)S(1)}, bf16[1,1,128,2048]{3,2,1,0:T(8,128)(2,1)S(1)}, u32[]{:S(2)}, u32[]{:S(2)}) %collective-permute-start.59) | collective-permute-done | bytes 524320 | tf_op jit(solution)/shard_map/ppermute | solution.py:512
  472.8 3.0 collective-permute-done.53
  476.0 5.2 collective-permute-done.47
  484.4 2.1 collective-permute-start.79
  487.6 1.8 collective-permute-start.67
  493.2 1.8 collective-permute-start.49
  498.8 1.8 collective-permute-start.80
  501.6 1.8 collective-permute-start.62
  512.9 2.8 collective-permute-done.62
  515.7 5.1 collective-permute-done.56
  (302 shorter events, 118.5 us)
Async XLA Ops:
  2.7 17.8 %collective-permute-start.9 = (bf16[128,512]{0,1:T(8,128)(2,1)S(1)}, bf16[128,512]{0,1:T(8,128)(2,1)S(1)}, u32[]{:S(2)}, u32[]{:S(2)}) collective-permute-start(bf16[128,512]{0,1:T(8,128)(2,1)S(1)} %pad_maximum_fusion.15), channel_id=1, source_target_pairs={{0,1},{1,2},{2,3},{3,0},{4,5},{5,6},{6,7},{7,4},{8,9},{9,10},{10,1... | collective-permute-start | bytes 393224 | tf_op jit(solution)/shard_map/ppermute | solution.py:516
  7.6 14.5 %collective-permute-start.3 = (bf16[128,512]{1,0:T(8,128)(2,1)S(1)}, bf16[128,512]{1,0:T(8,128)(2,1)S(1)}, u32[]{:S(2)}, u32[]{:S(2)}) collective-permute-start(bf16[128,512]{1,0:T(8,128)(2,1)S(1)} %pad_maximum_fusion.14), channel_id=1, source_target_pairs={{0,1},{1,2},{2,3},{3,0},{4,5},{5,6},{6,7},{7,4},{8,9},{9,10},{10,1... | collective-permute-start | bytes 393224 | tf_op jit(solution)/shard_map/ppermute | solution.py:516
  24.0 14.3 %collective-permute-start.16 = (bf16[128,512]{1,0:T(8,128)(2,1)S(1)}, bf16[128,512]{1,0:T(8,128)(2,1)S(1)}, u32[]{:S(2)}, u32[]{:S(2)}) collective-permute-start(bf16[128,512]{1,0:T(8,128)(2,1)S(1)} %collective-permute-done.15), channel_id=1, source_target_pairs={{0,1},{1,2},{2,3},{3,0},{4,5},{5,6},{6,7},{7,4},{8,9},{9,10},{10,1... | collective-permute-start | bytes 393224 | tf_op jit(solution)/shard_map/ppermute | solution.py:516
  27.1 14.0 %collective-permute-start.28 = (bf16[128,512]{1,0:T(8,128)(2,1)S(1)}, bf16[128,512]{1,0:T(8,128)(2,1)S(1)}, u32[]{:S(2)}, u32[]{:S(2)}) collective-permute-start(bf16[128,512]{1,0:T(8,128)(2,1)S(1)} %collective-permute-done.27), channel_id=1, source_target_pairs={{0,1},{1,2},{2,3},{3,0},{4,5},{5,6},{6,7},{7,4},{8,9},{9,10},{10,1... | collective-permute-start | bytes 393224 | tf_op jit(solution)/shard_map/ppermute | solution.py:516
  29.9 14.0 %collective-permute-start.22 = (bf16[128,512]{0,1:T(8,128)(2,1)S(1)}, bf16[128,512]{0,1:T(8,128)(2,1)S(1)}, u32[]{:S(2)}, u32[]{:S(2)}) collective-permute-start(bf16[128,512]{0,1:T(8,128)(2,1)S(1)} %collective-permute-done.21), channel_id=1, source_target_pairs={{0,1},{1,2},{2,3},{3,0},{4,5},{5,6},{6,7},{7,4},{8,9},{9,10},{10,1... | collective-permute-start | bytes 393224 | tf_op jit(solution)/shard_map/ppermute | solution.py:516
  32.7 14.0 %collective-permute-start.34 = (bf16[128,512]{0,1:T(8,128)(2,1)S(1)}, bf16[128,512]{0,1:T(8,128)(2,1)S(1)}, u32[]{:S(2)}, u32[]{:S(2)}) collective-permute-start(bf16[128,512]{0,1:T(8,128)(2,1)S(1)} %collective-permute-done.33), channel_id=1, source_target_pairs={{0,1},{1,2},{2,3},{3,0},{4,5},{5,6},{6,7},{7,4},{8,9},{9,10},{10,1... | collective-permute-start | bytes 393224 | tf_op jit(solution)/shard_map/ppermute | solution.py:516
  35.5 14.0 %collective-permute-start.11 = (bf16[128,512]{0,1:T(8,128)(2,1)S(1)}, bf16[128,512]{0,1:T(8,128)(2,1)S(1)}, u32[]{:S(2)}, u32[]{:S(2)}) collective-permute-start(bf16[128,512]{0,1:T(8,128)(2,1)S(1)} %collective-permute-done.10), channel_id=1, source_target_pairs={{0,1},{1,2},{2,3},{3,0},{4,5},{5,6},{6,7},{7,4},{8,9},{9,10},{10,1... | collective-permute-start | bytes 393224 | tf_op jit(solution)/shard_map/ppermute | solution.py:516
  38.3 14.0 %collective-permute-start.5 = (bf16[128,512]{1,0:T(8,128)(2,1)S(1)}, bf16[128,512]{1,0:T(8,128)(2,1)S(1)}, u32[]{:S(2)}, u32[]{:S(2)}) collective-permute-start(bf16[128,512]{1,0:T(8,128)(2,1)S(1)} %collective-permute-done.4), channel_id=1, source_target_pairs={{0,1},{1,2},{2,3},{3,0},{4,5},{5,6},{6,7},{7,4},{8,9},{9,10},{10,1... | collective-permute-start | bytes 393224 | tf_op jit(solution)/shard_map/ppermute | solution.py:516
  41.1 14.0 %collective-permute-start.17 = (bf16[128,512]{1,0:T(8,128)(2,1)S(1)}, bf16[128,512]{1,0:T(8,128)(2,1)S(1)}, u32[]{:S(2)}, u32[]{:S(2)}) collective-permute-start(bf16[128,512]{1,0:T(8,128)(2,1)S(1)} %collective-permute-done.16), channel_id=1, source_target_pairs={{0,1},{1,2},{2,3},{3,0},{4,5},{5,6},{6,7},{7,4},{8,9},{9,10},{10,1... | collective-permute-start | bytes 393224 | tf_op jit(solution)/shard_map/ppermute | solution.py:516
  43.9 19.4 %collective-permute-start.29 = (bf16[128,512]{1,0:T(8,128)(2,1)S(1)}, bf16[128,512]{1,0:T(8,128)(2,1)S(1)}, u32[]{:S(2)}, u32[]{:S(2)}) collective-permute-start(bf16[128,512]{1,0:T(8,128)(2,1)S(1)} %collective-permute-done.28), channel_id=1, source_target_pairs={{0,1},{1,2},{2,3},{3,0},{4,5},{5,6},{6,7},{7,4},{8,9},{9,10},{10,1... | collective-permute-start | bytes 393224 | tf_op jit(solution)/shard_map/ppermute | solution.py:516
  46.7 18.2 %collective-permute-start.23 = (bf16[128,512]{0,1:T(8,128)(2,1)S(1)}, bf16[128,512]{0,1:T(8,128)(2,1)S(1)}, u32[]{:S(2)}, u32[]{:S(2)}) collective-permute-start(bf16[128,512]{0,1:T(8,128)(2,1)S(1)} %collective-permute-done.22), channel_id=1, source_target_pairs={{0,1},{1,2},{2,3},{3,0},{4,5},{5,6},{6,7},{7,4},{8,9},{9,10},{10,1... | collective-permute-start | bytes 393224 | tf_op jit(solution)/shard_map/ppermute | solution.py:516
  49.5 17.8 %collective-permute-start.35 = (bf16[128,512]{0,1:T(8,128)(2,1)S(1)}, bf16[128,512]{0,1:T(8,128)(2,1)S(1)}, u32[]{:S(2)}, u32[]{:S(2)}) collective-permute-start(bf16[128,512]{0,1:T(8,128)(2,1)S(1)} %collective-permute-done.34), channel_id=1, source_target_pairs={{0,1},{1,2},{2,3},{3,0},{4,5},{5,6},{6,7},{7,4},{8,9},{9,10},{10,1... | collective-permute-start | bytes 393224 | tf_op jit(solution)/shard_map/ppermute | solution.py:516
  55.2 14.9 %collective-permute-start.6 = (bf16[1,1,128,2048]{3,2,1,0:T(8,128)(2,1)S(1)}, bf16[1,1,128,2048]{3,2,1,0:T(8,128)(2,1)S(1)}, u32[]{:S(2)}, u32[]{:S(2)}) collective-permute-start(bf16[1,1,128,2048]{3,2,1,0:T(8,128)(2,1)S(1)} %bitcast.108), channel_id=1, source_target_pairs={{0,8},{4,12},{8,0},{12,4},{16,24},{20,28},{24,16},{28,20},{1,9},{5... | collective-permute-start | bytes 1572872 | tf_op jit(solution)/shard_map/ppermute | solution.py:512
  62.7 18.6 %collective-permute-start.18 = (bf16[1,1,128,2048]{3,2,1,0:T(8,128)(2,1)S(1)}, bf16[1,1,128,2048]{3,2,1,0:T(8,128)(2,1)S(1)}, u32[]{:S(2)}, u32[]{:S(2)}) collective-permute-start(bf16[1,1,128,2048]{3,2,1,0:T(8,128)(2,1)S(1)} %maximum_bitcast_fusion), channel_id=1, source_target_pairs={{0,8},{4,12},{8,0},{12,4},{16,24},{20,28},{24,16},{28,20},{1,9},{5... | collective-permute-start | bytes 1572872 | tf_op jit(solution)/shard_map/ppermute | solution.py:512
  63.3 40.4 %collective-permute-start.13 = (bf16[2,1,128,2048]{2,3,1,0:T(8,128)(2,1)S(1)}, bf16[2,1,128,2048]{2,3,1,0:T(8,128)(2,1)S(1)}, u32[]{:S(2)}, u32[]{:S(2)}) collective-permute-start(bf16[2,1,128,2048]{2,3,1,0:T(8,128)(2,1)S(1)} %pad_maximum_fusion.9), channel_id=1, source_target_pairs={{0,8},{4,12},{8,0},{12,4},{16,24},{20,28},{24,16},{28,20},{1,9},{5... | collective-permute-start | bytes 3145736 | tf_op jit(solution)/shard_map/ppermute | solution.py:512
  64.9 45.0 %collective-permute-start.30 = (bf16[1,1,128,2048]{3,2,1,0:T(8,128)(2,1)S(1)}, bf16[1,1,128,2048]{3,2,1,0:T(8,128)(2,1)}, u32[]{:S(2)}, u32[]{:S(2)}) collective-permute-start(bf16[1,1,128,2048]{3,2,1,0:T(8,128)(2,1)S(1)} %maximum_bitcast_fusion.2), channel_id=1, source_target_pairs={{0,16},{4,20},{8,24},{12,28},{16,0},{20,4},{24,8},{28,12},{1,17},{... | collective-permute-start | bytes 1572872 | tf_op jit(solution)/shard_map/ppermute | solution.py:512
  67.4 44.2 %collective-permute-start.24 = (bf16[1,1,128,2048]{2,3,1,0:T(8,128)(2,1)}, bf16[1,1,128,2048]{2,3,1,0:T(8,128)(2,1)}, u32[]{:S(2)}, u32[]{:S(2)}) collective-permute-start(bf16[1,1,128,2048]{2,3,1,0:T(8,128)(2,1)} %maximum_bitcast_fusion.1), channel_id=1, source_target_pairs={{0,8},{4,12},{8,0},{12,4},{16,24},{20,28},{24,16},{28,20},{1,9},{5... | collective-permute-start | bytes 1572872 | tf_op jit(solution)/shard_map/ppermute | solution.py:512
  70.0 43.5 %collective-permute-start.36 = (bf16[1,1,128,2048]{2,3,1,0:T(8,128)(2,1)}, bf16[1,1,128,2048]{2,3,1,0:T(8,128)(2,1)}, u32[]{:S(2)}, u32[]{:S(2)}) collective-permute-start(bf16[1,1,128,2048]{2,3,1,0:T(8,128)(2,1)} %maximum_bitcast_fusion.3), channel_id=1, source_target_pairs={{0,16},{4,20},{8,24},{12,28},{16,0},{20,4},{24,8},{28,12},{1,17},{... | collective-permute-start | bytes 1572872 | tf_op jit(solution)/shard_map/ppermute | solution.py:512
  81.3 34.1 %collective-permute-start.7 = (bf16[1,2,128,2048]{3,2,1,0:T(8,128)(2,1)}, bf16[1,2,128,2048]{3,2,1,0:T(8,128)(2,1)}, u32[]{:S(2)}, u32[]{:S(2)}) collective-permute-start(bf16[1,2,128,2048]{3,2,1,0:T(8,128)(2,1)} %pad_maximum_fusion.8), channel_id=1, source_target_pairs={{0,16},{4,20},{8,24},{12,28},{16,0},{20,4},{24,8},{28,12},{1,17},{... | collective-permute-start | bytes 3145736 | tf_op jit(solution)/shard_map/ppermute | solution.py:512
  103.7 32.4 %collective-permute-start.19 = (bf16[1,2,128,2048]{3,2,1,0:T(8,128)(2,1)}, bf16[1,2,128,2048]{3,2,1,0:T(8,128)(2,1)}, u32[]{:S(2)}, u32[]{:S(2)}) collective-permute-start(bf16[1,2,128,2048]{3,2,1,0:T(8,128)(2,1)} %pad_maximum_fusion.10), channel_id=1, source_target_pairs={{0,16},{4,20},{8,24},{12,28},{16,0},{20,4},{24,8},{28,12},{1,17},{... | collective-permute-start | bytes 3145736 | tf_op jit(solution)/shard_map/ppermute | solution.py:512
  109.9 60.6 %collective-permute-start.14 = (bf16[512,2048]{1,0:T(8,128)(2,1)S(1)}, bf16[512,2048]{1,0:T(8,128)(2,1)}, u32[]{:S(2)}, u32[]{:S(2)}) collective-permute-start(bf16[512,2048]{1,0:T(8,128)(2,1)S(1)} %bitcast.95), channel_id=1, source_target_pairs={{0,4},{4,0},{8,12},{12,8},{16,20},{20,16},{24,28},{28,24},{1,5},{5... | collective-permute-start | bytes 6291464 | tf_op jit(solution)/shard_map/ppermute | solution.py:512
  111.6 27.4 %collective-permute-start.31 = (bf16[2,1,128,2048]{3,2,1,0:T(8,128)(2,1)S(1)}, bf16[2,1,128,2048]{3,2,1,0:T(8,128)(2,1)S(1)}, u32[]{:S(2)}, u32[]{:S(2)}) collective-permute-start(bf16[2,1,128,2048]{3,2,1,0:T(8,128)(2,1)S(1)} %pad_maximum_fusion.12), channel_id=1, source_target_pairs={{0,8},{4,12},{8,0},{12,4},{16,24},{20,28},{24,16},{28,20},{1,9},{5... | collective-permute-start | bytes 3145736 | tf_op jit(solution)/shard_map/ppermute | solution.py:512
  113.5 38.8 %collective-permute-start.25 = (bf16[1,2,128,2048]{2,3,1,0:T(8,128)(2,1)S(1)}, bf16[1,2,128,2048]{2,3,1,0:T(8,128)(2,1)S(1)}, u32[]{:S(2)}, u32[]{:S(2)}) collective-permute-start(bf16[1,2,128,2048]{2,3,1,0:T(8,128)(2,1)S(1)} %pad_maximum_fusion.11), channel_id=1, source_target_pairs={{0,16},{4,20},{8,24},{12,28},{16,0},{20,4},{24,8},{28,12},{1,17},{... | collective-permute-start | bytes 3145736 | tf_op jit(solution)/shard_map/ppermute | solution.py:512
  115.4 43.9 %collective-permute-start.37 = (bf16[2,1,128,2048]{2,3,1,0:T(8,128)(2,1)S(1)}, bf16[2,1,128,2048]{2,3,1,0:T(8,128)(2,1)S(1)}, u32[]{:S(2)}, u32[]{:S(2)}) collective-permute-start(bf16[2,1,128,2048]{2,3,1,0:T(8,128)(2,1)S(1)} %pad_maximum_fusion.13), channel_id=1, source_target_pairs={{0,8},{4,12},{8,0},{12,4},{16,24},{20,28},{24,16},{28,20},{1,9},{5... | collective-permute-start | bytes 3145736 | tf_op jit(solution)/shard_map/ppermute | solution.py:512
  136.1 49.2 %collective-permute-start.8 = (bf16[512,2048]{1,0:T(8,128)(2,1)}, bf16[512,2048]{1,0:T(8,128)(2,1)}, u32[]{:S(2)}, u32[]{:S(2)}) collective-permute-start(bf16[512,2048]{1,0:T(8,128)(2,1)} %bitcast.14.qk_own), channel_id=1, source_target_pairs={{0,4},{4,0},{8,12},{12,8},{16,20},{20,16},{24,28},{28,24},{1,5},{5... | collective-permute-start | bytes 6291464 | tf_op jit(solution)/shard_map/ppermute | solution.py:512
  138.9 57.5 %collective-permute-start.20 = (bf16[512,2048]{1,0:T(8,128)(2,1)}, bf16[512,2048]{1,0:T(8,128)(2,1)}, u32[]{:S(2)}, u32[]{:S(2)}) collective-permute-start(bf16[512,2048]{1,0:T(8,128)(2,1)} %bitcast.19.refs_0_), channel_id=1, source_target_pairs={{0,4},{4,0},{8,12},{12,8},{16,20},{20,16},{24,28},{28,24},{1,5},{5... | collective-permute-start | bytes 6291464 | tf_op jit(solution)/shard_map/ppermute | solution.py:512
  152.3 44.1 %collective-permute-start.32 = (bf16[512,2048]{1,0:T(8,128)(2,1)}, bf16[512,2048]{1,0:T(8,128)(2,1)}, u32[]{:S(2)}, u32[]{:S(2)}) collective-permute-start(bf16[512,2048]{1,0:T(8,128)(2,1)} %bitcast.24.refs_2_.refs_4_), channel_id=1, source_target_pairs={{0,4},{4,0},{8,12},{12,8},{16,20},{20,16},{24,28},{28,24},{1,5},{5... | collective-permute-start | bytes 6291464 | tf_op jit(solution)/shard_map/ppermute | solution.py:512
  170.0 38.0 %collective-permute-start.26 = (bf16[512,2048]{1,0:T(8,128)(2,1)}, bf16[512,2048]{1,0:T(8,128)(2,1)}, u32[]{:S(2)}, u32[]{:S(2)}) collective-permute-start(bf16[512,2048]{1,0:T(8,128)(2,1)} %bitcast.114), channel_id=1, source_target_pairs={{0,4},{4,0},{8,12},{12,8},{16,20},{20,16},{24,28},{28,24},{1,5},{5... | collective-permute-start | bytes 6291464 | tf_op jit(solution)/shard_map/ppermute | solution.py:512
  170.5 37.5 %collective-permute-start.38 = (bf16[512,2048]{1,0:T(8,128)(2,1)}, bf16[512,2048]{1,0:T(8,128)(2,1)S(1)}, u32[]{:S(2)}, u32[]{:S(2)}) collective-permute-start(bf16[512,2048]{1,0:T(8,128)(2,1)} %bitcast.116), channel_id=1, source_target_pairs={{0,4},{4,0},{8,12},{12,8},{16,20},{20,16},{24,28},{28,24},{1,5},{5... | collective-permute-start | bytes 6291464 | tf_op jit(solution)/shard_map/ppermute | solution.py:512
  247.2 16.8 %collective-permute-start.42 = (bf16[256,1024]{1,0:T(8,128)(2,1)}, bf16[256,1024]{1,0:T(8,128)(2,1)}, u32[]{:S(2)}, u32[]{:S(2)}) collective-permute-start(bf16[256,1024]{1,0:T(8,128)(2,1)} %get-tuple-element.55), channel_id=1, source_target_pairs={{0,1},{1,2},{2,3},{3,0},{4,5},{5,6},{6,7},{7,4},{8,9},{9,10},{10,1... | collective-permute-start | bytes 1572872 | tf_op jit(solution)/shard_map/ppermute | solution.py:516
  247.2 28.0 %collective-permute-start.39 = (bf16[256,1024]{1,0:T(8,128)(2,1)S(1)}, bf16[256,1024]{1,0:T(8,128)(2,1)S(1)}, u32[]{:S(2)}, u32[]{:S(2)}) collective-permute-start(bf16[256,1024]{1,0:T(8,128)(2,1)S(1)} %copy-done.20), channel_id=1, source_target_pairs={{0,1},{1,2},{2,3},{3,0},{4,5},{5,6},{6,7},{7,4},{8,9},{9,10},{10,1... | collective-permute-start | bytes 1572872 | tf_op jit(solution)/shard_map/ppermute | solution.py:516
  264.1 33.8 %collective-permute-start.43 = (bf16[256,1024]{1,0:T(8,128)(2,1)}, bf16[256,1024]{1,0:T(8,128)(2,1)}, u32[]{:S(2)}, u32[]{:S(2)}) collective-permute-start(bf16[256,1024]{1,0:T(8,128)(2,1)} %collective-permute-done.42), channel_id=1, source_target_pairs={{0,1},{1,2},{2,3},{3,0},{4,5},{5,6},{6,7},{7,4},{8,9},{9,10},{10,1... | collective-permute-start | bytes 1572872 | tf_op jit(solution)/shard_map/ppermute | solution.py:516
  264.1 103.3 %collective-permute-start.69 = (bf16[512,2048]{1,0:T(8,128)(2,1)}, bf16[512,2048]{1,0:T(8,128)(2,1)S(1)}, u32[]{:S(2)}, u32[]{:S(2)}) collective-permute-start(bf16[512,2048]{1,0:T(8,128)(2,1)} %get-tuple-element.69), channel_id=1, source_target_pairs={{0,4},{4,0},{8,12},{12,8},{16,20},{20,16},{24,28},{28,24},{1,5},{5... | collective-permute-start | bytes 6291464 | tf_op jit(solution)/shard_map/ppermute | solution.py:512
  275.2 31.3 %collective-permute-start.40 = (bf16[256,1024]{1,0:T(8,128)(2,1)S(1)}, bf16[256,1024]{1,0:T(8,128)(2,1)}, u32[]{:S(2)}, u32[]{:S(2)}) collective-permute-start(bf16[256,1024]{1,0:T(8,128)(2,1)S(1)} %collective-permute-done.39), channel_id=1, source_target_pairs={{0,1},{1,2},{2,3},{3,0},{4,5},{5,6},{6,7},{7,4},{8,9},{9,10},{10,1... | collective-permute-start | bytes 1572872 | tf_op jit(solution)/shard_map/ppermute | solution.py:516
  286.7 19.2 %collective-permute-start.85 = (f32[3,1024]{1,0:T(4,128)S(1)}, f32[3,1024]{1,0:T(4,128)S(1)}, u32[]{:S(2)}, u32[]{:S(2)}) collective-permute-start(f32[3,1024]{1,0:T(4,128)S(1)} %add.209), channel_id=1, source_target_pairs={{0,2},{1,3},{2,0},{3,1},{4,6},{5,7},{6,4},{7,5},{8,10},{9,11},{10,... | collective-permute-start | bytes 36872 | tf_op jit(solution)/shard_map/ppermute | solution.py:516
  297.8 16.9 %collective-permute-start.44 = (bf16[256,1024]{1,0:T(8,128)(2,1)}, bf16[256,1024]{1,0:T(8,128)(2,1)S(1)}, u32[]{:S(2)}, u32[]{:S(2)}) collective-permute-start(bf16[256,1024]{1,0:T(8,128)(2,1)} %collective-permute-done.43), channel_id=1, source_target_pairs={{0,1},{1,2},{2,3},{3,0},{4,5},{5,6},{6,7},{7,4},{8,9},{9,10},{10,1... | collective-permute-start | bytes 1572872 | tf_op jit(solution)/shard_map/ppermute | solution.py:516
  306.0 65.9 %collective-permute-start.75 = (bf16[512,2048]{1,0:T(8,128)(2,1)}, bf16[512,2048]{1,0:T(8,128)(2,1)}, u32[]{:S(2)}, u32[]{:S(2)}) collective-permute-start(bf16[512,2048]{1,0:T(8,128)(2,1)} %get-tuple-element.71), channel_id=1, source_target_pairs={{0,4},{4,0},{8,12},{12,8},{16,20},{20,16},{24,28},{28,24},{1,5},{5... | collective-permute-start | bytes 6291464 | tf_op jit(solution)/shard_map/ppermute | solution.py:512
  306.0 71.2 %collective-permute-start.57 = (bf16[512,2048]{1,0:T(8,128)(2,1)}, bf16[512,2048]{1,0:T(8,128)(2,1)}, u32[]{:S(2)}, u32[]{:S(2)}) collective-permute-start(bf16[512,2048]{1,0:T(8,128)(2,1)} %get-tuple-element.65), channel_id=1, source_target_pairs={{0,4},{4,0},{8,12},{12,8},{16,20},{20,16},{24,28},{28,24},{1,5},{5... | collective-permute-start | bytes 6291464 | tf_op jit(solution)/shard_map/ppermute | solution.py:512
  306.5 18.0 %collective-permute-start.41 = (bf16[256,1024]{1,0:T(8,128)(2,1)}, bf16[256,1024]{1,0:T(8,128)(2,1)S(1)}, u32[]{:S(2)}, u32[]{:S(2)}) collective-permute-start(bf16[256,1024]{1,0:T(8,128)(2,1)} %collective-permute-done.40), channel_id=1, source_target_pairs={{0,1},{1,2},{2,3},{3,0},{4,5},{5,6},{6,7},{7,4},{8,9},{9,10},{10,1... | collective-permute-start | bytes 1572872 | tf_op jit(solution)/shard_map/ppermute | solution.py:516
  314.7 67.5 %collective-permute-start.63 = (bf16[512,2048]{1,0:T(8,128)(2,1)}, bf16[512,2048]{1,0:T(8,128)(2,1)}, u32[]{:S(2)}, u32[]{:S(2)}) collective-permute-start(bf16[512,2048]{1,0:T(8,128)(2,1)} %get-tuple-element.67), channel_id=1, source_target_pairs={{0,4},{4,0},{8,12},{12,8},{16,20},{20,16},{24,28},{28,24},{1,5},{5... | collective-permute-start | bytes 6291464 | tf_op jit(solution)/shard_map/ppermute | solution.py:512
  324.4 62.5 %collective-permute-start.51 = (bf16[512,2048]{1,0:T(8,128)(2,1)}, bf16[512,2048]{1,0:T(8,128)(2,1)}, u32[]{:S(2)}, u32[]{:S(2)}) collective-permute-start(bf16[512,2048]{1,0:T(8,128)(2,1)} %get-tuple-element.63), channel_id=1, source_target_pairs={{0,4},{4,0},{8,12},{12,8},{16,20},{20,16},{24,28},{28,24},{1,5},{5... | collective-permute-start | bytes 6291464 | tf_op jit(solution)/shard_map/ppermute | solution.py:512
  367.4 29.5 %collective-permute-start.45 = (bf16[512,2048]{1,0:T(8,128)(2,1)}, bf16[512,2048]{1,0:T(8,128)(2,1)}, u32[]{:S(2)}, u32[]{:S(2)}) collective-permute-start(bf16[512,2048]{1,0:T(8,128)(2,1)} %get-tuple-element.61), channel_id=1, source_target_pairs={{0,4},{4,0},{8,12},{12,8},{16,20},{20,16},{24,28},{28,24},{1,5},{5... | collective-permute-start | bytes 6291464 | tf_op jit(solution)/shard_map/ppermute | solution.py:512
  371.8 29.2 %collective-permute-start.70 = (bf16[1,2,128,2048]{2,3,1,0:T(8,128)(2,1)}, bf16[1,2,128,2048]{2,3,1,0:T(8,128)(2,1)}, u32[]{:S(2)}, u32[]{:S(2)}) collective-permute-start(bf16[1,2,128,2048]{2,3,1,0:T(8,128)(2,1)} %copy.43), channel_id=1, source_target_pairs={{0,16},{4,20},{8,24},{12,28},{16,0},{20,4},{24,8},{28,12},{1,17},{... | collective-permute-start | bytes 3145736 | tf_op jit(solution)/shard_map/ppermute | solution.py:512
  377.2 26.8 %collective-permute-start.76 = (bf16[2,1,128,2048]{2,3,1,0:T(8,128)(2,1)}, bf16[2,1,128,2048]{2,3,1,0:T(8,128)(2,1)}, u32[]{:S(2)}, u32[]{:S(2)}) collective-permute-start(bf16[2,1,128,2048]{2,3,1,0:T(8,128)(2,1)} %copy.51), channel_id=1, source_target_pairs={{0,8},{4,12},{8,0},{12,4},{16,24},{20,28},{24,16},{28,20},{1,9},{5... | collective-permute-start | bytes 3145736 | tf_op jit(solution)/shard_map/ppermute | solution.py:512
  382.2 38.4 %collective-permute-start.58 = (bf16[1,2,128,2048]{3,2,1,0:T(8,128)(2,1)}, bf16[1,2,128,2048]{3,2,1,0:T(8,128)(2,1)}, u32[]{:S(2)}, u32[]{:S(2)}) collective-permute-start(bf16[1,2,128,2048]{3,2,1,0:T(8,128)(2,1)} %bitcast.44), channel_id=1, source_target_pairs={{0,16},{4,20},{8,24},{12,28},{16,0},{20,4},{24,8},{28,12},{1,17},{... | collective-permute-start | bytes 3145736 | tf_op jit(solution)/shard_map/ppermute | solution.py:512
  387.0 39.0 %collective-permute-start.64 = (bf16[2,1,128,2048]{3,2,1,0:T(8,128)(2,1)}, bf16[2,1,128,2048]{3,2,1,0:T(8,128)(2,1)}, u32[]{:S(2)}, u32[]{:S(2)}) collective-permute-start(bf16[2,1,128,2048]{3,2,1,0:T(8,128)(2,1)} %slice.386), channel_id=1, source_target_pairs={{0,8},{4,12},{8,0},{12,4},{16,24},{20,28},{24,16},{28,20},{1,9},{5... | collective-permute-start | bytes 3145736 | tf_op jit(solution)/shard_map/ppermute | solution.py:512
  396.9 51.5 %collective-permute-start.52 = (bf16[2,1,128,2048]{2,3,1,0:T(8,128)(2,1)}, bf16[2,1,128,2048]{2,3,1,0:T(8,128)(2,1)S(1)}, u32[]{:S(2)}, u32[]{:S(2)}) collective-permute-start(bf16[2,1,128,2048]{2,3,1,0:T(8,128)(2,1)} %copy.49), channel_id=1, source_target_pairs={{0,8},{4,12},{8,0},{12,4},{16,24},{20,28},{24,16},{28,20},{1,9},{5... | collective-permute-start | bytes 3145736 | tf_op jit(solution)/shard_map/ppermute | solution.py:512
  401.0 49.1 %collective-permute-start.46 = (bf16[1,2,128,2048]{3,2,1,0:T(8,128)(2,1)S(1)}, bf16[1,2,128,2048]{3,2,1,0:T(8,128)(2,1)S(1)}, u32[]{:S(2)}, u32[]{:S(2)}) collective-permute-start(bf16[1,2,128,2048]{3,2,1,0:T(8,128)(2,1)S(1)} %bitcast.118), channel_id=1, source_target_pairs={{0,16},{4,20},{8,24},{12,28},{16,0},{20,4},{24,8},{28,12},{1,17},{... | collective-permute-start | bytes 3145736 | tf_op jit(solution)/shard_map/ppermute | solution.py:512
  403.9 55.7 %collective-permute-start.71 = (bf16[1,1,128,2048]{2,3,1,0:T(8,128)(2,1)S(1)}, bf16[1,1,128,2048]{2,3,1,0:T(8,128)(2,1)S(1)}, u32[]{:S(2)}, u32[]{:S(2)}) collective-permute-start(bf16[1,1,128,2048]{2,3,1,0:T(8,128)(2,1)S(1)} %slice.396), channel_id=1, source_target_pairs={{0,8},{4,12},{8,0},{12,4},{16,24},{20,28},{24,16},{28,20},{1,9},{5... | collective-permute-start | bytes 1572872 | tf_op jit(solution)/shard_map/ppermute | solution.py:512
  420.6 39.7 %collective-permute-start.77 = (bf16[1,1,128,2048]{2,3,1,0:T(8,128)(2,1)S(1)}, bf16[1,1,128,2048]{2,3,1,0:T(8,128)(2,1)S(1)}, u32[]{:S(2)}, u32[]{:S(2)}) collective-permute-start(bf16[1,1,128,2048]{2,3,1,0:T(8,128)(2,1)S(1)} %slice.404), channel_id=1, source_target_pairs={{0,16},{4,20},{8,24},{12,28},{16,0},{20,4},{24,8},{28,12},{1,17},{... | collective-permute-start | bytes 1572872 | tf_op jit(solution)/shard_map/ppermute | solution.py:512
  426.0 44.8 %collective-permute-start.59 = (bf16[1,1,128,2048]{3,2,1,0:T(8,128)(2,1)S(1)}, bf16[1,1,128,2048]{3,2,1,0:T(8,128)(2,1)S(1)}, u32[]{:S(2)}, u32[]{:S(2)}) collective-permute-start(bf16[1,1,128,2048]{3,2,1,0:T(8,128)(2,1)S(1)} %slice.380), channel_id=1, source_target_pairs={{0,8},{4,12},{8,0},{12,4},{16,24},{20,28},{24,16},{28,20},{1,9},{5... | collective-permute-start | bytes 1572872 | tf_op jit(solution)/shard_map/ppermute | solution.py:512
  448.4 22.8 %collective-permute-start.65 = (bf16[1,1,128,2048]{3,2,1,0:T(8,128)(2,1)S(1)}, bf16[1,1,128,2048]{3,2,1,0:T(8,128)(2,1)S(1)}, u32[]{:S(2)}, u32[]{:S(2)}) collective-permute-start(bf16[1,1,128,2048]{3,2,1,0:T(8,128)(2,1)S(1)} %slice.388), channel_id=1, source_target_pairs={{0,16},{4,20},{8,24},{12,28},{16,0},{20,4},{24,8},{28,12},{1,17},{... | collective-permute-start | bytes 1572872 | tf_op jit(solution)/shard_map/ppermute | solution.py:512
  450.1 25.7 %collective-permute-start.53 = (bf16[1,1,128,2048]{2,3,1,0:T(8,128)(2,1)S(1)}, bf16[1,1,128,2048]{2,3,1,0:T(8,128)(2,1)S(1)}, u32[]{:S(2)}, u32[]{:S(2)}) collective-permute-start(bf16[1,1,128,2048]{2,3,1,0:T(8,128)(2,1)S(1)} %slice.366), channel_id=1, source_target_pairs={{0,16},{4,20},{8,24},{12,28},{16,0},{20,4},{24,8},{28,12},{1,17},{... | collective-permute-start | bytes 1572872 | tf_op jit(solution)/shard_map/ppermute | solution.py:512
  459.6 21.5 %collective-permute-start.47 = (bf16[1,1,128,2048]{3,2,1,0:T(8,128)(2,1)S(1)}, bf16[1,1,128,2048]{3,2,1,0:T(8,128)(2,1)S(1)}, u32[]{:S(2)}, u32[]{:S(2)}) collective-permute-start(bf16[1,1,128,2048]{3,2,1,0:T(8,128)(2,1)S(1)} %slice.352), channel_id=1, source_target_pairs={{0,8},{4,12},{8,0},{12,4},{16,24},{20,28},{24,16},{28,20},{1,9},{5... | collective-permute-start | bytes 1572872 | tf_op jit(solution)/shard_map/ppermute | solution.py:512
  460.3 21.0 %collective-permute-start.72 = (bf16[128,512]{0,1:T(8,128)(2,1)S(1)}, bf16[128,512]{0,1:T(8,128)(2,1)S(1)}, u32[]{:S(2)}, u32[]{:S(2)}) collective-permute-start(bf16[128,512]{0,1:T(8,128)(2,1)S(1)} %slice.400), channel_id=1, source_target_pairs={{0,3},{1,0},{2,1},{3,2},{4,7},{5,4},{6,5},{7,6},{8,11},{9,8},{10,9... | collective-permute-start | bytes 393224 | tf_op jit(solution)/shard_map/ppermute | solution.py:516
  471.2 13.2 %collective-permute-start.60 = (bf16[128,512]{1,0:T(8,128)(2,1)S(1)}, bf16[128,512]{1,0:T(8,128)(2,1)S(1)}, u32[]{:S(2)}, u32[]{:S(2)}) collective-permute-start(bf16[128,512]{1,0:T(8,128)(2,1)S(1)} %slice.384), channel_id=1, source_target_pairs={{0,3},{1,0},{2,1},{3,2},{4,7},{5,4},{6,5},{7,6},{8,11},{9,8},{10,9... | collective-permute-start | bytes 393224 | tf_op jit(solution)/shard_map/ppermute | solution.py:516
  487.6 14.0 %collective-permute-start.67 = (bf16[128,512]{1,0:T(8,128)(2,1)S(1)}, bf16[128,512]{1,0:T(8,128)(2,1)S(1)}, u32[]{:S(2)}, u32[]{:S(2)}) collective-permute-start(bf16[128,512]{1,0:T(8,128)(2,1)S(1)} %add_convert_fusion.24), channel_id=1, source_target_pairs={{0,3},{1,0},{2,1},{3,2},{4,7},{5,4},{6,5},{7,6},{8,11},{9,8},{10,9... | collective-permute-start | bytes 393224 | tf_op jit(solution)/shard_map/ppermute | solution.py:516
  490.4 14.0 %collective-permute-start.55 = (bf16[128,512]{0,1:T(8,128)(2,1)S(1)}, bf16[128,512]{0,1:T(8,128)(2,1)S(1)}, u32[]{:S(2)}, u32[]{:S(2)}) collective-permute-start(bf16[128,512]{0,1:T(8,128)(2,1)S(1)} %add_convert_fusion.30), channel_id=1, source_target_pairs={{0,3},{1,0},{2,1},{3,2},{4,7},{5,4},{6,5},{7,6},{8,11},{9,8},{10,9... | collective-permute-start | bytes 393224 | tf_op jit(solution)/shard_map/ppermute | solution.py:516
  493.2 14.0 %collective-permute-start.49 = (bf16[128,512]{1,0:T(8,128)(2,1)S(1)}, bf16[128,512]{1,0:T(8,128)(2,1)S(1)}, u32[]{:S(2)}, u32[]{:S(2)}) collective-permute-start(bf16[128,512]{1,0:T(8,128)(2,1)S(1)} %add_convert_fusion.33), channel_id=1, source_target_pairs={{0,3},{1,0},{2,1},{3,2},{4,7},{5,4},{6,5},{7,6},{8,11},{9,8},{10,9... | collective-permute-start | bytes 393224 | tf_op jit(solution)/shard_map/ppermute | solution.py:516
  496.0 14.0 %collective-permute-start.74 = (bf16[128,512]{0,1:T(8,128)(2,1)S(1)}, bf16[128,512]{0,1:T(8,128)(2,1)S(1)}, u32[]{:S(2)}, u32[]{:S(2)}) collective-permute-start(bf16[128,512]{0,1:T(8,128)(2,1)S(1)} %add_convert_fusion.20), channel_id=1, source_target_pairs={{0,3},{1,0},{2,1},{3,2},{4,7},{5,4},{6,5},{7,6},{8,11},{9,8},{10,9... | collective-permute-start | bytes 393224 | tf_op jit(solution)/shard_map/ppermute | solution.py:516
  498.8 14.0 %collective-permute-start.80 = (bf16[128,512]{0,1:T(8,128)(2,1)S(1)}, bf16[128,512]{0,1:T(8,128)(2,1)S(1)}, u32[]{:S(2)}, u32[]{:S(2)}) collective-permute-start(bf16[128,512]{0,1:T(8,128)(2,1)S(1)} %add_convert_fusion.17), channel_id=1, source_target_pairs={{0,3},{1,0},{2,1},{3,2},{4,7},{5,4},{6,5},{7,6},{8,11},{9,8},{10,9... | collective-permute-start | bytes 393224 | tf_op jit(solution)/shard_map/ppermute | solution.py:516
  501.6 14.0 %collective-permute-start.62 = (bf16[128,512]{1,0:T(8,128)(2,1)S(1)}, bf16[128,512]{1,0:T(8,128)(2,1)S(1)}, u32[]{:S(2)}, u32[]{:S(2)}) collective-permute-start(bf16[128,512]{1,0:T(8,128)(2,1)S(1)} %add_convert_fusion.26), channel_id=1, source_target_pairs={{0,3},{1,0},{2,1},{3,2},{4,7},{5,4},{6,5},{7,6},{8,11},{9,8},{10,9... | collective-permute-start | bytes 393224 | tf_op jit(solution)/shard_map/ppermute | solution.py:516
  504.4 20.1 %collective-permute-start.68 = (bf16[128,512]{1,0:T(8,128)(2,1)S(1)}, bf16[128,512]{1,0:T(8,128)(2,1)S(1)}, u32[]{:S(2)}, u32[]{:S(2)}) collective-permute-start(bf16[128,512]{1,0:T(8,128)(2,1)S(1)} %add_convert_fusion.23), channel_id=1, source_target_pairs={{0,3},{1,0},{2,1},{3,2},{4,7},{5,4},{6,5},{7,6},{8,11},{9,8},{10,9... | collective-permute-start | bytes 393224 | tf_op jit(solution)/shard_map/ppermute | solution.py:516
  507.2 13.6 %collective-permute-start.56 = (bf16[128,512]{0,1:T(8,128)(2,1)S(1)}, bf16[128,512]{0,1:T(8,128)(2,1)S(1)}, u32[]{:S(2)}, u32[]{:S(2)}) collective-permute-start(bf16[128,512]{0,1:T(8,128)(2,1)S(1)} %add_convert_fusion.29), channel_id=1, source_target_pairs={{0,3},{1,0},{2,1},{3,2},{4,7},{5,4},{6,5},{7,6},{8,11},{9,8},{10,9... | collective-permute-start | bytes 393224 | tf_op jit(solution)/shard_map/ppermute | solution.py:516
  (49 other events, 536.7 us)
